TPU v7x, 32 devices: a whole 2x2x4 slice. The times are simulated.
32 devices in a mesh: dp: 4 (over x, core), fsdp: 8 (over z, y).
Axes of the slice: x: 2, y: 2, z: 4, core: 2. Of those that a mesh axis runs over, the one named last changes fastest.
Arguments:
- hidden_in: bfloat16 [32, 512, 1024], P(('dp', 'fsdp')), may hold values from -6 to 6
- value_first: bfloat16 [32, 512, 1024], P(('dp', 'fsdp')), may hold values from -7.5 to 7.5
- segment_ids: int32 [32, 512], P(('dp', 'fsdp')), may hold values from 0 to 3, never falling along the last dimension, each value on 1 to 256 neighbouring positions
- attn_gain: bfloat16 [1024], P('fsdp'), may hold values from 0.5 to 1.5
- w_query: bfloat16 [1024, 1024], P('fsdp'), may hold values from -0.1875 to 0.1875
- w_key: bfloat16 [1024, 1024], P('fsdp'), may hold values from -0.1875 to 0.1875
- w_value: bfloat16 [1024, 1024], P('fsdp'), may hold values from -0.1875 to 0.1875
- w_output: bfloat16 [1024, 1024], P('fsdp'), may hold values from -1.5 to 1.5
- mlp_gain: bfloat16 [1024], P('fsdp'), may hold values from 0.5 to 1.5
- w_gate: bfloat16 [1024, 2816], P('fsdp'), may hold values from -0.1875 to 0.1875
- w_up: bfloat16 [1024, 2816], P('fsdp'), may hold values from -0.1875 to 0.1875
- w_down: bfloat16 [2816, 1024], P('fsdp'), may hold values from -0.21875 to 0.21875
- out_grad: bfloat16 [32, 512, 1024], P(('dp', 'fsdp')), may hold values from -6 to 6
- v1_grad_acc: float32 [32, 512, 1024], P(('dp', 'fsdp')), may hold values from -4 to 4
Outputs:
- block_out: bfloat16 [32, 512, 1024], P(('dp', 'fsdp'))
- input_grad: float32 [32, 512, 1024], P(('dp', 'fsdp'))
- grad_attn_gain: float32 [1024], P('fsdp')
- grad_query: float32 [1024, 1024], P('fsdp')
- grad_key: float32 [1024, 1024], P('fsdp')
- grad_value: float32 [1024, 1024], P('fsdp')
- grad_output: float32 [1024, 1024], P('fsdp')
- grad_mlp_gain: float32 [1024], P('fsdp')
- grad_gate: float32 [1024, 2816], P('fsdp')
- grad_up: float32 [1024, 2816], P('fsdp')
- grad_down: float32 [2816, 1024], P('fsdp')
- v1_grad_out: float32 [32, 512, 1024], P(('dp', 'fsdp'))
- value_norms: float32 [2], replicated
All inputs are finite; a program needn't handle non-finite values.
Results may differ from a plain program's by a relative error of at most 0.02.
Values may be sent and summed in bfloat16 or wider, within the bound.
No kernel may reach another device: no remote copies, remote signals or barrier semaphores. Data moves between devices by JAX's collectives and lax.ppermute only.
A program may use at most 192 MiB of HBM per device.

v0:
```python
import math

import jax
import jax.numpy as jnp
from jax import lax
from jax.sharding import PartitionSpec as P

HEADS = 16
HEAD_DIM = 64


eps_norm = 1e-06
rope_base = 10000.0
masked_score = -1e30


def positions_of(segment_ids):
    places = lax.broadcasted_iota(jnp.int32, segment_ids.shape, 1)
    before = jnp.concatenate([segment_ids[:, :1] - 1, segment_ids[:, :-1]], axis=1)
    starts = jnp.where(segment_ids != before, places, jnp.zeros_like(places))
    return places - lax.cummax(starts, axis=1)


def rope_tables(positions, half_dim):
    steps_f = jnp.arange(half_dim, dtype=jnp.float32)
    inverse = jnp.exp(steps_f * (-math.log(rope_base) / half_dim))
    angles = positions.astype(jnp.float32)[..., None] * inverse
    return (jnp.cos(angles), jnp.sin(angles))


def rotate(vectors, cosine, sine):
    half_dim = vectors.shape[-1] // 2
    first = vectors[..., :half_dim]
    second = vectors[..., half_dim:]
    cos_b = cosine[..., None, :]
    sin_b = sine[..., None, :]
    return jnp.concatenate(
        [first * cos_b - second * sin_b, second * cos_b + first * sin_b], axis=-1
    )


def rotate_back(grads, cosine, sine):
    half_dim = grads.shape[-1] // 2
    first = grads[..., :half_dim]
    second = grads[..., half_dim:]
    cos_b = cosine[..., None, :]
    sin_b = sine[..., None, :]
    return jnp.concatenate(
        [first * cos_b + second * sin_b, second * cos_b - first * sin_b], axis=-1
    )


def norm_forward(values, gain_f):
    inverse = lax.rsqrt(jnp.mean(values * values, axis=-1, keepdims=True) + eps_norm)
    return (values * inverse * gain_f, inverse)


def norm_backward(values, inverse, gain_f, grad_out):
    scaled = values * inverse
    grad_scaled = grad_out * gain_f
    grad_gain = jnp.sum(grad_out * scaled, axis=0)
    grad_values = inverse * (
        grad_scaled - scaled * jnp.mean(grad_scaled * scaled, axis=-1, keepdims=True)
    )
    return (grad_values, grad_gain)


def block_mask(segment_row, begin_at, block, length):
    row_ids = begin_at + jnp.arange(block)
    col_ids = jnp.arange(length)
    return (col_ids[None, :] <= row_ids[:, None]) & (segment_row[:, None] == segment_row[None, :])


def block_scores(q_blk, k_rot, segment_row, begin_at, block, length, scale):
    scores = jnp.einsum("qhd,khd->hqk", q_blk, k_rot, preferred_element_type=jnp.float32) * scale
    allowed = block_mask(segment_row, begin_at, block, length)
    return jnp.where(allowed[None], scores, masked_score)


def shards(
    hidden_in,
    value_first,
    segment_ids,
    attn_gain,
    w_query,
    w_key,
    w_value,
    w_output,
    mlp_gain,
    w_gate,
    w_up,
    w_down,
    out_grad,
    v1_grad_acc,
):
    length = hidden_in.shape[1]
    width = hidden_in.shape[2]
    block = min(512, length)
    n_blocks = length // block
    scale = HEAD_DIM ** (-0.5)
    gain_one, query_mat, key_mat, value_mat, output_mat = (
        lax.all_gather(attn_gain, "fsdp", axis=0, tiled=True),
        lax.all_gather(w_query, "fsdp", axis=0, tiled=True),
        lax.all_gather(w_key, "fsdp", axis=0, tiled=True),
        lax.all_gather(w_value, "fsdp", axis=0, tiled=True),
        lax.all_gather(w_output, "fsdp", axis=0, tiled=True),
    )
    gain_two, gate_mat, up_mat, down_mat = (
        lax.all_gather(mlp_gain, "fsdp", axis=0, tiled=True),
        lax.all_gather(w_gate, "fsdp", axis=0, tiled=True),
        lax.all_gather(w_up, "fsdp", axis=0, tiled=True),
        lax.all_gather(w_down, "fsdp", axis=0, tiled=True),
    )
    segment_row = segment_ids[0]
    cosine, sine = rope_tables(positions_of(segment_ids)[0], HEAD_DIM // 2)
    rows_in = hidden_in[0].astype(jnp.float32)
    first_f = value_first[0].astype(jnp.float32)
    gain_one_f = gain_one.astype(jnp.float32)
    normed_f, inverse_one = norm_forward(rows_in, gain_one_f)
    normed = normed_f.astype(jnp.bfloat16)
    queries = jnp.dot(normed, query_mat, preferred_element_type=jnp.float32).reshape(
        length, HEADS, HEAD_DIM
    )
    keys_in = jnp.dot(normed, key_mat, preferred_element_type=jnp.float32).reshape(
        length, HEADS, HEAD_DIM
    )
    values_own = jnp.dot(normed, value_mat, preferred_element_type=jnp.float32)
    q_rot = rotate(queries, cosine, sine).astype(jnp.bfloat16)
    k_rot = rotate(keys_in, cosine, sine).astype(jnp.bfloat16)
    blended = (0.5 * values_own + 0.5 * first_f).astype(jnp.bfloat16)
    blended_heads = blended.reshape(length, HEADS, HEAD_DIM)
    square_first = jnp.sum(first_f * first_f)
    blended_f = blended.astype(jnp.float32)
    square_blend = jnp.sum(blended_f * blended_f)

    def attend_block(begin_at):
        scores = block_scores(q_rot, k_rot, segment_row, begin_at, block, length, scale)
        top_val = jnp.max(scores, axis=-1, keepdims=True)
        expo = jnp.exp(scores - top_val)
        total = jnp.sum(expo, axis=-1, keepdims=True)
        probs = (expo / total).astype(jnp.bfloat16)
        outputs = jnp.einsum(
            "hqk,khd->qhd", probs, blended_heads, preferred_element_type=jnp.float32
        )
        return (outputs, (top_val + jnp.log(total))[..., 0])

    block_starts = jnp.arange(n_blocks, dtype=jnp.int32) * block
    attn_blocks, lse_blocks = lax.map(attend_block, block_starts)
    attended = attn_blocks.reshape(length, width).astype(jnp.bfloat16)
    mixed = rows_in + jnp.dot(attended, output_mat, preferred_element_type=jnp.float32)
    gain_two_f = gain_two.astype(jnp.float32)
    normed_two_f, inverse_two = norm_forward(mixed, gain_two_f)
    normed_two = normed_two_f.astype(jnp.bfloat16)
    gate = jnp.dot(normed_two, gate_mat, preferred_element_type=jnp.float32)
    up_val = jnp.dot(normed_two, up_mat, preferred_element_type=jnp.float32)
    sigma = jax.nn.sigmoid(gate)
    silu_gate = gate * sigma
    act = (silu_gate * up_val).astype(jnp.bfloat16)
    out_rows = mixed + jnp.dot(act, down_mat, preferred_element_type=jnp.float32)
    block_out = out_rows.astype(jnp.bfloat16)[None]
    gain_one, query_mat, key_mat, value_mat, output_mat = (
        lax.all_gather(attn_gain, "fsdp", axis=0, tiled=True),
        lax.all_gather(w_query, "fsdp", axis=0, tiled=True),
        lax.all_gather(w_key, "fsdp", axis=0, tiled=True),
        lax.all_gather(w_value, "fsdp", axis=0, tiled=True),
        lax.all_gather(w_output, "fsdp", axis=0, tiled=True),
    )
    gain_two, gate_mat, up_mat, down_mat = (
        lax.all_gather(mlp_gain, "fsdp", axis=0, tiled=True),
        lax.all_gather(w_gate, "fsdp", axis=0, tiled=True),
        lax.all_gather(w_up, "fsdp", axis=0, tiled=True),
        lax.all_gather(w_down, "fsdp", axis=0, tiled=True),
    )
    gain_one_f = gain_one.astype(jnp.float32)
    gain_two_f = gain_two.astype(jnp.float32)
    grad_rows_out = out_grad[0].astype(jnp.float32)
    grad_mlp = grad_rows_out.astype(jnp.bfloat16)
    grad_down_w = jnp.einsum("rf,rd->fd", act, grad_mlp, preferred_element_type=jnp.float32)
    grad_act = jnp.einsum("rd,fd->rf", grad_mlp, down_mat, preferred_element_type=jnp.float32)
    grad_gate = (grad_act * up_val * sigma * (1.0 + gate * (1.0 - sigma))).astype(jnp.bfloat16)
    grad_upv = (grad_act * silu_gate).astype(jnp.bfloat16)
    grad_gate_w = jnp.einsum("rd,rf->df", normed_two, grad_gate, preferred_element_type=jnp.float32)
    grad_up_w = jnp.einsum("rd,rf->df", normed_two, grad_upv, preferred_element_type=jnp.float32)
    grad_normed_two = jnp.einsum(
        "rf,df->rd", grad_gate, gate_mat, preferred_element_type=jnp.float32
    )
    grad_normed_two = grad_normed_two + jnp.einsum(
        "rf,df->rd", grad_upv, up_mat, preferred_element_type=jnp.float32
    )
    grad_mixed_norm, grad_gain_two = norm_backward(mixed, inverse_two, gain_two_f, grad_normed_two)
    grad_mixed = grad_rows_out + grad_mixed_norm
    grad_attn = grad_mixed.astype(jnp.bfloat16)
    grad_output_w = jnp.einsum("rd,re->de", attended, grad_attn, preferred_element_type=jnp.float32)
    grad_attended = jnp.einsum(
        "re,de->rd", grad_attn, output_mat, preferred_element_type=jnp.float32
    )
    grad_attended = grad_attended.astype(jnp.bfloat16).reshape(length, HEADS, HEAD_DIM)

    def back_block(running, pieces):
        grad_keys, grad_vals = running
        begin_at, lse_blk = pieces
        scores = block_scores(q_rot, k_rot, segment_row, begin_at, block, length, scale)
        probs = jnp.exp(scores - lse_blk[..., None])
        probs_low = probs.astype(jnp.bfloat16)
        grad_probs = jnp.einsum(
            "qhd,khd->hqk", grad_attended, blended_heads, preferred_element_type=jnp.float32
        )
        inner = jnp.sum(probs * grad_probs, axis=-1, keepdims=True)
        grad_scores = (probs * (grad_probs - inner)).astype(jnp.bfloat16)
        grad_q_blk = (
            jnp.einsum("hqk,khd->qhd", grad_scores, k_rot, preferred_element_type=jnp.float32)
            * scale
        )
        grad_keys = (
            grad_keys
            + jnp.einsum("hqk,qhd->khd", grad_scores, q_rot, preferred_element_type=jnp.float32)
            * scale
        )
        grad_vals = grad_vals + jnp.einsum(
            "hqk,qhd->khd", probs_low, grad_attended, preferred_element_type=jnp.float32
        )
        return ((grad_keys, grad_vals), grad_q_blk)

    zero_heads = jnp.zeros((length, HEADS, HEAD_DIM), jnp.float32)
    (grad_k_rot, grad_blended), grad_q_blocks = lax.scan(
        back_block, (zero_heads, zero_heads), (block_starts, lse_blocks)
    )
    grad_q_rot = grad_q_blocks.reshape(length, HEADS, HEAD_DIM)
    grad_queries = rotate_back(grad_q_rot, cosine, sine).reshape(length, width).astype(jnp.bfloat16)
    grad_keys_in = rotate_back(grad_k_rot, cosine, sine).reshape(length, width).astype(jnp.bfloat16)
    grad_first = 0.5 * grad_blended.reshape(length, width)
    grad_values = grad_first.astype(jnp.bfloat16)
    grad_query_w = jnp.einsum("rd,re->de", normed, grad_queries, preferred_element_type=jnp.float32)
    grad_key_w = jnp.einsum("rd,re->de", normed, grad_keys_in, preferred_element_type=jnp.float32)
    grad_value_w = jnp.einsum("rd,re->de", normed, grad_values, preferred_element_type=jnp.float32)
    grad_normed = jnp.einsum(
        "re,de->rd", grad_queries, query_mat, preferred_element_type=jnp.float32
    )
    grad_normed = grad_normed + jnp.einsum(
        "re,de->rd", grad_keys_in, key_mat, preferred_element_type=jnp.float32
    )
    grad_normed = grad_normed + jnp.einsum(
        "re,de->rd", grad_values, value_mat, preferred_element_type=jnp.float32
    )
    grad_rows_norm, grad_gain_one = norm_backward(rows_in, inverse_one, gain_one_f, grad_normed)
    input_grad = (grad_mixed + grad_rows_norm)[None]
    v1_grad_out = v1_grad_acc + grad_first[None]
    share_gain_one, share_query, share_key, share_value, share_output = (
        lax.psum_scatter(
            grad_gain_one.astype(jnp.bfloat16), "fsdp", scatter_dimension=0, tiled=True
        ).astype(jnp.float32),
        lax.psum_scatter(
            grad_query_w.astype(jnp.bfloat16), "fsdp", scatter_dimension=0, tiled=True
        ).astype(jnp.float32),
        lax.psum_scatter(
            grad_key_w.astype(jnp.bfloat16), "fsdp", scatter_dimension=0, tiled=True
        ).astype(jnp.float32),
        lax.psum_scatter(
            grad_value_w.astype(jnp.bfloat16), "fsdp", scatter_dimension=0, tiled=True
        ).astype(jnp.float32),
        lax.psum_scatter(
            grad_output_w.astype(jnp.bfloat16), "fsdp", scatter_dimension=0, tiled=True
        ).astype(jnp.float32),
    )
    share_gain_two, share_gate, share_up, share_down = (
        lax.psum_scatter(
            grad_gain_two.astype(jnp.bfloat16), "fsdp", scatter_dimension=0, tiled=True
        ).astype(jnp.float32),
        lax.psum_scatter(
            grad_gate_w.astype(jnp.bfloat16), "fsdp", scatter_dimension=0, tiled=True
        ).astype(jnp.float32),
        lax.psum_scatter(
            grad_up_w.astype(jnp.bfloat16), "fsdp", scatter_dimension=0, tiled=True
        ).astype(jnp.float32),
        lax.psum_scatter(
            grad_down_w.astype(jnp.bfloat16), "fsdp", scatter_dimension=0, tiled=True
        ).astype(jnp.float32),
    )
    (
        share_gain_one,
        share_query,
        share_key,
        share_value,
        share_output,
        share_gain_two,
        share_gate,
        share_up,
        share_down,
    ) = (
        lax.psum(share_gain_one.astype(jnp.bfloat16), "dp").astype(jnp.float32),
        lax.psum(share_query.astype(jnp.bfloat16), "dp").astype(jnp.float32),
        lax.psum(share_key.astype(jnp.bfloat16), "dp").astype(jnp.float32),
        lax.psum(share_value.astype(jnp.bfloat16), "dp").astype(jnp.float32),
        lax.psum(share_output.astype(jnp.bfloat16), "dp").astype(jnp.float32),
        lax.psum(share_gain_two.astype(jnp.bfloat16), "dp").astype(jnp.float32),
        lax.psum(share_gate.astype(jnp.bfloat16), "dp").astype(jnp.float32),
        lax.psum(share_up.astype(jnp.bfloat16), "dp").astype(jnp.float32),
        lax.psum(share_down.astype(jnp.bfloat16), "dp").astype(jnp.float32),
    )
    total_first, total_blend = lax.psum((square_first, square_blend), ("dp", "fsdp"))
    count = jnp.float32(lax.axis_size("dp") * lax.axis_size("fsdp") * length * width)
    value_norms = jnp.sqrt(jnp.stack([total_first, total_blend]) / count)
    return (
        block_out,
        input_grad,
        share_gain_one,
        share_query,
        share_key,
        share_value,
        share_output,
        share_gain_two,
        share_gate,
        share_up,
        share_down,
        v1_grad_out,
        value_norms,
    )


def solution(mesh):
    in_specs = (
        P(("dp", "fsdp"), None, None),
        P(("dp", "fsdp"), None, None),
        P(("dp", "fsdp"), None),
        P("fsdp"),
        P("fsdp", None),
        P("fsdp", None),
        P("fsdp", None),
        P("fsdp", None),
        P("fsdp"),
        P("fsdp", None),
        P("fsdp", None),
        P("fsdp", None),
        P(("dp", "fsdp"), None, None),
        P(("dp", "fsdp"), None, None),
    )
    out_specs = (
        P(("dp", "fsdp"), None, None),
        P(("dp", "fsdp"), None, None),
        P("fsdp"),
        P("fsdp", None),
        P("fsdp", None),
        P("fsdp", None),
        P("fsdp", None),
        P("fsdp"),
        P("fsdp", None),
        P("fsdp", None),
        P("fsdp", None),
        P(("dp", "fsdp"), None, None),
        P(),
    )
    return jax.shard_map(shards, mesh=mesh, in_specs=in_specs, out_specs=out_specs, check_vma=False)
```

profile of v0, /device:TPU:0, one launch (start us, length us, event | category | flops | bytes accessed | tf_op | source)
XLA Modules:
  0.0 1224.7 jit_solution(14413526482383940278)
XLA Ops:
  13.9 22.4 %all-gather = bf16[8,1,128]{2,1,0:T(2,128)(2,1)S(1)} all-gather(bf16[1,1,128]{2,1,0:T(2,128)(2,1)S(1)} %bitcast.174), channel_id=1, replica_groups=mesh['dp'=4,'fsdp'=8] {'fsdp'}, dimensions={0}, use_global_device_ids=true | all-gather | bytes 2304 | tf_op jit(solution)/shard_map/all_gather | solution.py:102
  36.4 16.7 %all-gather.1 = bf16[8,1,128]{2,1,0:T(2,128)(2,1)S(1)} all-gather(bf16[1,1,128]{2,1,0:T(2,128)(2,1)S(1)} %bitcast.175), channel_id=1, replica_groups=mesh['dp'=4,'fsdp'=8] {'fsdp'}, dimensions={0}, use_global_device_ids=true | all-gather | bytes 2304 | tf_op jit(solution)/shard_map/all_gather | solution.py:109
  54.0 8.1 all-gather.10.cloned.1.call-done
  62.1 3.7 multiply_reduce_fusion.1
  66.4 45.5 %all-gather.14.cloned.1.call-done = bf16[1024,1024]{1,0:T(8,128)(2,1)} async-done(((bf16[128,1024]{1,0:T(8,128)(2,1)}), bf16[1024,1024]{1,0:T(8,128)(2,1)}) %all-gather.14.cloned.1.call-update) | async-done | bytes 2097168 | tf_op jit(solution)/shard_map/all_gather | solution.py:104
  111.9 3.9 copy.49
  115.8 45.9 %all-gather.12.cloned.1.call-done = bf16[1024,1024]{1,0:T(8,128)(2,1)} async-done(((bf16[128,1024]{1,0:T(8,128)(2,1)}), bf16[1024,1024]{1,0:T(8,128)(2,1)}) %all-gather.12.cloned.1.call-update) | async-done | bytes 2097168 | tf_op jit(solution)/shard_map/all_gather | solution.py:103
  161.7 3.9 copy.48
  165.6 3.1 fusion.36
  170.9 7.3 fusion.59
  178.2 8.3 fusion
  186.5 8.9 fusion.30
  195.5 15.9 %all-gather.16.cloned.1.call-done = bf16[1024,1024]{1,0:T(8,128)(2,1)} async-done(((bf16[128,1024]{1,0:T(8,128)(2,1)}), bf16[1024,1024]{1,0:T(8,128)(2,1)}) %all-gather.16.cloned.1.call-update) | async-done | bytes 2097168 | tf_op jit(solution)/shard_map/all_gather | solution.py:106
  211.3 3.3 multiply_reduce_fusion.4
  216.0 88.2 %all-gather.20.cloned.1.call-done = bf16[1024,2816]{1,0:T(8,128)(2,1)} async-done(((bf16[128,2816]{1,0:T(8,128)(2,1)}), bf16[1024,2816]{1,0:T(8,128)(2,1)}) %all-gather.20.cloned.1.call-update) | async-done | bytes 5767184 | tf_op jit(solution)/shard_map/all_gather | solution.py:111
  304.2 8.6 fusion.62
  312.8 84.0 %all-gather.18.cloned.1.call-done = bf16[1024,2816]{1,0:T(8,128)(2,1)} async-done(((bf16[128,2816]{1,0:T(8,128)(2,1)}), bf16[1024,2816]{1,0:T(8,128)(2,1)}) %all-gather.18.cloned.1.call-update) | async-done | bytes 5767184 | tf_op jit(solution)/shard_map/all_gather | solution.py:110
  396.8 8.6 fusion.61
  405.4 84.1 %all-gather.22.cloned.1.call-done = bf16[2816,1024]{1,0:T(8,128)(2,1)} async-done(((bf16[352,1024]{1,0:T(8,128)(2,1)}), bf16[2816,1024]{1,0:T(8,128)(2,1)}) %all-gather.22.cloned.1.call-update) | async-done | bytes 5767184 | tf_op jit(solution)/shard_map/all_gather | solution.py:112
  489.5 11.3 multiply_convert_fusion.1
  500.9 3.2 fusion.63
  504.1 6.1 multiply_reduce_fusion.2
  516.4 3.9 convolution_convert_fusion.7
  521.7 10.2 fusion.60
  532.0 2.8 convolution_convert_fusion.4
  534.9 9.2 multiply_reduce_fusion
  544.1 8.4 multiply_convert_fusion
  552.5 3.8 multiply_bitcast_fusion
  560.0 2.8 convolution_convert_fusion.6
  562.9 2.8 convolution_convert_fusion.5
  567.0 6.9 convolution_convert_fusion
  575.1 6.8 convolution_convert_fusion.1
  582.0 7.0 convolution_convert_fusion.2
  593.3 39.3 %all-reduce.2 = (f32[1]{0:T(128)}, f32[1]{0:T(128)}) all-reduce(f32[1]{0:T(128)} %bitcast.36, f32[1]{0:T(128)} %bitcast.35), channel_id=1, replica_groups=mesh['dp'=4,'fsdp'=8] {'dp','fsdp'}, use_global_device_ids=true, to_apply=%region_32.33 | all-reduce | flops 2 | bytes 16 | tf_op jit(solution)/shard_map/psum | solution.py:300
  634.5 4.1 fusion.65
  638.6 2.7 fusion.64
  641.3 12.1 reduce-scatter.12.cloned.1.call-done
  653.4 71.1 %reduce-scatter.8.cloned.1.call-done = bf16[128,1024]{1,0:T(8,128)(2,1)} async-done(((bf16[1024,1024]{1,0:T(8,128)(2,1)}), bf16[128,1024]{1,0:T(8,128)(2,1)}) %reduce-scatter.8.cloned.1.call-update) | async-done | bytes 262160 | tf_op jit(solution)/shard_map/reduce_scatter | solution.py:252
  724.5 71.1 %reduce-scatter.10.cloned.1.call-done = bf16[128,1024]{1,0:T(8,128)(2,1)} async-done(((bf16[1024,1024]{1,0:T(8,128)(2,1)}), bf16[128,1024]{1,0:T(8,128)(2,1)}) %reduce-scatter.10.cloned.1.call-update) | async-done | bytes 262160 | tf_op jit(solution)/shard_map/reduce_scatter | solution.py:255
  795.6 113.1 %reduce-scatter.20.cloned.1.call-done = bf16[352,1024]{1,0:T(8,128)(2,1)} async-done(((bf16[2816,1024]{1,0:T(8,128)(2,1)}), bf16[352,1024]{1,0:T(8,128)(2,1)}) %reduce-scatter.20.cloned.1.call-update) | async-done | bytes 720912 | tf_op jit(solution)/shard_map/reduce_scatter | solution.py:275
  908.7 113.6 %reduce-scatter.18.cloned.1.call-done = bf16[128,2816]{1,0:T(8,128)(2,1)} async-done(((bf16[1024,2816]{1,0:T(8,128)(2,1)}), bf16[128,2816]{1,0:T(8,128)(2,1)}) %reduce-scatter.18.cloned.1.call-update) | async-done | bytes 720912 | tf_op jit(solution)/shard_map/reduce_scatter | solution.py:272
  1022.4 113.5 %reduce-scatter.16.cloned.1.call-done = bf16[128,2816]{1,0:T(8,128)(2,1)} async-done(((bf16[1024,2816]{1,0:T(8,128)(2,1)}), bf16[128,2816]{1,0:T(8,128)(2,1)}) %reduce-scatter.16.cloned.1.call-update) | async-done | bytes 720912 | tf_op jit(solution)/shard_map/reduce_scatter | solution.py:269
  1135.9 6.4 fusion.20
  1144.1 19.8 %all-reduce.3 = (bf16[1024]{0:T(1024)(128)(2,1)S(1)}, bf16[1024]{0:T(1024)(128)(2,1)S(1)}) all-reduce(bf16[1024]{0:T(1024)(128)(2,1)S(1)} %get-tuple-element.56, bf16[1024]{0:T(1024)(128)(2,1)S(1)} %get-tuple-element.54), channel_id=2, replica_groups=mesh['dp'=4,'fsdp'=8] {'fsdp'}, use_global_device_ids=true, to_apply=%region_10.11.clone | all-reduce | flops 2048 | bytes 8192
  1164.1 6.5 all-reduce.4
  1171.6 4.3 add.147
  1179.2 7.2 fusion.31
  1186.4 21.4 %all-reduce.8.cloned.1.call-done = (bf16[128,1024]{1,0:T(8,128)(2,1)}, bf16[128,1024]{1,0:T(8,128)(2,1)}, bf16[128,1024]{1,0:T(8,128)(2,1)}, bf16[128,1024]{1,0:...) async-done(((bf16[128,1024]{1,0:T(8,128)(2,1)}, bf16[128,1024]{1,0:T(8,128)(2,1)}, bf16[128,1024]{1,0:T(8,128)(2,1)}, ...) | async-done | bytes 3211280 | tf_op jit(solution)/shard_map/psum | solution.py:291
  (166 shorter events, 46.7 us)
Async XLA Ops:
  7.2 4.8 copy-start.37
  7.2 6.7 copy-start.38
  7.2 29.2 %copy-start.39 = (bf16[128]{0:T(256)(128)(2,1)S(1)}, bf16[128]{0:T(256)(128)(2,1)}, u32[]{:S(2)}) copy-start(bf16[128]{0:T(256)(128)(2,1)} %param.22) | copy-start | bytes 772
  7.2 45.8 %copy-start.2 = (bf16[1,512,1024]{2,1,0:T(8,128)(2,1)S(1)}, bf16[1,512,1024]{2,1,0:T(8,128)(2,1)}, u32[]{:S(2)}) copy-start(bf16[1,512,1024]{2,1,0:T(8,128)(2,1)} %param.14) | copy-start | bytes 3145732
  7.2 54.9 %all-gather.10.cloned.1.call-start = ((), (), s32[]{:S(2)}) async-start(), calls=%async_computation.7 | async-start | bytes 2359296 | tf_op jit(solution)/shard_map/all_gather | solution.py:105
  8.0 103.9 %all-gather.14.cloned.1.call-start = ((), (), s32[]{:S(2)}) async-start(), calls=%async_computation.9 | async-start | bytes 2359296 | tf_op jit(solution)/shard_map/all_gather | solution.py:104
  8.7 53.4 %copy-start.22 = (bf16[1,512,1024]{2,1,0:T(8,128)(2,1)S(1)}, bf16[1,512,1024]{2,1,0:T(8,128)(2,1)}, u32[]{:S(2)}) copy-start(bf16[1,512,1024]{2,1,0:T(8,128)(2,1)} %param.15) | copy-start | bytes 3145732
  8.7 153.0 %all-gather.12.cloned.1.call-start = ((), (), s32[]{:S(2)}) async-start(), calls=%async_computation.8 | async-start | bytes 2359296 | tf_op jit(solution)/shard_map/all_gather | solution.py:103
  9.5 201.9 %all-gather.16.cloned.1.call-start = ((), (), s32[]{:S(2)}) async-start(), calls=%async_computation.10 | async-start | bytes 2359296 | tf_op jit(solution)/shard_map/all_gather | solution.py:106
  10.0 294.2 %all-gather.20.cloned.1.call-start = ((), (), s32[]{:S(2)}) async-start(), calls=%async_computation.12 | async-start | bytes 6488064 | tf_op jit(solution)/shard_map/all_gather | solution.py:111
  10.6 386.2 %all-gather.18.cloned.1.call-start = ((), (), s32[]{:S(2)}) async-start(), calls=%async_computation.11 | async-start | bytes 6488064 | tf_op jit(solution)/shard_map/all_gather | solution.py:110
  11.2 478.3 %all-gather.22.cloned.1.call-start = ((), (), s32[]{:S(2)}) async-start(), calls=%async_computation.13 | async-start | bytes 6488064 | tf_op jit(solution)/shard_map/all_gather | solution.py:112
  11.9 629.4 %reduce-scatter.14.cloned.1.call-start = ((), (), s32[]{:S(2)}) async-start(), calls=%async_computation.17 | async-start | bytes 2359296 | tf_op jit(solution)/shard_map/reduce_scatter | solution.py:261
  53.7 116.3 %copy-start.33 = (f32[512,32]{0,1:T(8,128)}, f32[512,32]{0,1:T(8,128)S(1)}, u32[]{:S(2)}) copy-start(f32[512,32]{0,1:T(8,128)S(1)} %get-tuple-element.97) | copy-start | bytes 196612
  66.4 120.1 %copy-start.11 = (bf16[512,1024]{0,1:T(8,128)(2,1)}, bf16[512,1024]{0,1:T(8,128)(2,1)S(1)}, u32[]{:S(2)}) copy-start(bf16[512,1024]{0,1:T(8,128)(2,1)S(1)} %copy.47) | copy-start | bytes 3145732
  165.6 3.1 copy-start.21
  170.8 7.4 copy-start.12
  170.8 7.4 copy-start.14
  170.8 7.4 copy-start.16
  170.8 7.4 copy-start.18
  214.6 295.6 %copy-start = (f32[512,1024]{1,0:T(8,128)}, f32[512,1024]{1,0:T(8,128)S(1)}, u32[]{:S(2)}) copy-start(f32[512,1024]{1,0:T(8,128)S(1)} %get-tuple-element.101) | copy-start | bytes 6291460
  489.5 11.4 copy-start.40
  500.8 3.2 copy-start.44
  500.8 3.2 copy-start.42
  504.0 6.2 copy-start.24
  514.8 138.5 %reduce-scatter.12.cloned.1.call-start = ((), (), s32[]{:S(2)}) async-start(), calls=%async_computation.16 | async-start | bytes 2359296 | tf_op jit(solution)/shard_map/reduce_scatter | solution.py:258
  516.4 18.5 %copy-start.35 = (f32[16,512]{1,0:T(8,128)}, f32[16,512]{1,0:T(8,128)S(1)}, u32[]{:S(2)}) copy-start(f32[16,512]{1,0:T(8,128)S(1)} %log_add_fusion) | copy-start | bytes 98308
  521.7 10.2 copy-start.4
  534.8 189.7 %reduce-scatter.8.cloned.1.call-start = ((), (), s32[]{:S(2)}) async-start(), calls=%async_computation.14 | async-start | bytes 2359296 | tf_op jit(solution)/shard_map/reduce_scatter | solution.py:252
  544.1 8.4 copy-start.17
  552.5 3.8 copy-start.13
  552.5 3.8 copy-start.15
  558.6 4.3 copy-start.28
  562.9 232.7 %reduce-scatter.10.cloned.1.call-start = ((), (), s32[]{:S(2)}) async-start(), calls=%async_computation.15 | async-start | bytes 2359296 | tf_op jit(solution)/shard_map/reduce_scatter | solution.py:255
  565.8 342.9 %reduce-scatter.20.cloned.1.call-start = ((), (), s32[]{:S(2)}) async-start(), calls=%async_computation.20 | async-start | bytes 6488064 | tf_op jit(solution)/shard_map/reduce_scatter | solution.py:275
  573.9 448.4 %reduce-scatter.18.cloned.1.call-start = ((), (), s32[]{:S(2)}) async-start(), calls=%async_computation.19 | async-start | bytes 6488064 | tf_op jit(solution)/shard_map/reduce_scatter | solution.py:272
  582.0 553.9 %reduce-scatter.16.cloned.1.call-start = ((), (), s32[]{:S(2)}) async-start(), calls=%async_computation.18 | async-start | bytes 6488064 | tf_op jit(solution)/shard_map/reduce_scatter | solution.py:269
  589.0 45.5 %copy-start.19 = (bf16[1024,1024]{1,0:T(8,128)(2,1)S(1)}, bf16[1024,1024]{1,0:T(8,128)(2,1)}, u32[]{:S(2)}) copy-start(bf16[1024,1024]{1,0:T(8,128)(2,1)} %all-gather.14.cloned.1.call-done) | copy-start | bytes 6291460
  589.1 618.7 %all-reduce.8.cloned.1.call-start = ((), (), s32[]{:S(2)}) async-start(), calls=%async_computation.21 | async-start | bytes 6422528 | tf_op jit(solution)/shard_map/psum | solution.py:291
  634.5 4.1 copy-start.20
  634.5 4.1 copy-start.27
  1135.9 6.4 copy-start.5
  1171.6 4.3 copy-start.6
  1171.6 4.3 copy-start.9
  1175.9 3.3 copy-start.43
  1207.7 5.5 copy-start.36
  1207.7 6.4 copy-start.32
  1209.6 5.7 copy-start.31
  (12 other events, 19.0 us)
Sparse Core Ops, SparseCore 0:
  10.2 51.8 all-gather.9
  64.2 47.6 all-gather.13
  114.0 47.6 all-gather.11
  163.6 47.6 all-gather.15
  213.3 90.8 all-gather.19
  306.3 90.4 all-gather.17
  399.0 90.4 all-gather.21
  514.9 66.7 reduce-scatter.13
  585.3 68.0 reduce-scatter.11
  656.7 67.7 reduce-scatter.7
  728.0 67.5 reduce-scatter.9
  799.1 109.5 reduce-scatter.19
  912.4 109.9 reduce-scatter.17
  1025.9 109.9 reduce-scatter.15
  1138.6 69.1 all-reduce.7
where the time goes:
time: 1230 us; the launch traced here: 1220 us
  waiting for transfers between devices  892 us (73%)
  matrix products  146 us (12%)
  blocking collectives  105 us (9%)
  other arithmetic  43.2 us (4%)
  local copies, waits for them, and re-layouts  22 us (2%)
  between operations  16.2 us (1%)
    reduce_scatter x1, waiting for transfers between devices, shards(): lax.psum_scatter(grad_up_w.astype(jnp.bfloat16), 'fsdp', scatter_dimensio...  114 us
    reduce_scatter x1, waiting for transfers between devices, shards(): lax.psum_scatter(grad_gate_w.astype(jnp.bfloat16), 'fsdp', scatter_dimens...  114 us
    reduce_scatter x1, waiting for transfers between devices, shards(): lax.psum_scatter(grad_down_w.astype(jnp.bfloat16), 'fsdp', scatter_dimens...  113 us
    all_gather x1, waiting for transfers between devices, shards(): lax.all_gather(w_up, 'fsdp', axis=0, tiled=True)  88.2 us
    all_gather x1, waiting for transfers between devices, shards(): lax.all_gather(w_down, 'fsdp', axis=0, tiled=True)  84.1 us
    all_gather x1, waiting for transfers between devices, shards(): lax.all_gather(w_gate, 'fsdp', axis=0, tiled=True)  84 us
    reduce_scatter x1, waiting for transfers between devices, shards(): lax.psum_scatter(grad_query_w.astype(jnp.bfloat16), 'fsdp', scatter_dimen...  71.1 us
    reduce_scatter x1, waiting for transfers between devices, shards(): lax.psum_scatter(grad_key_w.astype(jnp.bfloat16), 'fsdp', scatter_dimensi...  71.1 us
  transfers between devices with their start and end apart: 15, of which 14 were waited for; matrix products, arithmetic and copies ran while one was open for 14% of the time, Pallas kernels for 0%

commit v1 on v0

v1 whole, which is shorter than its diff:
```python
import functools
import math

import jax
import jax.numpy as jnp
from jax import lax
from jax.experimental import pallas as pl
from jax.experimental.pallas import tpu as pltpu
from jax.sharding import PartitionSpec as P

HEAD_DIM = 64
LANES = 128
REACH = 256
BLOCK = 128

eps_norm = 1e-06
rope_base = 10000.0
masked_score = -1e30
bf16 = jnp.bfloat16
f32 = jnp.float32


def positions_of(segment_ids):
    places = lax.broadcasted_iota(jnp.int32, segment_ids.shape, 1)
    before = jnp.concatenate([segment_ids[:, :1] - 1, segment_ids[:, :-1]], axis=1)
    starts = jnp.where(segment_ids != before, places, jnp.zeros_like(places))
    return places - lax.cummax(starts, axis=1)


def rope_tables(positions):
    half = HEAD_DIM // 2
    lane = lax.broadcasted_iota(jnp.int32, (1, LANES), 1)
    inverse = jnp.exp((lane % half).astype(f32) * (-math.log(rope_base) / half))
    angles = positions.astype(f32)[:, None] * inverse
    sign = jnp.where(lane % HEAD_DIM < half, -1.0, 1.0).astype(f32)
    return jnp.cos(angles), jnp.sin(angles) * sign


def halves_swapped(u):
    half = HEAD_DIM // 2
    lane = lax.broadcasted_iota(jnp.int32, u.shape, 1)
    return jnp.where(
        lane % HEAD_DIM < half, pltpu.roll(u, LANES - half, 1), pltpu.roll(u, half, 1)
    )


def head_lanes(u, head):
    lane = lax.broadcasted_iota(jnp.int32, u.shape, 1)
    return jnp.where(lane // HEAD_DIM == head, u, jnp.zeros_like(u))


def dot_nt(a, b):
    return lax.dot_general(a, b, (((1,), (1,)), ((), ())), preferred_element_type=f32)


def dot_tn(a, b):
    return lax.dot_general(a, b, (((0,), (0,)), ((), ())), preferred_element_type=f32)


def dot_nn(a, b):
    return jnp.dot(a, b, preferred_element_type=f32)


def softmax_block(q_head, k_rows, begin, first_key, starts):
    scores = dot_nt(q_head, k_rows) * (HEAD_DIM ** (-0.5))
    row = begin + lax.broadcasted_iota(jnp.int32, scores.shape, 0)
    col = first_key + lax.broadcasted_iota(jnp.int32, scores.shape, 1)
    allowed = (col <= row) & (col >= starts)
    scores = jnp.where(allowed, scores, masked_score)
    expo = jnp.exp(scores - jnp.max(scores, axis=1, keepdims=True))
    return expo / jnp.sum(expo, axis=1, keepdims=True)


def key_range(begin):
    return max(0, (begin - REACH + 1) // BLOCK * BLOCK), begin + BLOCK


def attend_kernel(
    start_ref, cos_ref, sin_ref, q_ref, k_ref, v_ref, first_ref,
    out_ref, q_rot_ref, k_rot_ref, blend_ref,
):
    cosine, sine = cos_ref[...], sin_ref[...]
    queries, keys = q_ref[...], k_ref[...]
    q_rot = (queries * cosine + halves_swapped(queries) * sine).astype(bf16)
    k_rot = (keys * cosine + halves_swapped(keys) * sine).astype(bf16)
    blended = (0.5 * v_ref[...] + 0.5 * first_ref[...].astype(f32)).astype(bf16)
    q_rot_ref[...] = q_rot
    k_rot_ref[...] = k_rot
    blend_ref[...] = blended
    for begin in range(0, q_rot.shape[0], BLOCK):
        low, high = key_range(begin)
        starts = start_ref[begin : begin + BLOCK, :]
        total = jnp.zeros((BLOCK, LANES), f32)
        for head in range(LANES // HEAD_DIM):
            q_head = head_lanes(q_rot[begin : begin + BLOCK, :], head)
            probs = softmax_block(q_head, k_rot[low:high, :], begin, low, starts)
            total = total + dot_nn(probs.astype(bf16), head_lanes(blended[low:high, :], head))
        out_ref[begin : begin + BLOCK, :] = total.astype(bf16)


def attend_back_kernel(
    start_ref, cos_ref, sin_ref, q_rot_ref, k_rot_ref, blend_ref, grad_ref,
    dq_ref, dk_ref, dv_ref, dk_sum, dv_sum,
):
    scale = HEAD_DIM ** (-0.5)
    cosine, sine = cos_ref[...], sin_ref[...]
    q_rot, k_rot, blended, grads = q_rot_ref[...], k_rot_ref[...], blend_ref[...], grad_ref[...]
    dk_sum[...] = jnp.zeros_like(dk_sum)
    dv_sum[...] = jnp.zeros_like(dv_sum)
    for begin in range(0, q_rot.shape[0], BLOCK):
        low, high = key_range(begin)
        rows = slice(begin, begin + BLOCK)
        starts = start_ref[rows, :]
        dq = jnp.zeros((BLOCK, LANES), f32)
        for head in range(LANES // HEAD_DIM):
            q_head = head_lanes(q_rot[rows, :], head)
            k_head = head_lanes(k_rot[low:high, :], head)
            g_head = head_lanes(grads[rows, :], head)
            probs = softmax_block(q_head, k_rot[low:high, :], begin, low, starts)
            grad_probs = dot_nt(g_head, blended[low:high, :])
            inner = jnp.sum(probs * grad_probs, axis=1, keepdims=True)
            grad_scores = (probs * (grad_probs - inner)).astype(bf16)
            dq = dq + dot_nn(grad_scores, k_head)
            dk_sum[low:high, :] += dot_tn(grad_scores, q_head)
            dv_sum[low:high, :] += dot_tn(probs.astype(bf16), g_head)
        dq = dq * scale
        dq_ref[rows, :] = (
            dq * cosine[rows, :] - halves_swapped(dq) * sine[rows, :]
        ).astype(bf16)
    dk = dk_sum[...] * scale
    dk_ref[...] = (dk * cosine - halves_swapped(dk) * sine).astype(bf16)
    dv_ref[...] = (0.5 * dv_sum[...]).astype(bf16)


def attend(starts, cosine, sine, qkv, first, length):
    tokens, width = first.shape
    pairs = width // LANES
    per_row = lambda lanes: pl.BlockSpec((length, lanes), lambda r, h: (r, 0))
    part = lambda k: pl.BlockSpec((length, LANES), lambda r, h: (r, k * pairs + h))
    return pl.pallas_call(
        attend_kernel,
        grid=(tokens // length, pairs),
        in_specs=[per_row(1), per_row(LANES), per_row(LANES), part(0), part(1), part(2), part(0)],
        out_specs=[part(0)] * 4,
        out_shape=[jax.ShapeDtypeStruct((tokens, width), bf16)] * 4,
        name="attend",
    )(starts, cosine, sine, qkv, qkv, qkv, first)


def attend_back(starts, cosine, sine, q_rot, k_rot, blended, grads, length):
    tokens, width = grads.shape
    per_row = lambda lanes: pl.BlockSpec((length, lanes), lambda r, h: (r, 0))
    part = pl.BlockSpec((length, LANES), lambda r, h: (r, h))
    return pl.pallas_call(
        attend_back_kernel,
        grid=(tokens // length, width // LANES),
        in_specs=[per_row(1), per_row(LANES), per_row(LANES)] + [part] * 4,
        out_specs=[part] * 3,
        out_shape=[jax.ShapeDtypeStruct((tokens, width), bf16)] * 3,
        scratch_shapes=[pltpu.VMEM((length, LANES), f32)] * 2,
        name="attend_back",
    )(starts, cosine, sine, q_rot, k_rot, blended, grads)


def norm_stats(values):
    return lax.rsqrt(jnp.mean(values * values, axis=-1, keepdims=True) + eps_norm)


def norm_backward(values, inverse, gain_f, grad_out):
    scaled = values * inverse
    grad_scaled = grad_out * gain_f
    grad_gain = jnp.sum(grad_out * scaled, axis=0)
    grad_values = inverse * (
        grad_scaled - scaled * jnp.mean(grad_scaled * scaled, axis=-1, keepdims=True)
    )
    return grad_values, grad_gain


def shards(
    hidden_in, value_first, segment_ids, attn_gain, w_query, w_key, w_value, w_output,
    mlp_gain, w_gate, w_up, w_down, out_grad, v1_grad_acc,
):
    length, width = hidden_in.shape[1:]
    dp, fsdp = lax.axis_size("dp"), lax.axis_size("fsdp")
    core = lax.axis_index("dp") % 2
    hw = width // 2
    ff_half = w_gate.shape[1] // 2

    def swap(values):
        return lax.ppermute(values, "dp", [(i, i ^ 1) for i in range(dp)])

    def other_chip(values):
        total = values
        for step in range(1, dp // 2):
            total = total + lax.ppermute(
                values, "dp", [(i, (i + 2 * step) % dp) for i in range(dp)]
            )
        return total

    def pair(values):
        return jnp.concatenate([values, swap(values)], axis=0)

    def cols(values, which):
        half = values.shape[-1] // 2
        return lax.dynamic_slice_in_dim(values, which * half, half, values.ndim - 1)

    def rows(values, which):
        half = values.shape[0] // 2
        return lax.dynamic_slice_in_dim(values, which * half, half, 0)

    def in_order(mine, other, axis):
        return jnp.concatenate(
            [jnp.where(core == 0, mine, other), jnp.where(core == 0, other, mine)], axis=axis
        )

    def rows_from_cols(mine):
        return in_order(rows(mine, core), swap(rows(mine, 1 - core)), 1)

    def cols_from_rows(mine):
        return in_order(cols(mine, core), swap(cols(mine, 1 - core)), 0)

    def gather(shard):
        return lax.all_gather(shard, "fsdp", axis=0, tiled=True)

    def scatter(whole):
        return lax.psum_scatter(whole, "fsdp", scatter_dimension=0, tiled=True)

    def mine_and_partner(partial):
        return partial[:length] + swap(partial[length:].astype(bf16)).astype(f32)

    gains = jnp.stack([attn_gain, mlp_gain])
    gains = jnp.pad(gains, ((0, w_query.shape[0] - 2), (0, max(0, LANES - gains.shape[1]))))
    shard_a = jnp.concatenate(
        [cols(w, core) for w in (w_query, w_key, w_value, w_output)] + [gains], axis=1
    )
    shard_b = jnp.concatenate([cols(w_gate, core), cols(w_up, core)], axis=1)
    whole_a = gather(shard_a)
    whole_b = gather(shard_b)
    whole_d = gather(cols(w_down, core))
    qkv_mat = whole_a[:, : 3 * hw]
    output_mat = rows_from_cols(whole_a[:, 3 * hw : 4 * hw])
    gain_rows = whole_a[:, 4 * hw :].reshape(fsdp, w_query.shape[0], -1)
    gain_one = gain_rows[:, 0, : attn_gain.shape[0]].reshape(1, width).astype(f32)
    gain_two = gain_rows[:, 1, : attn_gain.shape[0]].reshape(1, width).astype(f32)
    down_mat = rows_from_cols(whole_d)

    segments = pair(segment_ids)
    positions = positions_of(segments)
    starts = (lax.broadcasted_iota(jnp.int32, positions.shape, 1) - positions).reshape(-1, 1)
    cosine, sine = rope_tables(positions.reshape(-1))
    hidden = pair(hidden_in[0]).astype(f32)
    first = value_first[0]
    first_half = jnp.concatenate([cols(first, core), swap(cols(first, 1 - core))], axis=0)
    cotangent = pair(out_grad[0])

    inverse_one = norm_stats(hidden)
    normed = (hidden * inverse_one * gain_one).astype(bf16)
    qkv = dot_nn(normed, qkv_mat)
    attended, q_rot, k_rot, blended = attend(starts, cosine, sine, qkv, first_half, length)
    first_f, blended_f = first.astype(f32), blended.astype(f32)
    square_first, square_blend = jnp.sum(first_f * first_f), jnp.sum(blended_f * blended_f)

    mixed = hidden[:length] + mine_and_partner(dot_nn(attended, output_mat))
    inverse_two = norm_stats(mixed)
    normed_two = pair((mixed * inverse_two * gain_two).astype(bf16))
    gate = dot_nn(normed_two, whole_b[:, :ff_half])
    up_val = dot_nn(normed_two, whole_b[:, ff_half:])
    sigma = jax.nn.sigmoid(gate)
    silu_gate = gate * sigma
    act = (silu_gate * up_val).astype(bf16)
    block_out = (mixed + mine_and_partner(dot_nn(act, down_mat))).astype(bf16)[None]

    grad_down = scatter(cols_from_rows(dot_tn(act, cotangent).astype(bf16)))
    grad_act = dot_nt(cotangent, down_mat)
    grad_gate = (grad_act * up_val * sigma * (1.0 + gate * (1.0 - sigma))).astype(bf16)
    grad_upv = (grad_act * silu_gate).astype(bf16)
    grad_b = scatter(
        jnp.concatenate(
            [dot_tn(normed_two, grad_gate).astype(bf16), dot_tn(normed_two, grad_upv).astype(bf16)],
            axis=1,
        )
    )
    grad_normed_two = mine_and_partner(
        dot_nt(grad_gate, whole_b[:, :ff_half]) + dot_nt(grad_upv, whole_b[:, ff_half:])
    )
    grad_mixed_norm, grad_gain_two = norm_backward(mixed, inverse_two, gain_two, grad_normed_two)
    grad_mixed = out_grad[0].astype(f32) + grad_mixed_norm
    grad_attn = pair(grad_mixed.astype(bf16))
    grad_out_w = cols_from_rows(dot_tn(attended, grad_attn).astype(bf16))
    grad_attended = dot_nt(grad_attn, output_mat).astype(bf16)
    dq, dk, dv = attend_back(starts, cosine, sine, q_rot, k_rot, blended, grad_attended, length)
    grad_a = scatter(
        jnp.concatenate(
            [dot_tn(normed, d).astype(bf16) for d in (dq, dk, dv)] + [grad_out_w], axis=1
        )
    )
    grad_normed = mine_and_partner(
        dot_nt(dq, qkv_mat[:, :hw]) + dot_nt(dk, qkv_mat[:, hw : 2 * hw])
        + dot_nt(dv, qkv_mat[:, 2 * hw :])
    )
    grad_rows_norm, grad_gain_one = norm_backward(
        hidden[:length], inverse_one[:length], gain_one, grad_normed
    )
    input_grad = (grad_mixed + grad_rows_norm)[None]
    grad_first = in_order(dv[:length], swap(dv[length:]), 1)
    v1_grad_out = v1_grad_acc + grad_first.astype(f32)[None]

    small = jnp.concatenate(
        [grad_gain_one, grad_gain_two, jnp.stack([square_first, square_blend])]
    )
    small = lax.psum(small, ("dp", "fsdp"))
    at = lax.axis_index("fsdp") * attn_gain.shape[0]
    share_gain_one = lax.dynamic_slice_in_dim(small[:width], at, attn_gain.shape[0])
    share_gain_two = lax.dynamic_slice_in_dim(small[width : 2 * width], at, attn_gain.shape[0])
    count = f32(dp * fsdp * length * width)
    value_norms = jnp.sqrt(small[2 * width :] / count)

    grad_down = other_chip(grad_down)
    grad_b = other_chip(grad_b)
    grad_a = other_chip(grad_a)

    def whole_columns(mine, other):
        return in_order(mine, other, 1).astype(f32)

    other_down, other_b, other_a = swap(grad_down), swap(grad_b), swap(grad_a)
    share_query, share_key, share_value, share_output = (
        whole_columns(grad_a[:, k * hw : (k + 1) * hw], other_a[:, k * hw : (k + 1) * hw])
        for k in range(4)
    )
    share_gate, share_up = (
        whole_columns(
            grad_b[:, k * ff_half : (k + 1) * ff_half], other_b[:, k * ff_half : (k + 1) * ff_half]
        )
        for k in range(2)
    )
    share_down = whole_columns(grad_down, other_down)
    return (
        block_out, input_grad, share_gain_one, share_query, share_key, share_value, share_output,
        share_gain_two, share_gate, share_up, share_down, v1_grad_out, value_norms,
    )


def solution(mesh):
    tokens = ("dp", "fsdp")
    in_specs = (
        P(tokens, None, None), P(tokens, None, None), P(tokens, None), P("fsdp"),
        P("fsdp", None), P("fsdp", None), P("fsdp", None), P("fsdp", None), P("fsdp"),
        P("fsdp", None), P("fsdp", None), P("fsdp", None), P(tokens, None, None),
        P(tokens, None, None),
    )
    out_specs = (
        P(tokens, None, None), P(tokens, None, None), P("fsdp"), P("fsdp", None),
        P("fsdp", None), P("fsdp", None), P("fsdp", None), P("fsdp"), P("fsdp", None),
        P("fsdp", None), P("fsdp", None), P(tokens, None, None), P(),
    )
    return jax.shard_map(shards, mesh=mesh, in_specs=in_specs, out_specs=out_specs, check_vma=False)
```

time: 1230 us -> 600 us (0.49)
  waiting for transfers between devices: 892 us -> 295 us
  blocking collectives: 105 us -> 39.4 us
  matrix products: 146 us -> 81 us
  Pallas kernels: 0 us -> 56.4 us
  other arithmetic: 43.2 us -> 67.2 us
    reduce_scatter x7 -> x3, waiting for transfers between devices: 495 us -> 117 us  [scatter(): return lax.psum_scatter(whole, 'fsdp', scatter_dimension=0, tiled=True)]
    all_gather x7 -> x3, waiting for transfers between devices: 372 us -> 161 us  [gather(): return lax.all_gather(shard, 'fsdp', axis=0, tiled=True)]
    dot_general x27 -> x19, matrix products: 146 us -> 81 us  [the longest x5 32.5 us: dot_nn(): return jnp.dot(a, b, preferred_element_type=f32)]
    pallas_call x0 -> x2, Pallas kernels: none -> 56.4 us  [the longest x1 35.3 us: attend_back(): pl.pallas_call(attend_back_kernel, grid=(tokens // length, width // LANES...]
    all_gather x2 -> x0, blocking collectives: 39.1 us -> none  [the longest x1 22.4 us: shards(): lax.all_gather(attn_gain, 'fsdp', axis=0, tiled=True)]
    concatenate x0 -> x9, other arithmetic: none -> 22.6 us  [the longest x1 15.2 us: shards(): jnp.concatenate([dot_tn(normed, d).astype(bf16) for d in (dq, dk, dv)] +...]
    psum x1 -> x0, waiting for transfers between devices: 21.4 us -> none  [shards(): lax.psum(share_query.astype(jnp.bfloat16), 'dp').astype(jnp.float32)]
    unnamed x1 -> x0, blocking collectives: 19.8 us -> none
  transfers between devices with their start and end apart: 15 -> 27, of which waited for: 14 -> 9; matrix products, arithmetic and copies ran while one was open for 14% -> 23% of each run, Pallas kernels for 0% -> 10%
where the time goes in v1:
time: 600 us; the launch traced here: 591 us
  waiting for transfers between devices  295 us (49%)
  matrix products  81 us (14%)
  other arithmetic  67.2 us (11%)
  Pallas kernels  56.4 us (9%)
  blocking collectives  39.4 us (7%)
  local copies, waits for them, and re-layouts  26.9 us (4%)
  between operations  15.3 us (3%)
  starting transfers between devices  9.84 us (2%)
    all_gather x3, waiting for transfers between devices, gather(): return lax.all_gather(shard, 'fsdp', axis=0, tiled=True)  161 us
    reduce_scatter x3, waiting for transfers between devices, scatter(): return lax.psum_scatter(whole, 'fsdp', scatter_dimension=0, tiled=True)  117 us
    psum x1, blocking collectives, shards(): small = lax.psum(small, ('dp', 'fsdp'))  39.4 us
    pallas_call x1, Pallas kernels, attend_back(): pl.pallas_call(attend_back_kernel, grid=(tokens // length, width // LANES...  35.3 us
    dot_general x5, matrix products, dot_nn(): return jnp.dot(a, b, preferred_element_type=f32)  32.5 us
    dot_general x7, matrix products, dot_tn(): lax.dot_general(a, b, (((0,), (0,)), ((), ())), preferred_element_type=f32)  26.7 us
    dot_general x7, matrix products, dot_nt(): lax.dot_general(a, b, (((1,), (1,)), ((), ())), preferred_element_type=f32)  21.9 us
    pallas_call x1, Pallas kernels, attend(): pl.pallas_call(attend_kernel, grid=(tokens // length, pairs), in_specs=[p...  21.1 us
  transfers between devices with their start and end apart: 27, of which 9 were waited for; matrix products, arithmetic and copies ran while one was open for 23% of the time, Pallas kernels for 10%

profile of v1, /device:TPU:0, one launch (start us, length us, event | category | flops | bytes accessed | tf_op | source)
XLA Modules:
  0.0 591.1 jit_solution(3075583607692270248)
XLA Ops:
  17.1 2.3 collective-permute-done.1
  21.6 3.0 fusion.26
  25.7 1.7 multiply_reduce_fusion
  27.4 64.3 %all-gather.4.cloned.1.call-done = bf16[1024,2176]{1,0:T(8,128)(2,1)} async-done(((bf16[128,2176]{1,0:T(8,128)(2,1)}), bf16[1024,2176]{1,0:T(8,128)(2,1)}) %all-gather.4.cloned.1.call-update) | async-done | bytes 4456464 | tf_op jit(solution)/shard_map/all_gather | solution.py:223
  93.2 8.4 %fusion.1.q_ref.k_ref.v_ref = f32[1024,1536]{1,0:T(8,128)} fusion(bf16[1024,2176]{1,0:T(8,128)(2,1)} %all-gather.4.cloned.1.call-done, f32[1024]{0:T(1024)S(1)} %bitcast.60, f32[1024]{0:T(1024)S(1)} %add_rsqrt_fusion, bf16[512,1024]{1,0:T(8,128)(2,1)} %collective-permute-done, bf16[512,1024]{1,0:T(8,128)(2,1)S(1)} %bitcast.47), kind=kOutput, calls=%fused_computation.13 | convolution fusion | flops 3228565504 | bytes 11542528 | tf_op jit(solution)/shard_map/dot_general | solution.py:61
  101.6 21.1 %attend.1 = (bf16[1024,512]{1,0:T(8,128)(2,1)}, bf16[1024,512]{1,0:T(8,128)(2,1)}, bf16[1024,512]{1,0:T(8,128)(2,1)}, bf16[1024,512]{1,0:T(8,128)(2,1)}) custom-call(s32[1024,1]{1,0:T(8,128)} %copy.30.start_ref, f32[1024,128]{1,0:T(8,128)} %get-tuple-element.70.cos_ref, f32[1024,128]{1,0:T(8,128)} %get-tuple-element.69.sin_ref, ...), custom_call_target="tpu_custom_call" | custom-call | tf_op jit(solution)/shard_map/attend/pallas_call | solution.py:140
  124.0 2.5 fusion.25
  126.4 2.1 copy-done.6
  129.2 21.1 %all-gather.8.cloned.1.call-done = bf16[2816,512]{1,0:T(8,128)(2,1)} async-done(((bf16[352,512]{1,0:T(8,128)(2,1)}), bf16[2816,512]{1,0:T(8,128)(2,1)}) %all-gather.8.cloned.1.call-update) | async-done | bytes 2883600 | tf_op jit(solution)/shard_map/all_gather | solution.py:223
  150.3 1.5 constant_dynamic-slice_fusion.2
  152.3 1.9 maximum_convert_fusion
  154.3 2.5 multiply_reduce_fusion.7
  161.7 7.1 %fusion.17 = f32[1024,1408]{1,0:T(8,128)} fusion(bf16[1408,512]{1,0:T(8,128)(2,1)S(1)} %get-tuple-element.41, bf16[1408,512]{1,0:T(8,128)(2,1)S(1)} %get-tuple-element.40, bf16[512,1024]{1,0:T(8,128)(2,1)S(1)} %collective-permute-done.8, bf16[512,1024]{1,0:T(8,128)(2,1)} %bitcast.13), kind=kOutput, calls=%fused_computation.53 | convolution fusion | flops 2962751488 | bytes 10747904 | tf_op jit(solution)/shard_map/dot_general | solution.py:53
  168.8 75.3 %all-gather.6.cloned.1.call-done = bf16[1024,2816]{1,0:T(8,128)(2,1)} async-done(((bf16[128,2816]{1,0:T(8,128)(2,1)}), bf16[1024,2816]{1,0:T(8,128)(2,1)}) %all-gather.6.cloned.1.call-update) | async-done | bytes 5767184 | tf_op jit(solution)/shard_map/all_gather | solution.py:223
  244.0 6.0 %fusion.5 = f32[1024,1408]{1,0:T(8,128)S(1)} fusion(bf16[1024,2816]{1,0:T(8,128)(2,1)} %all-gather.6.cloned.1.call-done, bf16[512,1024]{1,0:T(8,128)(2,1)} %collective-permute-done.5, bf16[512,1024]{1,0:T(8,128)(2,1)} %multiply_convert_fusion.4), kind=kOutput, calls=%fused_computation.19 | convolution fusion | flops 2956984320 | bytes 10747904 | tf_op jit(solution)/shard_map/dot_general | solution.py:61
  250.1 9.5 %multiply_convert_fusion.1 = (bf16[1024,1408]{1,0:T(8,128)(2,1)}, bf16[1024,1408]{1,0:T(8,128)(2,1)}, bf16[1024,1408]{1,0:T(8,128)(2,1)}) fusion(f32[1024,1408]{1,0:T(8,128)S(1)} %copy-done.31, f32[1024,1408]{1,0:T(8,128)S(1)} %fusion.5, bf16[1024,2816]{1,0:T(8,128)(2,1)S(1)} %copy-done.25, bf16[512,1024]{1,0:T(8,128)(2,1)} %collective-permute-done.5, ...), kind=kOutput, calls=%fused_computation.2 | convolution fusion | flops 2978611200 | bytes 25165824 | tf_op jit(solution)/shard_map/dot_general | solution.py:61
  259.5 5.3 convolution_convert_fusion
  265.1 1.6 copy-done.33
  266.7 3.4 fusion.3
  270.1 3.4 fusion.14
  276.0 1.8 pad_maximum_fusion.2
  278.0 6.2 %fusion.18 = f32[1024,1024]{1,0:T(8,128)S(1)} fusion(bf16[1024,1408]{1,0:T(8,128)(2,1)} %get-tuple-element.37, bf16[1408,512]{1,0:T(8,128)(2,1)} %copy-done.19, bf16[1408,512]{1,0:T(8,128)(2,1)} %copy-done.18), kind=kOutput, calls=%fused_computation.54 | convolution fusion | flops 2958557184 | bytes 9961472 | tf_op jit(solution)/shard_map/dot_general | solution.py:61
  284.6 2.0 multiply_reduce_fusion.3
  287.1 4.2 fusion.42
  291.5 2.5 collective-permute-done.10
  296.3 2.3 convolution_convert_fusion.7.grad_ref
  298.6 35.3 %attend_back.1 = (bf16[1024,512]{1,0:T(8,128)(2,1)}, bf16[1024,512]{1,0:T(8,128)(2,1)}, bf16[1024,512]{1,0:T(8,128)(2,1)}) custom-call(s32[1024,1]{1,0:T(8,128)} %copy.30.start_ref, f32[1024,128]{1,0:T(8,128)} %get-tuple-element.70.cos_ref, f32[1024,128]{1,0:T(8,128)} %get-tuple-element.69.sin_ref, bf16[1024,512]{1,0:T(8,128)(2,1)} %get-tuple-element.21.q_rot_ref, ...), custom_call_target="tpu_custom_call" | custom-call | tf_op jit(solution)/shard_map/attend_back/pallas_call | solution.py:154
  333.8 3.0 convolution_convert_fusion.4
  336.9 2.7 convolution_convert_fusion.5
  339.7 2.6 convolution_convert_fusion.6
  343.6 15.2 %maximum_maximum_fusion = bf16[1024,2048]{1,0:T(8,128)(2,1)} fusion(bf16[512,512]{1,0:T(8,128)(2,1)S(1)} %get-tuple-element.46, bf16[512,512]{1,0:T(8,128)(2,1)S(1)} %get-tuple-element.45, bf16[1024,512]{1,0:T(8,128)(2,1)S(1)} %convolution_convert_fusion.4, bf16[1024,512]{1,0:T(8,128)(2,1)S(1)} %convolution_convert_fusion.5, ...), kind=kLoop, calls=%fused_computation.6 | loop fusion | flops 20971520 | bytes 8388608 | tf_op jit(solution)/shard_map/concatenate | solution.py:293
  358.8 6.1 %convolution_convert_fusion.2 = bf16[1024,1408]{1,0:T(8,128)(2,1)S(1)} fusion(bf16[1024,1408]{1,0:T(8,128)(2,1)} %get-tuple-element.35, bf16[512,1024]{1,0:T(8,128)(2,1)} %collective-permute-done.5, bf16[512,1024]{1,0:T(8,128)(2,1)} %multiply_convert_fusion.4), kind=kOutput, calls=%fused_computation.12 | convolution fusion | flops 2958426112 | bytes 7864320 | tf_op jit(solution)/shard_map/dot_general | solution.py:57
  364.9 5.6 convolution_convert_fusion.1
  370.5 2.9 pad_maximum_fusion
  375.1 3.1 fusion.21
  380.9 2.0 copy-done.4
  385.2 2.5 multiply_reduce_fusion.1
  387.8 3.5 convert_add_fusion
  391.4 2.2 multiply_reduce_fusion.4
  393.6 1.4 concatenate.107
  394.9 39.4 %psum.7 = f32[2050]{0:T(1024)S(1)} all-reduce(f32[2050]{0:T(1024)S(1)} %concatenate.107), channel_id=1, replica_groups=mesh['dp'=4,'fsdp'=8] {'dp','fsdp'}, use_global_device_ids=true, to_apply=%region_10.11 | all-reduce | flops 2050 | bytes 16400 | tf_op jit(solution)/shard_map/psum | solution.py:311
  434.3 2.3 collective-permute-start.18
  436.6 9.7 %reduce-scatter.4.cloned.1.call-done = bf16[128,2048]{1,0:T(8,128)(2,1)} async-done(((bf16[1024,2048]{1,0:T(8,128)(2,1)}), bf16[128,2048]{1,0:T(8,128)(2,1)}) %reduce-scatter.4.cloned.1.call-update) | async-done | bytes 524304 | tf_op jit(solution)/shard_map/reduce_scatter | solution.py:226
  446.3 1.5 collective-permute-start.13
  447.8 4.5 add_bitcast_fusion
  452.5 107.6 %reduce-scatter.6.cloned.1.call-done = bf16[128,2816]{1,0:T(8,128)(2,1)} async-done(((bf16[1024,2816]{1,0:T(8,128)(2,1)}), bf16[128,2816]{1,0:T(8,128)(2,1)}) %reduce-scatter.6.cloned.1.call-update) | async-done | bytes 720912 | tf_op jit(solution)/shard_map/reduce_scatter | solution.py:226
  560.1 1.5 collective-permute-start.15
  565.8 11.6 %collective-permute-done.15 = bf16[128,2816]{1,0:T(8,128)(2,1)S(1)} collective-permute-done((bf16[128,2816]{1,0:T(8,128)(2,1)}, bf16[128,2816]{1,0:T(8,128)(2,1)S(1)}, u32[]{:S(2)}, u32[]{:S(2)}) %collective-permute-start.15) | collective-permute-done | bytes 720928 | tf_op jit(solution)/shard_map/ppermute | solution.py:195
  (190 shorter events, 46.9 us)
Async XLA Ops:
  7.2 5.6 copy-start
  7.2 84.5 %all-gather.4.cloned.1.call-start = ((), (), s32[]{:S(2)}) async-start(), calls=%async_computation.3 | async-start | bytes 5013504 | tf_op jit(solution)/shard_map/all_gather | solution.py:223
  9.2 6.6 %copy-start.14 = (bf16[1,512,1024]{2,1,0:T(8,128)(2,1)S(1)}, bf16[1,512,1024]{2,1,0:T(8,128)(2,1)}, u32[]{:S(2)}) copy-start(bf16[1,512,1024]{2,1,0:T(8,128)(2,1)} %param.14) | copy-start | bytes 3145732
  9.2 7.2 %copy-start.12 = (bf16[1,512,1024]{2,1,0:T(8,128)(2,1)S(1)}, bf16[1,512,1024]{2,1,0:T(8,128)(2,1)}, u32[]{:S(2)}) copy-start(bf16[1,512,1024]{2,1,0:T(8,128)(2,1)} %param.15) | copy-start | bytes 3145732
  12.7 137.6 %all-gather.8.cloned.1.call-start = ((), (), s32[]{:S(2)}) async-start(), calls=%async_computation.5 | async-start | bytes 3244032 | tf_op jit(solution)/shard_map/all_gather | solution.py:223
  13.6 230.5 %all-gather.6.cloned.1.call-start = ((), (), s32[]{:S(2)}) async-start(), calls=%async_computation.4 | async-start | bytes 6488064 | tf_op jit(solution)/shard_map/all_gather | solution.py:223
  15.7 418.6 %reduce-scatter.8.cloned.1.call-start = ((), (), s32[]{:S(2)}) async-start(), calls=%async_computation.8 | async-start | bytes 3244032 | tf_op jit(solution)/shard_map/reduce_scatter | solution.py:226
  15.8 9.9 %collective-permute-start = (bf16[512,1024]{1,0:T(8,128)(2,1)S(1)}, bf16[512,1024]{1,0:T(8,128)(2,1)}, u32[]{:S(2)}, u32[]{:S(2)}) collective-permute-start(bf16[512,1024]{1,0:T(8,128)(2,1)S(1)} %bitcast.45), channel_id=1, source_target_pairs={{0,8},{8,0},{16,24},{24,16},{1,9},{9,1},{17,25},{25,17},{2,10},{10... | collective-permute-start | bytes 3145736 | tf_op jit(solution)/shard_map/ppermute | solution.py:190
  16.4 8.2 %collective-permute-start.2 = (bf16[512,512]{1,0:T(8,128)(2,1)S(1)}, bf16[512,512]{1,0:T(8,128)(2,1)S(1)}, u32[]{:S(2)}, u32[]{:S(2)}) collective-permute-start(bf16[512,512]{1,0:T(8,128)(2,1)S(1)} %get-tuple-element.62), channel_id=1, source_target_pairs={{0,8},{8,0},{16,24},{24,16},{1,9},{9,1},{17,25},{25,17},{2,10},{10... | collective-permute-start | bytes 1572872 | tf_op jit(solution)/shard_map/ppermute | solution.py:190
  16.6 2.8 collective-permute-start.1
  93.1 29.6 %collective-permute-start.3 = (bf16[512,512]{1,0:T(8,128)(2,1)S(1)}, bf16[512,512]{1,0:T(8,128)(2,1)}, u32[]{:S(2)}, u32[]{:S(2)}) collective-permute-start(bf16[512,512]{1,0:T(8,128)(2,1)S(1)} %constant_dynamic-slice_fusion.6), channel_id=1, source_target_pairs={{0,8},{8,0},{16,24},{24,16},{1,9},{9,1},{17,25},{25,17},{2,10},{10... | collective-permute-start | bytes 1572872 | tf_op jit(solution)/shard_map/ppermute | solution.py:190
  128.7 25.6 %collective-permute-start.4 = (bf16[512,1024]{1,0:T(8,128)(2,1)S(1)}, bf16[512,1024]{1,0:T(8,128)(2,1)}, u32[]{:S(2)}, u32[]{:S(2)}) collective-permute-start(bf16[512,1024]{1,0:T(8,128)(2,1)S(1)} %slice.299), channel_id=1, source_target_pairs={{0,8},{8,0},{16,24},{24,16},{1,9},{9,1},{17,25},{25,17},{2,10},{10... | collective-permute-start | bytes 3145736 | tf_op jit(solution)/shard_map/ppermute | solution.py:190
  151.7 6.8 %collective-permute-start.6 = (bf16[1408,512]{1,0:T(8,128)(2,1)S(1)}, bf16[1408,512]{1,0:T(8,128)(2,1)S(1)}, u32[]{:S(2)}, u32[]{:S(2)}) collective-permute-start(bf16[1408,512]{1,0:T(8,128)(2,1)S(1)} %constant_dynamic-slice_fusion.2), channel_id=1, source_target_pairs={{0,8},{8,0},{16,24},{24,16},{1,9},{9,1},{17,25},{25,17},{2,10},{10... | collective-permute-start | bytes 4325384 | tf_op jit(solution)/shard_map/ppermute | solution.py:190
  151.8 8.0 %collective-permute-start.8 = (bf16[512,1024]{1,0:T(8,128)(2,1)}, bf16[512,1024]{1,0:T(8,128)(2,1)S(1)}, u32[]{:S(2)}, u32[]{:S(2)}) collective-permute-start(bf16[512,1024]{1,0:T(8,128)(2,1)} %bitcast.13), channel_id=1, source_target_pairs={{0,8},{8,0},{16,24},{24,16},{1,9},{9,1},{17,25},{25,17},{2,10},{10... | collective-permute-start | bytes 3145736 | tf_op jit(solution)/shard_map/ppermute | solution.py:190
  158.1 86.0 %collective-permute-start.5 = (bf16[512,1024]{1,0:T(8,128)(2,1)}, bf16[512,1024]{1,0:T(8,128)(2,1)}, u32[]{:S(2)}, u32[]{:S(2)}) collective-permute-start(bf16[512,1024]{1,0:T(8,128)(2,1)} %multiply_convert_fusion.4), channel_id=1, source_target_pairs={{0,8},{8,0},{16,24},{24,16},{1,9},{9,1},{17,25},{25,17},{2,10},{10... | collective-permute-start | bytes 3145736 | tf_op jit(solution)/shard_map/ppermute | solution.py:190
  244.0 6.0 %copy-start.25 = (bf16[1024,2816]{1,0:T(8,128)(2,1)S(1)}, bf16[1024,2816]{1,0:T(8,128)(2,1)}, u32[]{:S(2)}) copy-start(bf16[1024,2816]{1,0:T(8,128)(2,1)} %all-gather.6.cloned.1.call-done) | copy-start | bytes 17301508
  244.0 6.0 %copy-start.31 = (f32[1024,1408]{1,0:T(8,128)S(1)}, f32[1024,1408]{1,0:T(8,128)}, u32[]{:S(2)}) copy-start(f32[1024,1408]{1,0:T(8,128)} %fusion.17) | copy-start | bytes 17301508
  250.0 9.5 %copy-start.30 = (bf16[512,1024]{1,0:T(8,128)(2,1)S(1)}, bf16[512,1024]{1,0:T(8,128)(2,1)}, u32[]{:S(2)}) copy-start(bf16[512,1024]{1,0:T(8,128)(2,1)} %copy-done.29) | copy-start | bytes 3145732
  265.0 9.8 %collective-permute-start.17 = (bf16[1408,512]{1,0:T(8,128)(2,1)S(1)}, bf16[1408,512]{1,0:T(8,128)(2,1)S(1)}, u32[]{:S(2)}, u32[]{:S(2)}) collective-permute-start(bf16[1408,512]{1,0:T(8,128)(2,1)S(1)} %constant_dynamic-slice_fusion), channel_id=1, source_target_pairs={{0,8},{8,0},{16,24},{24,16},{1,9},{9,1},{17,25},{25,17},{2,10},{10... | collective-permute-start | bytes 4325384 | tf_op jit(solution)/shard_map/ppermute | solution.py:190
  266.7 3.4 copy-start.32
  274.8 9.7 %collective-permute-start.9 = (bf16[512,1024]{1,0:T(8,128)(2,1)}, bf16[512,1024]{1,0:T(8,128)(2,1)}, u32[]{:S(2)}, u32[]{:S(2)}) collective-permute-start(bf16[512,1024]{1,0:T(8,128)(2,1)} %slice.297), channel_id=1, source_target_pairs={{0,8},{8,0},{16,24},{24,16},{1,9},{9,1},{17,25},{25,17},{2,10},{10... | collective-permute-start | bytes 3145736 | tf_op jit(solution)/shard_map/ppermute | solution.py:190
  277.7 168.6 %reduce-scatter.4.cloned.1.call-start = ((), (), s32[]{:S(2)}) async-start(), calls=%async_computation.6 | async-start | bytes 4718592 | tf_op jit(solution)/shard_map/reduce_scatter | solution.py:226
  278.0 6.6 %copy-start.10 = (f32[1024,1024]{1,0:T(8,128)S(1)}, f32[1024,1024]{1,0:T(8,128)}, u32[]{:S(2)}) copy-start(f32[1024,1024]{1,0:T(8,128)} %copy-done.9) | copy-start | bytes 12582916
  284.3 2.7 collective-permute-start.7
  286.5 7.4 %copy-start.17 = (bf16[1024,512]{1,0:T(8,128)(2,1)S(1)}, bf16[1024,512]{1,0:T(8,128)(2,1)}, u32[]{:S(2)}) copy-start(bf16[1024,512]{1,0:T(8,128)(2,1)} %get-tuple-element.20) | copy-start | bytes 3145732
  291.3 2.7 collective-permute-start.10
  296.1 46.2 %collective-permute-start.12 = (bf16[512,512]{1,0:T(8,128)(2,1)}, bf16[512,512]{1,0:T(8,128)(2,1)}, u32[]{:S(2)}, u32[]{:S(2)}) collective-permute-start(bf16[512,512]{1,0:T(8,128)(2,1)} %constant_dynamic-slice_fusion.1), channel_id=1, source_target_pairs={{0,8},{8,0},{16,24},{24,16},{1,9},{9,1},{17,25},{25,17},{2,10},{10... | collective-permute-start | bytes 1572872 | tf_op jit(solution)/shard_map/ppermute | solution.py:190
  298.6 35.3 %copy-start.15 = (bf16[1,512,1024]{2,1,0:T(8,128)(2,1)S(1)}, bf16[1,512,1024]{2,1,0:T(8,128)(2,1)}, u32[]{:S(2)}) copy-start(bf16[1,512,1024]{2,1,0:T(8,128)(2,1)} %param.14) | copy-start | bytes 3145732
  358.8 201.3 %reduce-scatter.6.cloned.1.call-start = ((), (), s32[]{:S(2)}) async-start(), calls=%async_computation.7 | async-start | bytes 6488064 | tf_op jit(solution)/shard_map/reduce_scatter | solution.py:226
  358.8 6.1 %copy-start.34 = (bf16[1024,1408]{1,0:T(8,128)(2,1)S(1)}, bf16[1024,1408]{1,0:T(8,128)(2,1)}, u32[]{:S(2)}) copy-start(bf16[1024,1408]{1,0:T(8,128)(2,1)} %get-tuple-element.36) | copy-start | bytes 8650756
  374.7 3.6 slice-start
  374.7 3.5 slice-start.1
  374.7 3.5 copy-start.27
  374.7 13.0 %collective-permute-start.20 = (bf16[512,512]{1,0:T(8,128)(2,1)S(1)}, bf16[512,512]{1,0:T(8,128)(2,1)S(1)}, u32[]{:S(2)}, u32[]{:S(2)}) collective-permute-start(bf16[512,512]{1,0:T(8,128)(2,1)S(1)} %slice.173), channel_id=1, source_target_pairs={{0,8},{8,0},{16,24},{24,16},{1,9},{9,1},{17,25},{25,17},{2,10},{10... | collective-permute-start | bytes 1572872 | tf_op jit(solution)/shard_map/ppermute | solution.py:190
  379.5 4.5 copy-start.13
  384.0 7.4 %collective-permute-start.11 = (bf16[512,1024]{1,0:T(8,128)(2,1)}, bf16[512,1024]{1,0:T(8,128)(2,1)}, u32[]{:S(2)}, u32[]{:S(2)}) collective-permute-start(bf16[512,1024]{1,0:T(8,128)(2,1)} %slice.296), channel_id=1, source_target_pairs={{0,8},{8,0},{16,24},{24,16},{1,9},{9,1},{17,25},{25,17},{2,10},{10... | collective-permute-start | bytes 3145736 | tf_op jit(solution)/shard_map/ppermute | solution.py:190
  385.2 6.2 %copy-start.5 = (f32[1024,1024]{1,0:T(8,128)S(1)}, f32[1024,1024]{1,0:T(8,128)}, u32[]{:S(2)}) copy-start(f32[1024,1024]{1,0:T(8,128)} %copy-done.4) | copy-start | bytes 12582916
  387.8 3.5 copy-start.3
  391.4 56.4 %copy-start.8 = (f32[512,1024]{1,0:T(8,128)S(1)}, f32[512,1024]{1,0:T(8,128)}, u32[]{:S(2)}) copy-start(f32[512,1024]{1,0:T(8,128)} %get-tuple-element.32) | copy-start | bytes 6291460
  434.3 18.0 %collective-permute-start.18 = (bf16[352,512]{1,0:T(8,128)(2,1)}, bf16[352,512]{1,0:T(8,128)(2,1)S(1)}, u32[]{:S(2)}, u32[]{:S(2)}) collective-permute-start(bf16[352,512]{1,0:T(8,128)(2,1)} %reduce-scatter.8.cloned.1.call-done), channel_id=1, source_target_pairs={{0,16},{8,24},{16,0},{24,8},{1,17},{9,25},{17,1},{25,9},{2,18},{10... | collective-permute-start | bytes 1081352 | tf_op jit(solution)/shard_map/ppermute | solution.py:195
  446.3 116.4 %collective-permute-start.13 = (bf16[128,2048]{1,0:T(8,128)(2,1)}, bf16[128,2048]{1,0:T(8,128)(2,1)}, u32[]{:S(2)}, u32[]{:S(2)}) collective-permute-start(bf16[128,2048]{1,0:T(8,128)(2,1)} %reduce-scatter.4.cloned.1.call-done), channel_id=1, source_target_pairs={{0,16},{8,24},{16,0},{24,8},{1,17},{9,25},{17,1},{25,9},{2,18},{10... | collective-permute-start | bytes 1572872 | tf_op jit(solution)/shard_map/ppermute | solution.py:195
  447.8 4.5 copy-start.23
  447.8 115.0 %copy-start.22 = (bf16[128,2048]{1,0:T(8,128)(2,1)S(1)}, bf16[128,2048]{1,0:T(8,128)(2,1)}, u32[]{:S(2)}) copy-start(bf16[128,2048]{1,0:T(8,128)(2,1)} %reduce-scatter.4.cloned.1.call-done) | copy-start | bytes 1572868
  452.4 112.1 %collective-permute-start.19 = (bf16[352,512]{1,0:T(8,128)(2,1)S(1)}, bf16[352,512]{1,0:T(8,128)(2,1)S(1)}, u32[]{:S(2)}, u32[]{:S(2)}) collective-permute-start(bf16[352,512]{1,0:T(8,128)(2,1)S(1)} %add.173), channel_id=1, source_target_pairs={{0,8},{8,0},{16,24},{24,16},{1,9},{9,1},{17,25},{25,17},{2,10},{10... | collective-permute-start | bytes 1081352 | tf_op jit(solution)/shard_map/ppermute | solution.py:190
  560.1 17.4 %copy-start.21 = (bf16[128,2816]{1,0:T(8,128)(2,1)S(1)}, bf16[128,2816]{1,0:T(8,128)(2,1)}, u32[]{:S(2)}) copy-start(bf16[128,2816]{1,0:T(8,128)(2,1)} %reduce-scatter.6.cloned.1.call-done) | copy-start | bytes 2162692
  560.1 17.4 %collective-permute-start.15 = (bf16[128,2816]{1,0:T(8,128)(2,1)}, bf16[128,2816]{1,0:T(8,128)(2,1)S(1)}, u32[]{:S(2)}, u32[]{:S(2)}) collective-permute-start(bf16[128,2816]{1,0:T(8,128)(2,1)} %reduce-scatter.6.cloned.1.call-done), channel_id=1, source_target_pairs={{0,16},{8,24},{16,0},{24,8},{1,17},{9,25},{17,1},{25,9},{2,18},{10... | collective-permute-start | bytes 2162696 | tf_op jit(solution)/shard_map/ppermute | solution.py:195
  563.9 13.9 %collective-permute-start.14 = (bf16[128,2048]{1,0:T(8,128)(2,1)S(1)}, bf16[128,2048]{1,0:T(8,128)(2,1)S(1)}, u32[]{:S(2)}, u32[]{:S(2)}) collective-permute-start(bf16[128,2048]{1,0:T(8,128)(2,1)S(1)} %add.171), channel_id=1, source_target_pairs={{0,8},{8,0},{16,24},{24,16},{1,9},{9,1},{17,25},{25,17},{2,10},{10... | collective-permute-start | bytes 1572872 | tf_op jit(solution)/shard_map/ppermute | solution.py:190
  577.7 3.6 collective-permute-start.16
  (17 other events, 35.0 us)
Sparse Core Ops, SparseCore 0:
  12.8 78.8 all-gather.3
  94.5 55.7 all-gather.7
  153.0 90.9 all-gather.5
  277.9 70.5 reduce-scatter.7
  358.9 87.3 reduce-scatter.3
  449.8 110.2 reduce-scatter.5

commit v2 on v1

--- a/solution.py
+++ b/solution.py
@@ -5,6 +5,7 @@
 import jax.numpy as jnp
 from jax import lax
 from jax.experimental import pallas as pl
+from jax.experimental.layout import Layout, with_layout_constraint
 from jax.experimental.pallas import tpu as pltpu
 from jax.sharding import PartitionSpec as P
 
@@ -47,6 +48,10 @@
 def head_lanes(u, head):
     lane = lax.broadcasted_iota(jnp.int32, u.shape, 1)
     return jnp.where(lane // HEAD_DIM == head, u, jnp.zeros_like(u))
+
+
+def row_major(values):
+    return with_layout_constraint(values, Layout(major_to_minor=(0, 1)))
 
 
 def dot_nt(a, b):
@@ -162,6 +167,54 @@
     )(starts, cosine, sine, q_rot, k_rot, blended, grads)
 
 
+def order_kernel(at_ref, *refs):
+    *pieces, out_ref = refs
+    count = len(pieces)
+    for step, piece in enumerate(pieces):
+        out_ref[lax.rem(at_ref[0] + count - step, count)] = piece[...]
+
+
+def in_ring_order(place, pieces):
+    in_vmem = pl.BlockSpec(memory_space=pltpu.VMEM)
+    return pl.pallas_call(
+        order_kernel,
+        in_specs=[pl.BlockSpec(memory_space=pltpu.SMEM)] + [in_vmem] * len(pieces),
+        out_specs=in_vmem,
+        out_shape=jax.ShapeDtypeStruct((len(pieces),) + pieces[0].shape, pieces[0].dtype),
+        name="ring_order",
+    )(jnp.stack([place]), *pieces)
+
+
+def join_kernel(at_ref, mine_ref, far_ref, other_ref, out_ref):
+    size = other_ref.shape[3]
+    shared = mine_ref.shape[2] - size
+    side, chip = at_ref[0], at_ref[1]
+    for from_side, own in enumerate((mine_ref, far_ref)):
+        row = side if from_side == 0 else 1 - side
+        if shared:
+            out_ref[:, row, :, :shared] = own[:, :, :shared]
+        for which in range(2):
+            @pl.when(chip == which)
+            def _():
+                first, second = shared + which * size, shared + (1 - which) * size
+                out_ref[:, row, :, first : first + size] = own[:, :, shared:]
+                out_ref[:, row, :, second : second + size] = other_ref[from_side]
+
+
+def joined(side, chip, mine, far, other):
+    ring, height, held = mine.shape
+    in_vmem = pl.BlockSpec(memory_space=pltpu.VMEM)
+    full = jax.ShapeDtypeStruct((ring, 2, height, held + other.shape[3]), mine.dtype)
+    whole = pl.pallas_call(
+        join_kernel,
+        in_specs=[pl.BlockSpec(memory_space=pltpu.SMEM)] + [in_vmem] * 3,
+        out_specs=in_vmem,
+        out_shape=full,
+        name="joined",
+    )(jnp.stack([side, chip]), mine, far, other)
+    return whole.reshape(ring * 2 * height, full.shape[3])
+
+
 def norm_stats(values):
     return lax.rsqrt(jnp.mean(values * values, axis=-1, keepdims=True) + eps_norm)
 
@@ -182,20 +235,27 @@
 ):
     length, width = hidden_in.shape[1:]
     dp, fsdp = lax.axis_size("dp"), lax.axis_size("fsdp")
-    core = lax.axis_index("dp") % 2
+    core, chip = lax.axis_index("dp") % 2, lax.axis_index("dp") // 2
+    chips = dp // 2
     hw = width // 2
-    ff_half = w_gate.shape[1] // 2
 
     def swap(values):
         return lax.ppermute(values, "dp", [(i, i ^ 1) for i in range(dp)])
 
-    def other_chip(values):
-        total = values
-        for step in range(1, dp // 2):
-            total = total + lax.ppermute(
-                values, "dp", [(i, (i + 2 * step) % dp) for i in range(dp)]
-            )
-        return total
+    def to_chip(values, step):
+        return lax.ppermute(values, "dp", [(i, (i + 2 * step) % dp) for i in range(dp)])
+
+    def part(values, which):
+        share = values.shape[-1] // chips
+        return lax.dynamic_slice_in_dim(values, which * share, share, values.ndim - 1)
+
+    def chip_parts(values):
+        return [part(values, chip)] + [
+            to_chip(part(values, (chip + step) % chips), step) for step in range(1, chips)
+        ]
+
+    def added(parts):
+        return sum(p.astype(f32) for p in parts).astype(bf16)
 
     def pair(values):
         return jnp.concatenate([values, swap(values)], axis=0)
@@ -225,24 +285,73 @@
     def scatter(whole):
         return lax.psum_scatter(whole, "fsdp", scatter_dimension=0, tiled=True)
 
+    ring, place = fsdp // 2, lax.axis_index("fsdp") // 2
+    side = lax.axis_index("fsdp") % 2
+
+    def sides(values):
+        return lax.ppermute(values, "fsdp", [(i, i ^ 1) for i in range(fsdp)])
+
+    def around(values, step):
+        return lax.ppermute(values, "fsdp", [(i, (i + 2 * step) % fsdp) for i in range(fsdp)])
+
+    def shared_lanes(shard):
+        lanes = shard.shape[1] // LANES
+        return (lanes - 2 * (lanes * 4 // 11)) * LANES
+
+    def held_columns(shard):
+        shared = shared_lanes(shard)
+        size = (shard.shape[1] - shared) // 2
+        held = lax.dynamic_slice_in_dim(shard, shared + chip * size, size, 1)
+        return jnp.concatenate([shard[:, :shared], held], axis=1) if shared else held
+
+    def ring_pieces(held):
+        return [held] + [around(held, step) for step in range(1, ring)]
+
+    def swapped_halves(shard, mine, far):
+        shared = shared_lanes(shard)
+        return jnp.stack([mine[:, :, shared:], far[:, :, shared:]])
+
     def mine_and_partner(partial):
         return partial[:length] + swap(partial[length:].astype(bf16)).astype(f32)
 
     gains = jnp.stack([attn_gain, mlp_gain])
     gains = jnp.pad(gains, ((0, w_query.shape[0] - 2), (0, max(0, LANES - gains.shape[1]))))
-    shard_a = jnp.concatenate(
-        [cols(w, core) for w in (w_query, w_key, w_value, w_output)] + [gains], axis=1
-    )
-    shard_b = jnp.concatenate([cols(w_gate, core), cols(w_up, core)], axis=1)
-    whole_a = gather(shard_a)
-    whole_b = gather(shard_b)
-    whole_d = gather(cols(w_down, core))
-    qkv_mat = whole_a[:, : 3 * hw]
-    output_mat = rows_from_cols(whole_a[:, 3 * hw : 4 * hw])
-    gain_rows = whole_a[:, 4 * hw :].reshape(fsdp, w_query.shape[0], -1)
+    by_ring, tie = chips == 2 and fsdp <= 8, lax.optimization_barrier
+    shard_a = jnp.concatenate([gains] + [cols(w, core) for w in (w_query, w_key, w_value)], axis=1)
+    shard_b = jnp.concatenate([cols(w_output, core), cols(w_gate, core)], axis=1)
+    shard_c, shard_d = cols(w_up, core), cols(w_down, core)
+    if by_ring:
+        join = functools.partial(joined, side, chip)
+        pieces_a = ring_pieces(held_columns(shard_a))
+        pieces_a, held_b = tie((pieces_a, held_columns(shard_b)))
+        pieces_b = ring_pieces(held_b)
+        mine_a = in_ring_order(place, pieces_a)
+        far_a = sides(mine_a)
+        pieces_b, far_a, mine_a, held_c = tie((pieces_b, far_a, mine_a, held_columns(shard_c)))
+        pieces_c = ring_pieces(held_c)
+        mine_b = in_ring_order(place, pieces_b)
+        far_b = sides(mine_b)
+        other_a = to_chip(swapped_halves(shard_a, mine_a, far_a), 1)
+        pieces_c, far_b, mine_b, other_a, held_d = tie(
+            (pieces_c, far_b, mine_b, other_a, held_columns(shard_d))
+        )
+        pieces_d = ring_pieces(held_d)
+        mine_c = in_ring_order(place, pieces_c)
+        halves_b = swapped_halves(shard_b, mine_b, far_b)
+        mine_c, halves_b, other_a = tie((mine_c, halves_b, other_a))
+        far_c, other_b = sides(mine_c), to_chip(halves_b, 1)
+        whole_a = join(mine_a, far_a, other_a)
+        pieces_d, far_c, mine_c, other_b, whole_a = tie((pieces_d, far_c, mine_c, other_b, whole_a))
+        mine_d = in_ring_order(place, pieces_d)
+        halves_c = swapped_halves(shard_c, mine_c, far_c)
+        mine_d, halves_c, whole_a = tie((mine_d, halves_c, whole_a))
+        far_d, other_c = sides(mine_d), to_chip(halves_c, 1)
+    else:
+        whole_a = gather(shard_a)
+    qkv_mat = whole_a[:, gains.shape[1] :]
+    gain_rows = whole_a[:, : gains.shape[1]].reshape(fsdp, w_query.shape[0], -1)
     gain_one = gain_rows[:, 0, : attn_gain.shape[0]].reshape(1, width).astype(f32)
     gain_two = gain_rows[:, 1, : attn_gain.shape[0]].reshape(1, width).astype(f32)
-    down_mat = rows_from_cols(whole_d)
 
     segments = pair(segment_ids)
     positions = positions_of(segments)
@@ -257,43 +366,63 @@
     normed = (hidden * inverse_one * gain_one).astype(bf16)
     qkv = dot_nn(normed, qkv_mat)
     attended, q_rot, k_rot, blended = attend(starts, cosine, sine, qkv, first_half, length)
+    if by_ring:
+        attended, far_d, other_c = tie((attended, far_d, other_c))
+        halves_d = swapped_halves(shard_d, mine_d, far_d)
+        halves_d, attended, other_c = tie((halves_d, attended, other_c))
+        other_d = to_chip(halves_d, 1)
+        whole_b = join(mine_b, far_b, other_b)
+    else:
+        whole_b = gather(shard_b)
+    output_mat, gate_mat = rows_from_cols(whole_b[:, :hw]), whole_b[:, hw:]
     first_f, blended_f = first.astype(f32), blended.astype(f32)
     square_first, square_blend = jnp.sum(first_f * first_f), jnp.sum(blended_f * blended_f)
 
     mixed = hidden[:length] + mine_and_partner(dot_nn(attended, output_mat))
     inverse_two = norm_stats(mixed)
     normed_two = pair((mixed * inverse_two * gain_two).astype(bf16))
-    gate = dot_nn(normed_two, whole_b[:, :ff_half])
-    up_val = dot_nn(normed_two, whole_b[:, ff_half:])
+    gate = dot_nn(normed_two, gate_mat)
+    up_mat = join(mine_c, far_c, other_c) if by_ring else gather(shard_c)
+    up_val = dot_nn(normed_two, up_mat)
+    if by_ring:
+        other_d, gate, up_val = tie((other_d, gate, up_val))
+        whole_d = join(mine_d, far_d, other_d)
+    else:
+        whole_d = gather(shard_d)
+    down_mat = rows_from_cols(whole_d)
     sigma = jax.nn.sigmoid(gate)
     silu_gate = gate * sigma
     act = (silu_gate * up_val).astype(bf16)
     block_out = (mixed + mine_and_partner(dot_nn(act, down_mat))).astype(bf16)[None]
 
-    grad_down = scatter(cols_from_rows(dot_tn(act, cotangent).astype(bf16)))
     grad_act = dot_nt(cotangent, down_mat)
     grad_gate = (grad_act * up_val * sigma * (1.0 + gate * (1.0 - sigma))).astype(bf16)
     grad_upv = (grad_act * silu_gate).astype(bf16)
-    grad_b = scatter(
-        jnp.concatenate(
-            [dot_tn(normed_two, grad_gate).astype(bf16), dot_tn(normed_two, grad_upv).astype(bf16)],
-            axis=1,
-        )
-    )
+    grad_b = jnp.concatenate(
+        [dot_tn(normed_two, grad_gate).astype(bf16), dot_tn(normed_two, grad_upv).astype(bf16)],
+        axis=1,
+    )
+    grad_b, act, grad_gate, grad_upv = tie((grad_b, act, grad_gate, grad_upv))
+    grad_b = scatter(grad_b)
+    grad_down = chip_parts(cols_from_rows(dot_tn(act, cotangent).astype(bf16)))
     grad_normed_two = mine_and_partner(
-        dot_nt(grad_gate, whole_b[:, :ff_half]) + dot_nt(grad_upv, whole_b[:, ff_half:])
+        dot_nt(grad_gate, gate_mat) + dot_nt(grad_upv, up_mat)
     )
     grad_mixed_norm, grad_gain_two = norm_backward(mixed, inverse_two, gain_two, grad_normed_two)
     grad_mixed = out_grad[0].astype(f32) + grad_mixed_norm
     grad_attn = pair(grad_mixed.astype(bf16))
     grad_out_w = cols_from_rows(dot_tn(attended, grad_attn).astype(bf16))
     grad_attended = dot_nt(grad_attn, output_mat).astype(bf16)
+    grad_out_w = chip_parts(grad_out_w)
     dq, dk, dv = attend_back(starts, cosine, sine, q_rot, k_rot, blended, grad_attended, length)
-    grad_a = scatter(
-        jnp.concatenate(
-            [dot_tn(normed, d).astype(bf16) for d in (dq, dk, dv)] + [grad_out_w], axis=1
-        )
-    )
+    grad_down, grad_out_w, dq = tie((grad_down, grad_out_w, dq))
+    height, down_height = w_query.shape[0], w_down.shape[0]
+    blocks = -(-down_height // height)
+    grad_down = added(grad_down).reshape(fsdp, down_height, -1)
+    grad_down = jnp.pad(grad_down, ((0, 0), (0, blocks * height - down_height), (0, 0)))
+    grad_down = [
+        grad_down[:, k * height : (k + 1) * height].reshape(fsdp * height, -1) for k in range(blocks)
+    ]
     grad_normed = mine_and_partner(
         dot_nt(dq, qkv_mat[:, :hw]) + dot_nt(dk, qkv_mat[:, hw : 2 * hw])
         + dot_nt(dv, qkv_mat[:, 2 * hw :])
@@ -305,35 +434,67 @@
     grad_first = in_order(dv[:length], swap(dv[length:]), 1)
     v1_grad_out = v1_grad_acc + grad_first.astype(f32)[None]
 
-    small = jnp.concatenate(
-        [grad_gain_one, grad_gain_two, jnp.stack([square_first, square_blend])]
-    )
-    small = lax.psum(small, ("dp", "fsdp"))
-    at = lax.axis_index("fsdp") * attn_gain.shape[0]
-    share_gain_one = lax.dynamic_slice_in_dim(small[:width], at, attn_gain.shape[0])
-    share_gain_two = lax.dynamic_slice_in_dim(small[width : 2 * width], at, attn_gain.shape[0])
-    count = f32(dp * fsdp * length * width)
-    value_norms = jnp.sqrt(small[2 * width :] / count)
-
-    grad_down = other_chip(grad_down)
-    grad_b = other_chip(grad_b)
-    grad_a = other_chip(grad_a)
-
-    def whole_columns(mine, other):
-        return in_order(mine, other, 1).astype(f32)
-
-    other_down, other_b, other_a = swap(grad_down), swap(grad_b), swap(grad_a)
-    share_query, share_key, share_value, share_output = (
-        whole_columns(grad_a[:, k * hw : (k + 1) * hw], other_a[:, k * hw : (k + 1) * hw])
-        for k in range(4)
-    )
-    share_gate, share_up = (
-        whole_columns(
-            grad_b[:, k * ff_half : (k + 1) * ff_half], other_b[:, k * ff_half : (k + 1) * ff_half]
+    rest = jnp.stack([square_first, square_blend])
+    terms = []
+    for _ in range(3):
+        terms.append(lax.reduce_precision(rest, 8, 7))
+        rest = rest - terms[-1]
+    terms = jnp.concatenate([jnp.zeros((2,), f32)] + terms)
+    row = lax.broadcasted_iota(jnp.int32, (width, 1), 0) % attn_gain.shape[0]
+    extra = jnp.concatenate(
+        [
+            grad_gain_one[:, None], grad_gain_two[:, None],
+            jnp.where(row == lax.axis_index("fsdp"), terms[None, 2:], 0.0),
+        ],
+        axis=1,
+    )
+    extra = jnp.pad(extra, ((0, 0), (0, LANES - extra.shape[1]))).astype(bf16)
+    grad_a = jnp.concatenate(
+        [dot_tn(normed, d).astype(bf16) for d in (dq, dk, dv)]
+        + [added(grad_out_w)] + grad_down + [extra],
+        axis=1,
+    )
+    grad_a = row_major(scatter(row_major(grad_a)))
+
+    def from_chips(values):
+        return [values] + [to_chip(values, step) for step in range(1, chips)]
+
+    def whole_columns(half, other, at, size):
+        return in_order(half[:, at : at + size], other[:, at : at + size], 1).astype(f32)
+
+    ff_half, share = gate_mat.shape[1], hw // chips
+    half = added(from_chips(grad_b))
+    other = swap(half)
+    share_gate, share_up = (whole_columns(half, other, k * ff_half, ff_half) for k in range(2))
+    got = [row_major(g) for g in from_chips(grad_a)]
+    split_at = 3 * hw + (1 + blocks) * share
+    by_chip = [
+        functools.reduce(
+            lambda kept, back: jnp.where(
+                (chip - back) % chips == which, got[back][:, 3 * hw : split_at], kept
+            ),
+            range(1, chips), got[0][:, 3 * hw : split_at],
         )
-        for k in range(2)
-    )
-    share_down = whole_columns(grad_down, other_down)
+        for which in range(chips)
+    ]
+    half = jnp.concatenate(
+        [added([g[:, : 3 * hw] for g in got])]
+        + [p[:, k * share : (k + 1) * share] for k in range(1 + blocks) for p in by_chip]
+        + [g[:, split_at:] for g in got],
+        axis=1,
+    )
+    other = swap(half)
+    share_query, share_key, share_value, share_output, *down_blocks = (
+        whole_columns(half, other, k * hw, hw) for k in range(4 + blocks)
+    )
+    share_down = jnp.concatenate(down_blocks, axis=0)[:down_height]
+    gain_sums = sum(
+        which[:, at : at + LANES].astype(f32)
+        for which in (half, other) for at in range((4 + blocks) * hw, half.shape[1], LANES)
+    )
+    share_gain_one, share_gain_two = gain_sums[:, 0], gain_sums[:, 1]
+    squares = jnp.sum(gain_sums[:, 2:8], axis=0).reshape(3, 2).sum(axis=0)
+    value_norms = jnp.sqrt(squares / f32(dp * fsdp * length * width))
     return (
         block_out, input_grad, share_gain_one, share_query, share_key, share_value, share_output,
         share_gain_two, share_gate, share_up, share_down, v1_grad_out, value_norms,

time: 600 us -> 533 us (0.89)
  waiting for transfers between devices: 295 us -> 202 us
  blocking collectives: 39.4 us -> 0 us
  starting transfers between devices: 9.84 us -> 45.8 us
  Pallas kernels: 56.4 us -> 82.6 us
  local copies, waits for them, and re-layouts: 26.9 us -> 35.4 us
    all_gather x3 -> x0, waiting for transfers between devices: 161 us -> none  [gather(): return lax.all_gather(shard, 'fsdp', axis=0, tiled=True)]
    ppermute x3 -> x24, waiting for transfers between devices: 11.7 us -> 92.1 us  [the longest x12 66.2 us: around(): lax.ppermute(values, 'fsdp', [(i, (i + 2 * step) % fsdp) for i in range(f...]
    psum x1 -> x0, blocking collectives: 39.4 us -> none  [shards(): small = lax.psum(small, ('dp', 'fsdp'))]
    ppermute x3 -> x24, starting transfers between devices: 5.22 us -> 42.6 us  [the longest x12 29 us: around(): lax.ppermute(values, 'fsdp', [(i, (i + 2 * step) % fsdp) for i in range(f...]
    pallas_call x0 -> x8, Pallas kernels: none -> 26.2 us  [the longest x4 16.4 us: joined(): pl.pallas_call(join_kernel, in_specs=[pl.BlockSpec(memory_space=pltpu.SME...]
    concatenate x3 -> x8, other arithmetic: 16.8 us -> 1.08 us  [the longest x4 0.8 us: held_columns(): jnp.concatenate([shard[:, :shared], held], axis=1)]
    reduce_scatter x3 -> x2, waiting for transfers between devices: 117 us -> 107 us  [scatter(): return lax.psum_scatter(whole, 'fsdp', scatter_dimension=0, tiled=True)]
    convert_element_type x7 -> x9, other arithmetic: 7.04 us -> 13.1 us  [the longest x6 5.77 us: whole_columns(): in_order(half[:, at:at + size], other[:, at:at + size], 1).astype(f32)]
  transfers between devices with their start and end apart: 27 -> 43, of which waited for: 9 -> 18; matrix products, arithmetic and copies ran while one was open for 23% -> 23% of each run, Pallas kernels for 10% -> 14%
where the time goes in v2:
time: 533 us; the launch traced here: 526 us
  waiting for transfers between devices  202 us (38%)
  Pallas kernels  82.6 us (15%)
  matrix products  78 us (15%)
  other arithmetic  66.5 us (12%)
  starting transfers between devices  45.8 us (9%)
  local copies, waits for them, and re-layouts  35.4 us (7%)
  between operations  15.4 us (3%)
    reduce_scatter x2, waiting for transfers between devices, scatter(): return lax.psum_scatter(whole, 'fsdp', scatter_dimension=0, tiled=True)  107 us
    ppermute x12, waiting for transfers between devices, around(): lax.ppermute(values, 'fsdp', [(i, (i + 2 * step) % fsdp) for i in range(f...  66.2 us
    pallas_call x1, Pallas kernels, attend_back(): pl.pallas_call(attend_back_kernel, grid=(tokens // length, width // LANES...  35.3 us
    ppermute x12, starting transfers between devices, around(): lax.ppermute(values, 'fsdp', [(i, (i + 2 * step) % fsdp) for i in range(f...  29 us
    dot_general x5, matrix products, dot_nn(): return jnp.dot(a, b, preferred_element_type=f32)  28.1 us
    dot_general x7, matrix products, dot_tn(): lax.dot_general(a, b, (((0,), (0,)), ((), ())), preferred_element_type=f32)  27.6 us
    ppermute x8, waiting for transfers between devices, to_chip(): lax.ppermute(values, 'dp', [(i, (i + 2 * step) % dp) for i in range(dp)])  25.8 us
    dot_general x7, matrix products, dot_nt(): lax.dot_general(a, b, (((1,), (1,)), ((), ())), preferred_element_type=f32)  22.4 us
  transfers between devices with their start and end apart: 43, of which 18 were waited for; matrix products, arithmetic and copies ran while one was open for 23% of the time, Pallas kernels for 14%

profile of v2, /device:TPU:0, one launch (start us, length us, event | category | flops | bytes accessed | tf_op | source)
XLA Modules:
  0.0 525.7 jit_solution(13595807054046106108)
XLA Ops:
  10.1 3.1 collective-permute-start.1
  13.2 2.6 collective-permute-start.2
  18.3 5.0 collective-permute-done.1.refs_1_
  23.2 11.8 %collective-permute-done.2.refs_2_ = bf16[128,1152]{1,0:T(8,128)(2,1)S(1)} collective-permute-done((bf16[128,1152]{1,0:T(8,128)(2,1)S(1)}, bf16[128,1152]{1,0:T(8,128)(2,1)S(1)}, u32[]{:S(2)}, u32[]{:S(2)}) %collective-permute-start.2) | collective-permute-done | bytes 294944 | tf_op jit(solution)/shard_map/ppermute | solution.py:295
  40.6 6.7 %collective-permute-start.4 = (bf16[128,1280]{1,0:T(8,128)(2,1)S(1)}, bf16[128,1280]{1,0:T(8,128)(2,1)S(1)}, u32[]{:S(2)}, u32[]{:S(2)}) collective-permute-start(bf16[128,1280]{1,0:T(8,128)(2,1)S(1)} %pad_maximum_fusion.22.refs_0_), channel_id=1, source_target_pairs={{0,2},{1,3},{2,4},{3,5},{4,6},{5,7},{6,0},{7,1},{8,10},{9,11},{10,... | collective-permute-start | bytes 983048 | tf_op jit(solution)/shard_map/ppermute | solution.py:295
  51.5 5.6 %collective-permute-done.4.refs_1_ = bf16[128,1280]{1,0:T(8,128)(2,1)S(1)} collective-permute-done((bf16[128,1280]{1,0:T(8,128)(2,1)S(1)}, bf16[128,1280]{1,0:T(8,128)(2,1)S(1)}, u32[]{:S(2)}, u32[]{:S(2)}) %collective-permute-start.4) | collective-permute-done | bytes 327712 | tf_op jit(solution)/shard_map/ppermute | solution.py:295
  57.2 13.8 %collective-permute-done.5.refs_2_ = bf16[128,1280]{1,0:T(8,128)(2,1)S(1)} collective-permute-done((bf16[128,1280]{1,0:T(8,128)(2,1)S(1)}, bf16[128,1280]{1,0:T(8,128)(2,1)S(1)}, u32[]{:S(2)}, u32[]{:S(2)}) %collective-permute-start.5) | collective-permute-done | bytes 327712 | tf_op jit(solution)/shard_map/ppermute | solution.py:295
  71.9 2.8 ring_order.5.mine_ref
  82.6 8.2 %collective-permute-start.10 = (bf16[128,896]{1,0:T(8,128)(2,1)S(1)}, bf16[128,896]{1,0:T(8,128)(2,1)S(1)}, u32[]{:S(2)}, u32[]{:S(2)}) collective-permute-start(bf16[128,896]{1,0:T(8,128)(2,1)S(1)} %copy-done.38), channel_id=1, source_target_pairs={{0,6},{1,7},{2,0},{3,1},{4,2},{5,3},{6,4},{7,5},{8,14},{9,15},{10,... | collective-permute-start | bytes 688136 | tf_op jit(solution)/shard_map/ppermute | solution.py:295
  91.6 5.2 collective-permute-done.10.refs_3_
  96.8 5.5 %collective-permute-done.8.refs_1_ = bf16[128,896]{1,0:T(8,128)(2,1)S(1)} collective-permute-done((bf16[128,896]{1,0:T(8,128)(2,1)S(1)}, bf16[128,896]{1,0:T(8,128)(2,1)S(1)}, u32[]{:S(2)}, u32[]{:S(2)}) %collective-permute-start.8) | collective-permute-done | bytes 229408 | tf_op jit(solution)/shard_map/ppermute | solution.py:295
  102.2 9.0 %collective-permute-done.9.refs_2_ = bf16[128,896]{1,0:T(8,128)(2,1)S(1)} collective-permute-done((bf16[128,896]{1,0:T(8,128)(2,1)S(1)}, bf16[128,896]{1,0:T(8,128)(2,1)S(1)}, u32[]{:S(2)}, u32[]{:S(2)}) %collective-permute-start.9) | collective-permute-done | bytes 229408 | tf_op jit(solution)/shard_map/ppermute | solution.py:295
  120.8 3.0 fusion.30
  131.6 4.0 joined.4
  137.2 8.9 %collective-permute-done.14.refs_2_ = bf16[352,384]{1,0:T(8,128)(2,1)S(1)} collective-permute-done((bf16[352,384]{1,0:T(8,128)(2,1)S(1)}, bf16[352,384]{1,0:T(8,128)(2,1)S(1)}, u32[]{:S(2)}, u32[]{:S(2)}) %collective-permute-start.14) | collective-permute-done | bytes 270368 | tf_op jit(solution)/shard_map/ppermute | solution.py:295
  154.4 4.8 joined.5
  161.6 8.3 %fusion.1.q_ref.k_ref.v_ref = f32[1024,1536]{1,0:T(8,128)} fusion(bf16[1024,1664]{1,0:T(8,128)(2,1)} %bitcast.78, f32[1024]{0:T(1024)S(1)} %bitcast.105, f32[1024]{0:T(1024)S(1)} %add_rsqrt_fusion, bf16[512,1024]{1,0:T(8,128)(2,1)} %collective-permute-done, bf16[512,1024]{1,0:T(8,128)(2,1)S(1)} %bitcast.91), kind=kOutput, calls=%fused_computation.16 | convolution fusion | flops 3228565504 | bytes 11542528 | tf_op jit(solution)/shard_map/dot_general | solution.py:66
  169.9 21.2 %attend.1 = (bf16[1024,512]{1,0:T(8,128)(2,1)}, bf16[1024,512]{1,0:T(8,128)(2,1)}, bf16[1024,512]{1,0:T(8,128)(2,1)}, bf16[1024,512]{1,0:T(8,128)(2,1)}) custom-call(s32[1024,1]{1,0:T(8,128)} %copy.37.start_ref, f32[1024,128]{1,0:T(8,128)} %get-tuple-element.213.cos_ref, f32[1024,128]{1,0:T(8,128)} %get-tuple-element.212.sin_ref, ...), custom_call_target="tpu_custom_call" | custom-call | tf_op jit(solution)/shard_map/attend/pallas_call | solution.py:145
  202.2 3.6 joined.6
  206.8 8.4 %fusion.5 = f32[1024,1408]{1,0:T(8,128)} fusion(bf16[1024,1920]{1,0:T(8,128)(2,1)} %bitcast.83, bf16[512,1024]{1,0:T(8,128)(2,1)} %collective-permute-done.25, bf16[512,1024]{1,0:T(8,128)(2,1)} %multiply_convert_fusion.4), kind=kOutput, calls=%fused_computation.22 | convolution fusion | flops 2956984320 | bytes 10747904 | tf_op jit(solution)/shard_map/dot_general | solution.py:66
  215.2 6.7 %fusion.56 = f32[1024,1408]{1,0:T(8,128)} fusion(bf16[1024,1408]{1,0:T(8,128)(2,1)S(1)} %bitcast.97, bf16[512,1024]{1,0:T(8,128)(2,1)} %collective-permute-done.25, bf16[512,1024]{1,0:T(8,128)(2,1)} %multiply_convert_fusion.4), kind=kOutput, calls=%fused_computation.242 | convolution fusion | flops 2956984320 | bytes 10747904 | tf_op jit(solution)/shard_map/dot_general | solution.py:66
  221.8 2.8 collective-permute-done.24.other_ref
  224.7 4.0 joined.7
  228.6 2.6 constant_dynamic-slice_fusion.2
  231.7 2.4 multiply_reduce_fusion.2
  236.4 2.5 broadcast_select_fusion.3
  240.5 5.3 %fusion.13 = f32[1024,1408]{1,0:T(8,128)S(1)} fusion(bf16[1408,512]{1,0:T(8,128)(2,1)S(1)} %get-tuple-element.151, bf16[1408,512]{1,0:T(8,128)(2,1)S(1)} %get-tuple-element.150, bf16[512,1024]{1,0:T(8,128)(2,1)} %collective-permute-done.28, bf16[512,1024]{1,0:T(8,128)(2,1)} %bitcast.28), kind=kOutput, calls=%fused_computation.52 | convolution fusion | flops 2962751488 | bytes 10747904 | tf_op jit(solution)/shard_map/dot_general | solution.py:58
  245.8 4.3 multiply_convert_fusion.1
  250.2 6.9 %convolution_convert_fusion.2 = bf16[1024,1408]{1,0:T(8,128)(2,1)S(1)} fusion(bf16[1024,1408]{1,0:T(8,128)(2,1)S(1)} %get-tuple-element.116, bf16[512,1024]{1,0:T(8,128)(2,1)} %collective-permute-done.25, bf16[512,1024]{1,0:T(8,128)(2,1)} %multiply_convert_fusion.4), kind=kOutput, calls=%fused_computation.11 | convolution fusion | flops 2958426112 | bytes 7864320 | tf_op jit(solution)/shard_map/dot_general | solution.py:62
  257.1 5.4 %convolution_convert_fusion.1 = bf16[1024,1408]{1,0:T(8,128)(2,1)S(1)} fusion(bf16[1024,1408]{1,0:T(8,128)(2,1)S(1)} %get-tuple-element.117, bf16[512,1024]{1,0:T(8,128)(2,1)} %collective-permute-done.25, bf16[512,1024]{1,0:T(8,128)(2,1)} %multiply_convert_fusion.4), kind=kOutput, calls=%fused_computation.10 | convolution fusion | flops 2958426112 | bytes 7864320 | tf_op jit(solution)/shard_map/dot_general | solution.py:62
  262.4 2.9 pad_maximum_fusion
  265.9 6.3 %fusion.62 = f32[1024,1024]{1,0:T(8,128)S(1)} fusion(bf16[1024,1408]{1,0:T(8,128)(2,1)} %copy-done.21, bf16[1024,1408]{1,0:T(8,128)(2,1)} %bitcast.96), kind=kOutput, calls=%fused_computation.247 | convolution fusion | flops 2952790016 | bytes 9961472 | tf_op jit(solution)/shard_map/dot_general | solution.py:58
  272.2 3.5 fusion.10
  275.9 3.4 fusion.14
  280.0 4.8 convolution_convert_fusion
  285.9 3.9 fusion.58
  300.1 35.3 %attend_back.1 = (bf16[1024,512]{1,0:T(8,128)(2,1)}, bf16[1024,512]{1,0:T(8,128)(2,1)}, bf16[1024,512]{1,0:T(8,128)(2,1)}) custom-call(s32[1024,1]{1,0:T(8,128)} %copy.37.start_ref, f32[1024,128]{1,0:T(8,128)} %get-tuple-element.213.cos_ref, f32[1024,128]{1,0:T(8,128)} %get-tuple-element.212.sin_ref, bf16[1024,512]{1,0:T(8,128)(2,1)} %get-tuple-element.119.q_rot_ref, ...), custom_call_target="tpu_custom_call" | custom-call | tf_op jit(solution)/shard_map/attend_back/pallas_call | solution.py:159
  338.1 2.6 fusion.23
  342.0 8.8 %collective-permute-done.34 = bf16[1024,256]{1,0:T(8,128)(2,1)S(1)} collective-permute-done((bf16[1024,256]{1,0:T(8,128)(2,1)S(1)}, bf16[1024,256]{1,0:T(8,128)(2,1)S(1)}, u32[]{:S(2)}, u32[]{:S(2)}) %collective-permute-start.34) | collective-permute-done | bytes 524320 | tf_op jit(solution)/shard_map/ppermute | solution.py:246
  352.4 3.9 fusion.17
  356.3 2.6 fusion.16
  360.7 2.6 fusion.15
  363.8 3.9 copy-done.3
  373.3 5.8 %reduce-scatter.5.cloned.1.call-done = bf16[128,2816]{1,0:T(8,128)(2,1)} async-done(((bf16[1024,2816]{1,0:T(8,128)(2,1)}), bf16[128,2816]{1,0:T(8,128)(2,1)}) %reduce-scatter.5.cloned.1.call-update) | async-done | bytes 720912 | tf_op jit(solution)/shard_map/reduce_scatter | solution.py:286
  380.6 3.4 convert_add_fusion
  384.0 3.6 add_bitcast_fusion
  387.7 101.4 %reduce-scatter.3.cloned.1.call-done = bf16[128,2688]{1,0:T(8,128)(2,1)} async-done(((bf16[1024,2688]{1,0:T(8,128)(2,1)}), bf16[128,2688]{1,0:T(8,128)(2,1)}) %reduce-scatter.3.cloned.1.call-update) | async-done | bytes 688144 | tf_op jit(solution)/shard_map/reduce_scatter | solution.py:286
  491.8 13.9 %collective-permute-done.36 = bf16[128,2688]{1,0:T(8,128)(2,1)S(1)} collective-permute-done((bf16[128,2688]{1,0:T(8,128)(2,1)}, bf16[128,2688]{1,0:T(8,128)(2,1)S(1)}, u32[]{:S(2)}, u32[]{:S(2)}) %collective-permute-start.36) | collective-permute-done | bytes 688160 | tf_op jit(solution)/shard_map/ppermute | solution.py:246
  (315 shorter events, 113.5 us)
Async XLA Ops:
  7.2 371.9 %reduce-scatter.5.cloned.1.call-start = ((), (), s32[]{:S(2)}) async-start(), calls=%async_computation.3 | async-start | bytes 6488064 | tf_op jit(solution)/shard_map/reduce_scatter | solution.py:286
  10.1 13.1 %collective-permute-start.1 = (bf16[128,1152]{1,0:T(8,128)(2,1)S(1)}, bf16[128,1152]{1,0:T(8,128)(2,1)S(1)}, u32[]{:S(2)}, u32[]{:S(2)}) collective-permute-start(bf16[128,1152]{1,0:T(8,128)(2,1)S(1)} %pad_maximum_fusion.23.refs_0_), channel_id=1, source_target_pairs={{0,2},{1,3},{2,4},{3,5},{4,6},{5,7},{6,0},{7,1},{8,10},{9,11},{10,... | collective-permute-start | bytes 884744 | tf_op jit(solution)/shard_map/ppermute | solution.py:295
  13.2 21.8 %collective-permute-start.2 = (bf16[128,1152]{1,0:T(8,128)(2,1)S(1)}, bf16[128,1152]{1,0:T(8,128)(2,1)S(1)}, u32[]{:S(2)}, u32[]{:S(2)}) collective-permute-start(bf16[128,1152]{1,0:T(8,128)(2,1)S(1)} %pad_maximum_fusion.23.refs_0_), channel_id=1, source_target_pairs={{0,4},{1,5},{2,6},{3,7},{4,0},{5,1},{6,2},{7,3},{8,12},{9,13},{10,... | collective-permute-start | bytes 884744 | tf_op jit(solution)/shard_map/ppermute | solution.py:295
  15.8 19.2 %collective-permute-start.3 = (bf16[128,1152]{1,0:T(8,128)(2,1)S(1)}, bf16[128,1152]{1,0:T(8,128)(2,1)S(1)}, u32[]{:S(2)}, u32[]{:S(2)}) collective-permute-start(bf16[128,1152]{1,0:T(8,128)(2,1)S(1)} %pad_maximum_fusion.23.refs_0_), channel_id=1, source_target_pairs={{0,6},{1,7},{2,0},{3,1},{4,2},{5,3},{6,4},{7,5},{8,14},{9,15},{10,... | collective-permute-start | bytes 884744 | tf_op jit(solution)/shard_map/ppermute | solution.py:295
  18.3 53.6 %copy-start.31 = (bf16[128,1280]{1,0:T(8,128)(2,1)}, bf16[128,1280]{1,0:T(8,128)(2,1)S(1)}, u32[]{:S(2)}) copy-start(bf16[128,1280]{1,0:T(8,128)(2,1)S(1)} %pad_maximum_fusion.22.refs_0_) | copy-start | bytes 983044
  38.2 32.9 %collective-permute-start.7 = (bf16[4,128,1152]{2,1,0:T(8,128)(2,1)}, bf16[4,128,1152]{2,1,0:T(8,128)(2,1)S(1)}, u32[]{:S(2)}, u32[]{:S(2)}) collective-permute-start(bf16[4,128,1152]{2,1,0:T(8,128)(2,1)} %ring_order.4.mine_ref), channel_id=1, source_target_pairs={{0,1},{1,0},{2,3},{3,2},{4,5},{5,4},{6,7},{7,6},{8,9},{9,8},{10,11... | collective-permute-start | bytes 3538952 | tf_op jit(solution)/shard_map/ppermute | solution.py:292
  39.7 51.1 %collective-permute-start.18 = (s32[1,512]{1,0:T(1,128)S(1)}, s32[1,512]{1,0:T(1,128)S(1)}, u32[]{:S(2)}, u32[]{:S(2)}) collective-permute-start(s32[1,512]{1,0:T(1,128)S(1)} %copy-done.52), channel_id=1, source_target_pairs={{0,8},{8,0},{16,24},{24,16},{1,9},{9,1},{17,25},{25,17},{2,10},{10... | collective-permute-start | bytes 6152 | tf_op jit(solution)/shard_map/ppermute | solution.py:243
  40.6 16.6 %collective-permute-start.4 = (bf16[128,1280]{1,0:T(8,128)(2,1)S(1)}, bf16[128,1280]{1,0:T(8,128)(2,1)S(1)}, u32[]{:S(2)}, u32[]{:S(2)}) collective-permute-start(bf16[128,1280]{1,0:T(8,128)(2,1)S(1)} %pad_maximum_fusion.22.refs_0_), channel_id=1, source_target_pairs={{0,2},{1,3},{2,4},{3,5},{4,6},{5,7},{6,0},{7,1},{8,10},{9,11},{10,... | collective-permute-start | bytes 983048 | tf_op jit(solution)/shard_map/ppermute | solution.py:295
  47.4 23.6 %collective-permute-start.5 = (bf16[128,1280]{1,0:T(8,128)(2,1)S(1)}, bf16[128,1280]{1,0:T(8,128)(2,1)S(1)}, u32[]{:S(2)}, u32[]{:S(2)}) collective-permute-start(bf16[128,1280]{1,0:T(8,128)(2,1)S(1)} %pad_maximum_fusion.22.refs_0_), channel_id=1, source_target_pairs={{0,4},{1,5},{2,6},{3,7},{4,0},{5,1},{6,2},{7,3},{8,12},{9,13},{10,... | collective-permute-start | bytes 983048 | tf_op jit(solution)/shard_map/ppermute | solution.py:295
  49.0 22.0 %collective-permute-start.6 = (bf16[128,1280]{1,0:T(8,128)(2,1)S(1)}, bf16[128,1280]{1,0:T(8,128)(2,1)S(1)}, u32[]{:S(2)}, u32[]{:S(2)}) collective-permute-start(bf16[128,1280]{1,0:T(8,128)(2,1)S(1)} %pad_maximum_fusion.22.refs_0_), channel_id=1, source_target_pairs={{0,6},{1,7},{2,0},{3,1},{4,2},{5,3},{6,4},{7,5},{8,14},{9,15},{10,... | collective-permute-start | bytes 983048 | tf_op jit(solution)/shard_map/ppermute | solution.py:295
  74.7 37.2 %collective-permute-start.11 = (bf16[4,128,1280]{2,1,0:T(8,128)(2,1)}, bf16[4,128,1280]{2,1,0:T(8,128)(2,1)}, u32[]{:S(2)}, u32[]{:S(2)}) collective-permute-start(bf16[4,128,1280]{2,1,0:T(8,128)(2,1)} %ring_order.5.mine_ref), channel_id=1, source_target_pairs={{0,1},{1,0},{2,3},{3,2},{4,5},{5,4},{6,7},{7,6},{8,9},{9,8},{10,11... | collective-permute-start | bytes 3932168 | tf_op jit(solution)/shard_map/ppermute | solution.py:292
  76.3 36.7 %copy-start.7 = (bf16[4,128,1280]{2,1,0:T(8,128)(2,1)S(1)}, bf16[4,128,1280]{2,1,0:T(8,128)(2,1)}, u32[]{:S(2)}) copy-start(bf16[4,128,1280]{2,1,0:T(8,128)(2,1)} %ring_order.5.mine_ref) | copy-start | bytes 3932164
  77.4 33.8 %collective-permute-start.12 = (bf16[2,4,128,512]{3,2,1,0:T(8,128)(2,1)}, bf16[2,4,128,512]{3,2,1,0:T(8,128)(2,1)}, u32[]{:S(2)}, u32[]{:S(2)}) collective-permute-start(bf16[2,4,128,512]{3,2,1,0:T(8,128)(2,1)} %pad_maximum_fusion.12), channel_id=1, source_target_pairs={{0,16},{8,24},{16,0},{24,8},{1,17},{9,25},{17,1},{25,9},{2,18},{10... | collective-permute-start | bytes 3145736 | tf_op jit(solution)/shard_map/ppermute | solution.py:246
  80.9 48.3 %copy-start.33 = (bf16[352,384]{1,0:T(8,128)(2,1)}, bf16[352,384]{1,0:T(8,128)(2,1)S(1)}, u32[]{:S(2)}) copy-start(bf16[352,384]{1,0:T(8,128)(2,1)S(1)} %pad_maximum_fusion.24.refs_0_) | copy-start | bytes 811012
  82.6 14.2 %collective-permute-start.10 = (bf16[128,896]{1,0:T(8,128)(2,1)S(1)}, bf16[128,896]{1,0:T(8,128)(2,1)S(1)}, u32[]{:S(2)}, u32[]{:S(2)}) collective-permute-start(bf16[128,896]{1,0:T(8,128)(2,1)S(1)} %copy-done.38), channel_id=1, source_target_pairs={{0,6},{1,7},{2,0},{3,1},{4,2},{5,3},{6,4},{7,5},{8,14},{9,15},{10,... | collective-permute-start | bytes 688136 | tf_op jit(solution)/shard_map/ppermute | solution.py:295
  90.8 11.5 %collective-permute-start.8 = (bf16[128,896]{1,0:T(8,128)(2,1)S(1)}, bf16[128,896]{1,0:T(8,128)(2,1)S(1)}, u32[]{:S(2)}, u32[]{:S(2)}) collective-permute-start(bf16[128,896]{1,0:T(8,128)(2,1)S(1)} %copy-done.38), channel_id=1, source_target_pairs={{0,2},{1,3},{2,4},{3,5},{4,6},{5,7},{6,0},{7,1},{8,10},{9,11},{10,... | collective-permute-start | bytes 688136 | tf_op jit(solution)/shard_map/ppermute | solution.py:295
  90.8 20.4 %collective-permute-start.9 = (bf16[128,896]{1,0:T(8,128)(2,1)S(1)}, bf16[128,896]{1,0:T(8,128)(2,1)S(1)}, u32[]{:S(2)}, u32[]{:S(2)}) collective-permute-start(bf16[128,896]{1,0:T(8,128)(2,1)S(1)} %copy-done.38), channel_id=1, source_target_pairs={{0,4},{1,5},{2,6},{3,7},{4,0},{5,1},{6,2},{7,3},{8,12},{9,13},{10,... | collective-permute-start | bytes 688136 | tf_op jit(solution)/shard_map/ppermute | solution.py:295
  96.8 32.4 %collective-permute-start = (bf16[512,1024]{1,0:T(8,128)(2,1)}, bf16[512,1024]{1,0:T(8,128)(2,1)}, u32[]{:S(2)}, u32[]{:S(2)}) collective-permute-start(bf16[512,1024]{1,0:T(8,128)(2,1)} %bitcast.89), channel_id=1, source_target_pairs={{0,8},{8,0},{16,24},{24,16},{1,9},{9,1},{17,25},{25,17},{2,10},{10... | collective-permute-start | bytes 3145736 | tf_op jit(solution)/shard_map/ppermute | solution.py:243
  102.2 21.7 %collective-permute-start.19 = (bf16[512,512]{1,0:T(8,128)(2,1)}, bf16[512,512]{1,0:T(8,128)(2,1)}, u32[]{:S(2)}, u32[]{:S(2)}) collective-permute-start(bf16[512,512]{1,0:T(8,128)(2,1)} %get-tuple-element.187), channel_id=1, source_target_pairs={{0,8},{8,0},{16,24},{24,16},{1,9},{9,1},{17,25},{25,17},{2,10},{10... | collective-permute-start | bytes 1572872 | tf_op jit(solution)/shard_map/ppermute | solution.py:243
  116.7 29.6 %collective-permute-start.17 = (bf16[2,4,128,640]{3,2,1,0:T(8,128)(2,1)}, bf16[2,4,128,640]{3,2,1,0:T(8,128)(2,1)}, u32[]{:S(2)}, u32[]{:S(2)}) collective-permute-start(bf16[2,4,128,640]{3,2,1,0:T(8,128)(2,1)} %pad_maximum_fusion.11), channel_id=1, source_target_pairs={{0,16},{8,24},{16,0},{24,8},{1,17},{9,25},{17,1},{25,9},{2,18},{10... | collective-permute-start | bytes 3932168 | tf_op jit(solution)/shard_map/ppermute | solution.py:246
  119.3 26.8 %collective-permute-start.16 = (bf16[4,128,896]{2,1,0:T(8,128)(2,1)}, bf16[4,128,896]{2,1,0:T(8,128)(2,1)}, u32[]{:S(2)}, u32[]{:S(2)}) collective-permute-start(bf16[4,128,896]{2,1,0:T(8,128)(2,1)} %ring_order.6.mine_ref), channel_id=1, source_target_pairs={{0,1},{1,0},{2,3},{3,2},{4,5},{5,4},{6,7},{7,6},{8,9},{9,8},{10,11... | collective-permute-start | bytes 2752520 | tf_op jit(solution)/shard_map/ppermute | solution.py:292
  126.0 11.2 %collective-permute-start.13 = (bf16[352,384]{1,0:T(8,128)(2,1)S(1)}, bf16[352,384]{1,0:T(8,128)(2,1)S(1)}, u32[]{:S(2)}, u32[]{:S(2)}) collective-permute-start(bf16[352,384]{1,0:T(8,128)(2,1)S(1)} %pad_maximum_fusion.24.refs_0_), channel_id=1, source_target_pairs={{0,2},{1,3},{2,4},{3,5},{4,6},{5,7},{6,0},{7,1},{8,10},{9,11},{10,... | collective-permute-start | bytes 811016 | tf_op jit(solution)/shard_map/ppermute | solution.py:295
  127.2 18.8 %collective-permute-start.14 = (bf16[352,384]{1,0:T(8,128)(2,1)S(1)}, bf16[352,384]{1,0:T(8,128)(2,1)S(1)}, u32[]{:S(2)}, u32[]{:S(2)}) collective-permute-start(bf16[352,384]{1,0:T(8,128)(2,1)S(1)} %pad_maximum_fusion.24.refs_0_), channel_id=1, source_target_pairs={{0,4},{1,5},{2,6},{3,7},{4,0},{5,1},{6,2},{7,3},{8,12},{9,13},{10,... | collective-permute-start | bytes 811016 | tf_op jit(solution)/shard_map/ppermute | solution.py:295
  129.2 16.9 %collective-permute-start.15 = (bf16[352,384]{1,0:T(8,128)(2,1)S(1)}, bf16[352,384]{1,0:T(8,128)(2,1)S(1)}, u32[]{:S(2)}, u32[]{:S(2)}) collective-permute-start(bf16[352,384]{1,0:T(8,128)(2,1)S(1)} %pad_maximum_fusion.24.refs_0_), channel_id=1, source_target_pairs={{0,6},{1,7},{2,0},{3,1},{4,2},{5,3},{6,4},{7,5},{8,14},{9,15},{10,... | collective-permute-start | bytes 811016 | tf_op jit(solution)/shard_map/ppermute | solution.py:295
  152.3 41.1 %collective-permute-start.20 = (bf16[4,352,384]{2,1,0:T(8,128)(2,1)}, bf16[4,352,384]{2,1,0:T(8,128)(2,1)}, u32[]{:S(2)}, u32[]{:S(2)}) collective-permute-start(bf16[4,352,384]{2,1,0:T(8,128)(2,1)} %ring_order.7.mine_ref), channel_id=1, source_target_pairs={{0,1},{1,0},{2,3},{3,2},{4,5},{5,4},{6,7},{7,6},{8,9},{9,8},{10,11... | collective-permute-start | bytes 3244040 | tf_op jit(solution)/shard_map/ppermute | solution.py:292
  153.4 40.0 %collective-permute-start.21 = (bf16[2,4,128,512]{3,2,1,0:T(8,128)(2,1)}, bf16[2,4,128,512]{3,2,1,0:T(8,128)(2,1)}, u32[]{:S(2)}, u32[]{:S(2)}) collective-permute-start(bf16[2,4,128,512]{3,2,1,0:T(8,128)(2,1)} %pad_maximum_fusion.13), channel_id=1, source_target_pairs={{0,16},{8,24},{16,0},{24,8},{1,17},{9,25},{17,1},{25,9},{2,18},{10... | collective-permute-start | bytes 3145736 | tf_op jit(solution)/shard_map/ppermute | solution.py:246
  161.5 30.7 %collective-permute-start.22 = (bf16[512,512]{1,0:T(8,128)(2,1)S(1)}, bf16[512,512]{1,0:T(8,128)(2,1)S(1)}, u32[]{:S(2)}, u32[]{:S(2)}) collective-permute-start(bf16[512,512]{1,0:T(8,128)(2,1)S(1)} %constant_dynamic-slice_fusion.3), channel_id=1, source_target_pairs={{0,8},{8,0},{16,24},{24,16},{1,9},{9,1},{17,25},{25,17},{2,10},{10... | collective-permute-start | bytes 1572872 | tf_op jit(solution)/shard_map/ppermute | solution.py:243
  196.8 2.8 collective-permute-start.23
  202.1 4.6 collective-permute-start.25
  205.8 18.9 %collective-permute-start.24 = (bf16[2,4,352,128]{3,2,1,0:T(8,128)(2,1)}, bf16[2,4,352,128]{3,2,1,0:T(8,128)(2,1)}, u32[]{:S(2)}, u32[]{:S(2)}) collective-permute-start(bf16[2,4,352,128]{3,2,1,0:T(8,128)(2,1)} %pad_maximum_fusion.19), channel_id=1, source_target_pairs={{0,16},{8,24},{16,0},{24,8},{1,17},{9,25},{17,1},{25,9},{2,18},{10... | collective-permute-start | bytes 2162696 | tf_op jit(solution)/shard_map/ppermute | solution.py:246
  231.2 5.3 %collective-permute-start.26 = (bf16[1408,512]{1,0:T(8,128)(2,1)}, bf16[1408,512]{1,0:T(8,128)(2,1)}, u32[]{:S(2)}, u32[]{:S(2)}) collective-permute-start(bf16[1408,512]{1,0:T(8,128)(2,1)} %constant_dynamic-slice_fusion.2), channel_id=1, source_target_pairs={{0,8},{8,0},{16,24},{24,16},{1,9},{9,1},{17,25},{25,17},{2,10},{10... | collective-permute-start | bytes 4325384 | tf_op jit(solution)/shard_map/ppermute | solution.py:243
  231.2 7.8 %collective-permute-start.28 = (bf16[512,1024]{1,0:T(8,128)(2,1)}, bf16[512,1024]{1,0:T(8,128)(2,1)}, u32[]{:S(2)}, u32[]{:S(2)}) collective-permute-start(bf16[512,1024]{1,0:T(8,128)(2,1)} %bitcast.28), channel_id=1, source_target_pairs={{0,8},{8,0},{16,24},{24,16},{1,9},{9,1},{17,25},{25,17},{2,10},{10... | collective-permute-start | bytes 3145736 | tf_op jit(solution)/shard_map/ppermute | solution.py:243
  265.4 223.6 %reduce-scatter.3.cloned.1.call-start = ((), (), s32[]{:S(2)}) async-start(), calls=%async_computation.2 | async-start | bytes 6193152 | tf_op jit(solution)/shard_map/reduce_scatter | solution.py:286
  275.8 9.3 %collective-permute-start.29 = (bf16[512,1024]{1,0:T(8,128)(2,1)S(1)}, bf16[512,1024]{1,0:T(8,128)(2,1)S(1)}, u32[]{:S(2)}, u32[]{:S(2)}) collective-permute-start(bf16[512,1024]{1,0:T(8,128)(2,1)S(1)} %slice.493), channel_id=1, source_target_pairs={{0,8},{8,0},{16,24},{24,16},{1,9},{9,1},{17,25},{25,17},{2,10},{10... | collective-permute-start | bytes 3145736 | tf_op jit(solution)/shard_map/ppermute | solution.py:243
  279.5 6.4 %collective-permute-start.27 = (bf16[512,1024]{1,0:T(8,128)(2,1)S(1)}, bf16[512,1024]{1,0:T(8,128)(2,1)S(1)}, u32[]{:S(2)}, u32[]{:S(2)}) collective-permute-start(bf16[512,1024]{1,0:T(8,128)(2,1)S(1)} %slice.494), channel_id=1, source_target_pairs={{0,8},{8,0},{16,24},{24,16},{1,9},{9,1},{17,25},{25,17},{2,10},{10... | collective-permute-start | bytes 3145736 | tf_op jit(solution)/shard_map/ppermute | solution.py:243
  285.0 6.8 %collective-permute-start.30 = (bf16[1408,512]{1,0:T(8,128)(2,1)S(1)}, bf16[1408,512]{1,0:T(8,128)(2,1)S(1)}, u32[]{:S(2)}, u32[]{:S(2)}) collective-permute-start(bf16[1408,512]{1,0:T(8,128)(2,1)S(1)} %constant_dynamic-slice_fusion.1), channel_id=1, source_target_pairs={{0,8},{8,0},{16,24},{24,16},{1,9},{9,1},{17,25},{25,17},{2,10},{10... | collective-permute-start | bytes 4325384 | tf_op jit(solution)/shard_map/ppermute | solution.py:243
  289.8 2.7 collective-permute-start.32
  295.3 40.1 %collective-permute-start.33 = (bf16[512,512]{1,0:T(8,128)(2,1)}, bf16[512,512]{1,0:T(8,128)(2,1)}, u32[]{:S(2)}, u32[]{:S(2)}) collective-permute-start(bf16[512,512]{1,0:T(8,128)(2,1)} %constant_dynamic-slice_fusion), channel_id=1, source_target_pairs={{0,8},{8,0},{16,24},{24,16},{1,9},{9,1},{17,25},{25,17},{2,10},{10... | collective-permute-start | bytes 1572872 | tf_op jit(solution)/shard_map/ppermute | solution.py:243
  296.8 45.1 %collective-permute-start.31 = (bf16[2816,256]{1,0:T(8,128)(2,1)}, bf16[2816,256]{1,0:T(8,128)(2,1)}, u32[]{:S(2)}, u32[]{:S(2)}) collective-permute-start(bf16[2816,256]{1,0:T(8,128)(2,1)} %get-tuple-element.152), channel_id=1, source_target_pairs={{0,16},{8,24},{16,0},{24,8},{1,17},{9,25},{17,1},{25,9},{2,18},{10... | collective-permute-start | bytes 4325384 | tf_op jit(solution)/shard_map/ppermute | solution.py:246
  300.1 35.3 %copy-start.37 = (bf16[512,1024]{1,0:T(8,128)(2,1)S(1)}, bf16[512,1024]{1,0:T(8,128)(2,1)}, u32[]{:S(2)}) copy-start(bf16[512,1024]{1,0:T(8,128)(2,1)} %copy-done.36) | copy-start | bytes 3145732
  336.9 13.9 %collective-permute-start.34 = (bf16[1024,256]{1,0:T(8,128)(2,1)S(1)}, bf16[1024,256]{1,0:T(8,128)(2,1)S(1)}, u32[]{:S(2)}, u32[]{:S(2)}) collective-permute-start(bf16[1024,256]{1,0:T(8,128)(2,1)S(1)} %get-tuple-element.184), channel_id=1, source_target_pairs={{0,16},{8,24},{16,0},{24,8},{1,17},{9,25},{17,1},{25,9},{2,18},{10... | collective-permute-start | bytes 1572872 | tf_op jit(solution)/shard_map/ppermute | solution.py:246
  352.3 11.4 %collective-permute-start.35 = (bf16[512,1024]{1,0:T(8,128)(2,1)S(1)}, bf16[512,1024]{1,0:T(8,128)(2,1)S(1)}, u32[]{:S(2)}, u32[]{:S(2)}) collective-permute-start(bf16[512,1024]{1,0:T(8,128)(2,1)S(1)} %slice.492), channel_id=1, source_target_pairs={{0,8},{8,0},{16,24},{24,16},{1,9},{9,1},{17,25},{25,17},{2,10},{10... | collective-permute-start | bytes 3145736 | tf_op jit(solution)/shard_map/ppermute | solution.py:243
  369.7 2.1 collective-permute-start.40
  379.1 111.4 %collective-permute-start.38 = (bf16[128,2816]{1,0:T(8,128)(2,1)}, bf16[128,2816]{1,0:T(8,128)(2,1)}, u32[]{:S(2)}, u32[]{:S(2)}) collective-permute-start(bf16[128,2816]{1,0:T(8,128)(2,1)} %reduce-scatter.5.cloned.1.call-done), channel_id=1, source_target_pairs={{0,16},{8,24},{16,0},{24,8},{1,17},{9,25},{17,1},{25,9},{2,18},{10... | collective-permute-start | bytes 2162696 | tf_op jit(solution)/shard_map/ppermute | solution.py:246
  384.0 106.5 %copy-start.39 = (bf16[128,2816]{1,0:T(8,128)(2,1)S(1)}, bf16[128,2816]{1,0:T(8,128)(2,1)}, u32[]{:S(2)}) copy-start(bf16[128,2816]{1,0:T(8,128)(2,1)} %reduce-scatter.5.cloned.1.call-done) | copy-start | bytes 2162692
  489.0 16.7 %collective-permute-start.36 = (bf16[128,2688]{1,0:T(8,128)(2,1)}, bf16[128,2688]{1,0:T(8,128)(2,1)S(1)}, u32[]{:S(2)}, u32[]{:S(2)}) collective-permute-start(bf16[128,2688]{1,0:T(8,128)(2,1)} %reduce-scatter.3.cloned.1.call-done), channel_id=1, source_target_pairs={{0,16},{8,24},{16,0},{24,8},{1,17},{9,25},{17,1},{25,9},{2,18},{10... | collective-permute-start | bytes 2064392 | tf_op jit(solution)/shard_map/ppermute | solution.py:246
  491.8 17.1 %collective-permute-start.39 = (bf16[128,2816]{1,0:T(8,128)(2,1)S(1)}, bf16[128,2816]{1,0:T(8,128)(2,1)S(1)}, u32[]{:S(2)}, u32[]{:S(2)}) collective-permute-start(bf16[128,2816]{1,0:T(8,128)(2,1)S(1)} %add_convert_fusion.1), channel_id=1, source_target_pairs={{0,8},{8,0},{16,24},{24,16},{1,9},{9,1},{17,25},{25,17},{2,10},{10... | collective-permute-start | bytes 2162696 | tf_op jit(solution)/shard_map/ppermute | solution.py:243
  508.8 2.6 collective-permute-start.37
  (53 other events, 352.1 us)
Sparse Core Ops, SparseCore 0:
  265.5 113.5 reduce-scatter.4
  382.7 106.2 reduce-scatter.2

commit v3 on v2

--- a/solution.py
+++ b/solution.py
@@ -296,7 +296,7 @@
 
     def shared_lanes(shard):
         lanes = shard.shape[1] // LANES
-        return (lanes - 2 * (lanes * 4 // 11)) * LANES
+        return (lanes - 2 * (lanes // 2)) * LANES
 
     def held_columns(shard):
         shared = shared_lanes(shard)
@@ -327,27 +327,19 @@
         pieces_b = ring_pieces(held_b)
         mine_a = in_ring_order(place, pieces_a)
         far_a = sides(mine_a)
-        pieces_b, far_a, mine_a, held_c = tie((pieces_b, far_a, mine_a, held_columns(shard_c)))
-        pieces_c = ring_pieces(held_c)
+        pieces_b, far_a, mine_a, shard_c, shard_d = tie((pieces_b, far_a, mine_a, shard_c, shard_d))
         mine_b = in_ring_order(place, pieces_b)
-        far_b = sides(mine_b)
-        other_a = to_chip(swapped_halves(shard_a, mine_a, far_a), 1)
-        pieces_c, far_b, mine_b, other_a, held_d = tie(
-            (pieces_c, far_b, mine_b, other_a, held_columns(shard_d))
-        )
-        pieces_d = ring_pieces(held_d)
-        mine_c = in_ring_order(place, pieces_c)
+        halves_a = swapped_halves(shard_a, mine_a, far_a)
+        mine_b, halves_a = tie((mine_b, halves_a))
+        far_b, other_a = sides(mine_b), to_chip(halves_a, 1)
+        far_b, other_a = tie((far_b, other_a))
         halves_b = swapped_halves(shard_b, mine_b, far_b)
-        mine_c, halves_b, other_a = tie((mine_c, halves_b, other_a))
-        far_c, other_b = sides(mine_c), to_chip(halves_b, 1)
+        halves_b, other_a = tie((halves_b, other_a))
+        other_b = to_chip(halves_b, 1)
         whole_a = join(mine_a, far_a, other_a)
-        pieces_d, far_c, mine_c, other_b, whole_a = tie((pieces_d, far_c, mine_c, other_b, whole_a))
-        mine_d = in_ring_order(place, pieces_d)
-        halves_c = swapped_halves(shard_c, mine_c, far_c)
-        mine_d, halves_c, whole_a = tie((mine_d, halves_c, whole_a))
-        far_d, other_c = sides(mine_d), to_chip(halves_c, 1)
     else:
         whole_a = gather(shard_a)
+    up_mat, whole_d = gather(shard_c), gather(shard_d)
     qkv_mat = whole_a[:, gains.shape[1] :]
     gain_rows = whole_a[:, : gains.shape[1]].reshape(fsdp, w_query.shape[0], -1)
     gain_one = gain_rows[:, 0, : attn_gain.shape[0]].reshape(1, width).astype(f32)
@@ -367,10 +359,7 @@
     qkv = dot_nn(normed, qkv_mat)
     attended, q_rot, k_rot, blended = attend(starts, cosine, sine, qkv, first_half, length)
     if by_ring:
-        attended, far_d, other_c = tie((attended, far_d, other_c))
-        halves_d = swapped_halves(shard_d, mine_d, far_d)
-        halves_d, attended, other_c = tie((halves_d, attended, other_c))
-        other_d = to_chip(halves_d, 1)
+        attended, other_b = tie((attended, other_b))
         whole_b = join(mine_b, far_b, other_b)
     else:
         whole_b = gather(shard_b)
@@ -382,13 +371,7 @@
     inverse_two = norm_stats(mixed)
     normed_two = pair((mixed * inverse_two * gain_two).astype(bf16))
     gate = dot_nn(normed_two, gate_mat)
-    up_mat = join(mine_c, far_c, other_c) if by_ring else gather(shard_c)
     up_val = dot_nn(normed_two, up_mat)
-    if by_ring:
-        other_d, gate, up_val = tie((other_d, gate, up_val))
-        whole_d = join(mine_d, far_d, other_d)
-    else:
-        whole_d = gather(shard_d)
     down_mat = rows_from_cols(whole_d)
     sigma = jax.nn.sigmoid(gate)
     silu_gate = gate * sigma
@@ -416,13 +399,13 @@
     grad_out_w = chip_parts(grad_out_w)
     dq, dk, dv = attend_back(starts, cosine, sine, q_rot, k_rot, blended, grad_attended, length)
     grad_down, grad_out_w, dq = tie((grad_down, grad_out_w, dq))
-    height, down_height = w_query.shape[0], w_down.shape[0]
-    blocks = -(-down_height // height)
-    grad_down = added(grad_down).reshape(fsdp, down_height, -1)
-    grad_down = jnp.pad(grad_down, ((0, 0), (0, blocks * height - down_height), (0, 0)))
-    grad_down = [
-        grad_down[:, k * height : (k + 1) * height].reshape(fsdp * height, -1) for k in range(blocks)
-    ]
+    grad_do = jnp.concatenate(
+        [added(parts).reshape(fsdp, -1, hw // chips) for parts in (grad_down, grad_out_w)], axis=1
+    )
+    if by_ring:
+        grad_do = grad_do.reshape(ring, 2, *grad_do.shape[1:])
+        at_side = lambda which: lax.dynamic_slice_in_dim(grad_do, which, 1, 1)[:, 0]
+        do_mine, do_far = at_side(side), at_side(1 - side)
     grad_normed = mine_and_partner(
         dot_nt(dq, qkv_mat[:, :hw]) + dot_nt(dk, qkv_mat[:, hw : 2 * hw])
         + dot_nt(dv, qkv_mat[:, 2 * hw :])
@@ -449,12 +432,17 @@
         axis=1,
     )
     extra = jnp.pad(extra, ((0, 0), (0, LANES - extra.shape[1]))).astype(bf16)
-    grad_a = jnp.concatenate(
-        [dot_tn(normed, d).astype(bf16) for d in (dq, dk, dv)]
-        + [added(grad_out_w)] + grad_down + [extra],
-        axis=1,
-    )
-    grad_a = row_major(scatter(row_major(grad_a)))
+    grad_q, grad_k = (chip_parts(dot_tn(normed, d).astype(bf16)) for d in (dq, dk))
+    grad_v = dot_tn(normed, dv).astype(bf16)
+    grad_a = jnp.concatenate([added(grad_q), added(grad_k), grad_v, extra], axis=1)
+    if by_ring:
+        grad_a, grad_b, do_mine, do_far = tie((grad_a, grad_b, do_mine, do_far))
+        grad_do = added([do_mine, sides(do_far)])
+        at_place = lambda step: lax.dynamic_slice_in_dim(grad_do, (place + step) % ring, 1, 0)[0]
+        grad_do = added([at_place(0)] + [around(at_place(step), step) for step in range(1, ring)])
+    else:
+        grad_do = scatter(grad_do.reshape(-1, hw // chips))
+    grad_a = scatter(row_major(grad_a))
 
     def from_chips(values):
         return [values] + [to_chip(values, step) for step in range(1, chips)]
@@ -462,35 +450,40 @@
     def whole_columns(half, other, at, size):
         return in_order(half[:, at : at + size], other[:, at : at + size], 1).astype(f32)
 
-    ff_half, share = gate_mat.shape[1], hw // chips
+    ff_half = gate_mat.shape[1]
     half = added(from_chips(grad_b))
     other = swap(half)
     share_gate, share_up = (whole_columns(half, other, k * ff_half, ff_half) for k in range(2))
-    got = [row_major(g) for g in from_chips(grad_a)]
-    split_at = 3 * hw + (1 + blocks) * share
-    by_chip = [
-        functools.reduce(
-            lambda kept, back: jnp.where(
-                (chip - back) % chips == which, got[back][:, 3 * hw : split_at], kept
-            ),
-            range(1, chips), got[0][:, 3 * hw : split_at],
-        )
-        for which in range(chips)
-    ]
+    def chip_order(got):
+        return [
+            functools.reduce(
+                lambda kept, back: jnp.where((chip - back) % chips == which, got[back], kept),
+                range(1, chips), got[0],
+            )
+            for which in range(chips)
+        ]
+
+    half = jnp.concatenate(chip_order(from_chips(grad_do)), axis=1)
+    both = whole_columns(half, swap(half), 0, hw)
+    share_down, share_output = both[: w_down.shape[0]], both[w_down.shape[0] :]
+    got, share = from_chips(grad_a), hw // chips
+    at_v = 2 * share
     half = jnp.concatenate(
-        [added([g[:, : 3 * hw] for g in got])]
-        + [p[:, k * share : (k + 1) * share] for k in range(1 + blocks) for p in by_chip]
-        + [g[:, split_at:] for g in got],
+        [
+            piece for k in range(2)
+            for piece in chip_order([g[:, k * share : (k + 1) * share] for g in got])
+        ]
+        + [added([g[:, at_v : at_v + hw] for g in got])]
+        + [g[:, at_v + hw :] for g in got],
         axis=1,
     )
     other = swap(half)
-    share_query, share_key, share_value, share_output, *down_blocks = (
-        whole_columns(half, other, k * hw, hw) for k in range(4 + blocks)
-    )
-    share_down = jnp.concatenate(down_blocks, axis=0)[:down_height]
+    share_query, share_key, share_value = (
+        whole_columns(half, other, k * hw, hw) for k in range(3)
+    )
     gain_sums = sum(
         which[:, at : at + LANES].astype(f32)
-        for which in (half, other) for at in range((4 + blocks) * hw, half.shape[1], LANES)
+        for which in (half, other) for at in range(3 * hw, half.shape[1], LANES)
     )
     share_gain_one, share_gain_two = gain_sums[:, 0], gain_sums[:, 1]
     squares = jnp.sum(gain_sums[:, 2:8], axis=0).reshape(3, 2).sum(axis=0)

time: 533 us -> 455 us (0.85)
  waiting for transfers between devices: 202 us -> 155 us
  local copies, waits for them, and re-layouts: 35.4 us -> 22.2 us
  Pallas kernels: 82.6 us -> 69.7 us
  starting transfers between devices: 45.8 us -> 35.6 us
  matrix products: 78 us -> 86.2 us
    reduce_scatter x2, waiting for transfers between devices: 107 us -> 3.59 us  [scatter(): return lax.psum_scatter(whole, 'fsdp', scatter_dimension=0, tiled=True)]
    ppermute x4 -> x3, waiting for transfers between devices: 0.01 us -> 40.2 us  [sides(): return lax.ppermute(values, 'fsdp', [(i, i ^ 1) for i in range(fsdp)])]
    ppermute x8 -> x9, waiting for transfers between devices: 25.8 us -> 51 us  [to_chip(): lax.ppermute(values, 'dp', [(i, (i + 2 * step) % dp) for i in range(dp)])]
    ppermute x12 -> x9, waiting for transfers between devices: 66.2 us -> 47.2 us  [around(): lax.ppermute(values, 'fsdp', [(i, (i + 2 * step) % fsdp) for i in range(f...]
    ppermute x12 -> x9, starting transfers between devices: 29 us -> 19.8 us  [around(): lax.ppermute(values, 'fsdp', [(i, (i + 2 * step) % fsdp) for i in range(f...]
    all_gather x0 -> x2, waiting for transfers between devices: none -> 9.13 us  [gather(): return lax.all_gather(shard, 'fsdp', axis=0, tiled=True)]
    pallas_call x4 -> x2, Pallas kernels: 16.4 us -> 8.6 us  [joined(): pl.pallas_call(join_kernel, in_specs=[pl.BlockSpec(memory_space=pltpu.SME...]
    unnamed x128 -> x91, local copies, waits for them, and re-layouts: 12.1 us -> 5.34 us
  transfers between devices with their start and end apart: 43 -> 43, of which waited for: 18 -> 19; matrix products, arithmetic and copies ran while one was open for 23% -> 27% of each run, Pallas kernels for 14% -> 15%
where the time goes in v3:
time: 455 us; the launch traced here: 447 us
  waiting for transfers between devices  155 us (34%)
  matrix products  86.2 us (19%)
  Pallas kernels  69.7 us (15%)
  other arithmetic  63 us (14%)
  starting transfers between devices  35.6 us (8%)
  local copies, waits for them, and re-layouts  22.2 us (5%)
  between operations  15.4 us (3%)
    ppermute x9, waiting for transfers between devices, to_chip(): lax.ppermute(values, 'dp', [(i, (i + 2 * step) % dp) for i in range(dp)])  51 us
    ppermute x9, waiting for transfers between devices, around(): lax.ppermute(values, 'fsdp', [(i, (i + 2 * step) % fsdp) for i in range(f...  47.2 us
    ppermute x3, waiting for transfers between devices, sides(): return lax.ppermute(values, 'fsdp', [(i, i ^ 1) for i in range(fsdp)])  40.2 us
    pallas_call x1, Pallas kernels, attend_back(): pl.pallas_call(attend_back_kernel, grid=(tokens // length, width // LANES...  35.4 us
    dot_general x7, matrix products, dot_tn(): lax.dot_general(a, b, (((0,), (0,)), ((), ())), preferred_element_type=f32)  29.1 us
    dot_general x7, matrix products, dot_nt(): lax.dot_general(a, b, (((1,), (1,)), ((), ())), preferred_element_type=f32)  28.6 us
    dot_general x5, matrix products, dot_nn(): return jnp.dot(a, b, preferred_element_type=f32)  28.6 us
    pallas_call x1, Pallas kernels, attend(): pl.pallas_call(attend_kernel, grid=(tokens // length, pairs), in_specs=[p...  21.1 us
  transfers between devices with their start and end apart: 43, of which 19 were waited for; matrix products, arithmetic and copies ran while one was open for 27% of the time, Pallas kernels for 15%

profile of v3, /device:TPU:0, one launch (start us, length us, event | category | flops | bytes accessed | tf_op | source)
XLA Modules:
  0.0 446.6 jit_solution(12312967975588316915)
XLA Ops:
  10.2 3.1 collective-permute-start.2
  13.3 2.6 collective-permute-start.3
  18.3 3.7 collective-permute-done.2.refs_1_
  21.9 9.0 %collective-permute-done.3.refs_2_ = bf16[128,896]{1,0:T(8,128)(2,1)S(1)} collective-permute-done((bf16[128,896]{1,0:T(8,128)(2,1)S(1)}, bf16[128,896]{1,0:T(8,128)(2,1)S(1)}, u32[]{:S(2)}, u32[]{:S(2)}) %collective-permute-start.3) | collective-permute-done | bytes 229408 | tf_op jit(solution)/shard_map/ppermute | solution.py:295
  31.6 2.3 ring_order.2.mine_ref
  35.4 4.8 %collective-permute-start.5 = (bf16[128,1024]{1,0:T(8,128)(2,1)S(1)}, bf16[128,1024]{1,0:T(8,128)(2,1)S(1)}, u32[]{:S(2)}, u32[]{:S(2)}) collective-permute-start(bf16[128,1024]{1,0:T(8,128)(2,1)S(1)} %pad_maximum_fusion.19.refs_0_), channel_id=1, source_target_pairs={{0,2},{1,3},{2,4},{3,5},{4,6},{5,7},{6,0},{7,1},{8,10},{9,11},{10,... | collective-permute-start | bytes 786440 | tf_op jit(solution)/shard_map/ppermute | solution.py:295
  46.1 3.0 collective-permute-done.5.refs_1_
  49.1 9.2 %collective-permute-done.6.refs_2_ = bf16[128,1024]{1,0:T(8,128)(2,1)S(1)} collective-permute-done((bf16[128,1024]{1,0:T(8,128)(2,1)S(1)}, bf16[128,1024]{1,0:T(8,128)(2,1)S(1)}, u32[]{:S(2)}, u32[]{:S(2)}) %collective-permute-start.6) | collective-permute-done | bytes 262176 | tf_op jit(solution)/shard_map/ppermute | solution.py:295
  60.3 2.3 ring_order.3.mine_ref
  69.1 26.2 %collective-permute-done.9.far_ref = bf16[4,128,1024]{2,1,0:T(8,128)(2,1)S(1)} collective-permute-done((bf16[4,128,1024]{2,1,0:T(8,128)(2,1)S(1)}, bf16[4,128,1024]{2,1,0:T(8,128)(2,1)S(1)}, u32[]{:S(2)}, u32[]{:S(2)}) %collective-permute-start.9) | collective-permute-done | bytes 1048608 | tf_op jit(solution)/shard_map/ppermute | solution.py:292
  95.3 5.8 %collective-permute-done.10.other_ref = bf16[2,4,128,768]{3,2,1,0:T(8,128)(2,1)} collective-permute-done((bf16[2,4,128,768]{3,2,1,0:T(8,128)(2,1)}, bf16[2,4,128,768]{3,2,1,0:T(8,128)(2,1)}, u32[]{:S(2)}, u32[]{:S(2)}) %collective-permute-start.10) | collective-permute-done | bytes 1572896 | tf_op jit(solution)/shard_map/ppermute | solution.py:246
  104.1 3.0 fusion.28
  110.3 4.0 joined.2
  115.3 8.7 %fusion.2.q_ref.k_ref.v_ref = f32[1024,1536]{1,0:T(8,128)} fusion(bf16[1024,1664]{1,0:T(8,128)(2,1)} %bitcast.76, f32[1024]{0:T(1024)S(1)} %bitcast.89, f32[1024]{0:T(1024)S(1)} %add_rsqrt_fusion, bf16[512,1024]{1,0:T(8,128)(2,1)} %collective-permute-done, bf16[512,1024]{1,0:T(8,128)(2,1)} %bitcast), kind=kOutput, calls=%fused_computation.18 | convolution fusion | flops 3228565504 | bytes 11542528 | tf_op jit(solution)/shard_map/dot_general | solution.py:66
  124.0 21.1 %attend.1 = (bf16[1024,512]{1,0:T(8,128)(2,1)}, bf16[1024,512]{1,0:T(8,128)(2,1)}, bf16[1024,512]{1,0:T(8,128)(2,1)}, bf16[1024,512]{1,0:T(8,128)(2,1)}) custom-call(s32[1024,1]{1,0:T(8,128)} %copy.37.start_ref, f32[1024,128]{1,0:T(8,128)} %get-tuple-element.161.cos_ref, f32[1024,128]{1,0:T(8,128)} %get-tuple-element.160.sin_ref, ...), custom_call_target="tpu_custom_call" | custom-call | tf_op jit(solution)/shard_map/attend/pallas_call | solution.py:145
  145.1 4.6 %joined.3 = bf16[4,2,128,1920]{3,2,1,0:T(8,128)(2,1)} custom-call(s32[2]{0:T(128)} %pad_add_fusion.2.at_ref, bf16[4,128,1024]{2,1,0:T(8,128)(2,1)} %ring_order.3.mine_ref, bf16[4,128,1024]{2,1,0:T(8,128)(2,1)} %copy-done.15, bf16[2,4,128,896]{3,2,1,0:T(8,128)(2,1)} %collective-permute-done.12.other_ref), custom_call_target="tpu_custom_call" | custom-call | tf_op jit(solution)/shard_map/joined/pallas_call | solution.py:208
  161.3 2.5 multiply_reduce_fusion.7
  165.1 2.6 constant_dynamic-slice_fusion.4
  168.0 2.4 multiply_reduce_fusion.2
  170.4 2.4 multiply_reduce_fusion.1
  174.2 9.1 %all-gather.3.cloned.1.call-done = bf16[1024,1408]{1,0:T(8,128)(2,1)} async-done(((bf16[128,1408]{1,0:T(8,128)(2,1)}), bf16[1024,1408]{1,0:T(8,128)(2,1)}) %all-gather.3.cloned.1.call-update) | async-done | bytes 2883600 | tf_op jit(solution)/shard_map/all_gather | solution.py:283
  183.3 6.0 %fusion.55 = f32[1024,1408]{1,0:T(8,128)S(1)} fusion(bf16[1024,1408]{1,0:T(8,128)(2,1)} %all-gather.3.cloned.1.call-done, bf16[512,1024]{1,0:T(8,128)(2,1)} %collective-permute-done.15, bf16[512,1024]{1,0:T(8,128)(2,1)} %multiply_convert_fusion.4), kind=kOutput, calls=%fused_computation.233 | convolution fusion | flops 2956984320 | bytes 10747904 | tf_op jit(solution)/shard_map/dot_general | solution.py:66
  192.9 5.1 %fusion.12 = f32[1024,1408]{1,0:T(8,128)S(1)} fusion(bf16[1408,512]{1,0:T(8,128)(2,1)S(1)} %get-tuple-element.121, bf16[1408,512]{1,0:T(8,128)(2,1)S(1)} %get-tuple-element.120, bf16[512,1024]{1,0:T(8,128)(2,1)} %collective-permute-done.18, bf16[512,1024]{1,0:T(8,128)(2,1)} %bitcast.22), kind=kOutput, calls=%fused_computation.60 | convolution fusion | flops 2962751488 | bytes 10747904 | tf_op jit(solution)/shard_map/dot_general | solution.py:58
  198.0 9.2 %multiply_convert_fusion.1 = (bf16[1024,1408]{1,0:T(8,128)(2,1)}, bf16[1024,1408]{1,0:T(8,128)(2,1)S(1)}, bf16[1024,1408]{1,0:T(8,128)(2,1)}) fusion(f32[1024,1408]{1,0:T(8,128)S(1)} %fusion.12, f32[1024,1408]{1,0:T(8,128)S(1)} %fusion.55, bf16[1024,1920]{1,0:T(8,128)(2,1)S(1)} %bitcast.82, bf16[512,1024]{1,0:T(8,128)(2,1)} %collective-permute-done.15, ...), kind=kOutput, calls=%fused_computation.2 | convolution fusion | flops 2978611200 | bytes 25165824 | tf_op jit(solution)/shard_map/dot_general | solution.py:66
  207.3 6.4 %convolution_convert_fusion.1 = bf16[1024,1408]{1,0:T(8,128)(2,1)S(1)} fusion(bf16[1024,1408]{1,0:T(8,128)(2,1)S(1)} %get-tuple-element.77, bf16[512,1024]{1,0:T(8,128)(2,1)} %collective-permute-done.15, bf16[512,1024]{1,0:T(8,128)(2,1)} %multiply_convert_fusion.4), kind=kOutput, calls=%fused_computation.12 | convolution fusion | flops 2958426112 | bytes 7864320 | tf_op jit(solution)/shard_map/dot_general | solution.py:62
  213.7 5.3 %convolution_convert_fusion.2 = bf16[1024,1408]{1,0:T(8,128)(2,1)S(1)} fusion(bf16[1024,1408]{1,0:T(8,128)(2,1)S(1)} %copy-done.43, bf16[512,1024]{1,0:T(8,128)(2,1)} %collective-permute-done.15, bf16[512,1024]{1,0:T(8,128)(2,1)} %multiply_convert_fusion.4), kind=kOutput, calls=%fused_computation.13 | convolution fusion | flops 2958426112 | bytes 7864320 | tf_op jit(solution)/shard_map/dot_general | solution.py:62
  219.1 2.9 pad_maximum_fusion
  222.0 8.2 %fusion.4 = f32[1024,1024]{1,0:T(8,128)} fusion(bf16[1024,1408]{1,0:T(8,128)(2,1)} %get-tuple-element.76, bf16[1024,1920]{1,0:T(8,128)(2,1)} %bitcast.81), kind=kOutput, calls=%fused_computation.22 | convolution fusion | flops 2952790016 | bytes 9961472 | tf_op jit(solution)/shard_map/dot_general | solution.py:58
  230.5 7.5 %convolution_add_fusion = f32[1024,1024]{1,0:T(8,128)S(1)} fusion(f32[1024,1024]{1,0:T(8,128)} %fusion.4, bf16[1024,1408]{1,0:T(8,128)(2,1)} %copy-done.42, bf16[1024,1408]{1,0:T(8,128)(2,1)} %all-gather.3.cloned.1.call-done), kind=kOutput, calls=%fused_computation.59 | convolution fusion | flops 2953838592 | bytes 14155776 | tf_op jit(solution)/shard_map/dot_general | solution.py:58
  238.2 3.4 fusion.13
  242.3 4.8 %convolution_convert_fusion = bf16[1408,1024]{1,0:T(8,128)(2,1)S(1)} fusion(bf16[1024,1408]{1,0:T(8,128)(2,1)S(1)} %copy-done.41, bf16[512,1024]{1,0:T(8,128)(2,1)} %collective-permute-done.18, bf16[512,1024]{1,0:T(8,128)(2,1)} %bitcast.22), kind=kOutput, calls=%fused_computation.11 | convolution fusion | flops 2958426112 | bytes 7864320 | tf_op jit(solution)/shard_map/dot_general | solution.py:62
  248.3 3.9 fusion.57
  257.8 2.3 convolution_convert_fusion.6.grad_ref
  260.0 35.4 %attend_back.1 = (bf16[1024,512]{1,0:T(8,128)(2,1)}, bf16[1024,512]{1,0:T(8,128)(2,1)}, bf16[1024,512]{1,0:T(8,128)(2,1)}) custom-call(s32[1024,1]{1,0:T(8,128)} %copy.37.start_ref, f32[1024,128]{1,0:T(8,128)} %get-tuple-element.161.cos_ref, f32[1024,128]{1,0:T(8,128)} %get-tuple-element.160.sin_ref, bf16[1024,512]{1,0:T(8,128)(2,1)} %get-tuple-element.79.q_rot_ref, ...), custom_call_target="tpu_custom_call" | custom-call | tf_op jit(solution)/shard_map/attend_back/pallas_call | solution.py:159
  295.4 3.0 fusion.17
  298.4 3.0 convolution_convert_fusion.4
  302.3 3.9 convolution_convert_fusion.3
  310.4 6.0 %collective-permute-done.27 = bf16[1024,256]{1,0:T(8,128)(2,1)S(1)} collective-permute-done((bf16[1024,256]{1,0:T(8,128)(2,1)S(1)}, bf16[1024,256]{1,0:T(8,128)(2,1)S(1)}, u32[]{:S(2)}, u32[]{:S(2)}) %collective-permute-start.27) | collective-permute-done | bytes 524320 | tf_op jit(solution)/shard_map/ppermute | solution.py:246
  317.3 9.8 %collective-permute-done.24 = bf16[1024,256]{1,0:T(8,128)(2,1)S(1)} collective-permute-done((bf16[1024,256]{1,0:T(8,128)(2,1)S(1)}, bf16[1024,256]{1,0:T(8,128)(2,1)S(1)}, u32[]{:S(2)}, u32[]{:S(2)}) %collective-permute-start.24) | collective-permute-done | bytes 524320 | tf_op jit(solution)/shard_map/ppermute | solution.py:246
  328.6 4.2 convolution_convert_fusion.5
  336.7 9.8 %collective-permute-done.26 = bf16[1024,256]{1,0:T(8,128)(2,1)S(1)} collective-permute-done((bf16[1024,256]{1,0:T(8,128)(2,1)S(1)}, bf16[1024,256]{1,0:T(8,128)(2,1)S(1)}, u32[]{:S(2)}, u32[]{:S(2)}) %collective-permute-start.26) | collective-permute-done | bytes 524320 | tf_op jit(solution)/shard_map/ppermute | solution.py:246
  348.4 2.8 fusion.8
  358.0 13.2 %collective-permute-done.36 = bf16[128,2816]{1,0:T(8,128)(2,1)S(1)} collective-permute-done((bf16[128,2816]{1,0:T(8,128)(2,1)}, bf16[128,2816]{1,0:T(8,128)(2,1)S(1)}, u32[]{:S(2)}, u32[]{:S(2)}) %collective-permute-start.36) | collective-permute-done | bytes 720928 | tf_op jit(solution)/shard_map/ppermute | solution.py:246
  372.7 14.0 %collective-permute-done.30 = bf16[4,480,256]{2,1,0:T(8,128)(2,1)S(1)} collective-permute-done((bf16[4,480,256]{2,1,0:T(8,128)(2,1)}, bf16[4,480,256]{2,1,0:T(8,128)(2,1)S(1)}, u32[]{:S(2)}, u32[]{:S(2)}) %collective-permute-start.30) | collective-permute-done | bytes 983072 | tf_op jit(solution)/shard_map/ppermute | solution.py:292
  387.1 2.7 collective-permute-start.33
  396.2 20.8 %collective-permute-done.32 = bf16[480,256]{1,0:T(8,128)(2,1)S(1)} collective-permute-done((bf16[480,256]{1,0:T(8,128)(2,1)S(1)}, bf16[480,256]{1,0:T(8,128)(2,1)S(1)}, u32[]{:S(2)}, u32[]{:S(2)}) %collective-permute-start.32) | collective-permute-done | bytes 245792 | tf_op jit(solution)/shard_map/ppermute | solution.py:295
  419.8 3.6 reduce-scatter.5.cloned.1.call-done
  424.6 6.5 %collective-permute-done.28 = bf16[128,1152]{1,0:T(8,128)(2,1)S(1)} collective-permute-done((bf16[128,1152]{1,0:T(8,128)(2,1)}, bf16[128,1152]{1,0:T(8,128)(2,1)S(1)}, u32[]{:S(2)}, u32[]{:S(2)}) %collective-permute-start.28) | collective-permute-done | bytes 294944 | tf_op jit(solution)/shard_map/ppermute | solution.py:246
  (273 shorter events, 95.2 us)
Async XLA Ops:
  7.2 157.9 %all-gather.5.cloned.1.call-start = ((), (), s32[]{:S(2)}) async-start(), calls=%async_computation.3 | async-start | bytes 3244032 | tf_op jit(solution)/shard_map/all_gather | solution.py:283
  10.2 11.7 %collective-permute-start.2 = (bf16[128,896]{1,0:T(8,128)(2,1)S(1)}, bf16[128,896]{1,0:T(8,128)(2,1)S(1)}, u32[]{:S(2)}, u32[]{:S(2)}) collective-permute-start(bf16[128,896]{1,0:T(8,128)(2,1)S(1)} %pad_maximum_fusion.20.refs_0_), channel_id=1, source_target_pairs={{0,2},{1,3},{2,4},{3,5},{4,6},{5,7},{6,0},{7,1},{8,10},{9,11},{10,... | collective-permute-start | bytes 688136 | tf_op jit(solution)/shard_map/ppermute | solution.py:295
  13.3 17.6 %collective-permute-start.3 = (bf16[128,896]{1,0:T(8,128)(2,1)S(1)}, bf16[128,896]{1,0:T(8,128)(2,1)S(1)}, u32[]{:S(2)}, u32[]{:S(2)}) collective-permute-start(bf16[128,896]{1,0:T(8,128)(2,1)S(1)} %pad_maximum_fusion.20.refs_0_), channel_id=1, source_target_pairs={{0,4},{1,5},{2,6},{3,7},{4,0},{5,1},{6,2},{7,3},{8,12},{9,13},{10,... | collective-permute-start | bytes 688136 | tf_op jit(solution)/shard_map/ppermute | solution.py:295
  15.9 15.0 %collective-permute-start.4 = (bf16[128,896]{1,0:T(8,128)(2,1)S(1)}, bf16[128,896]{1,0:T(8,128)(2,1)}, u32[]{:S(2)}, u32[]{:S(2)}) collective-permute-start(bf16[128,896]{1,0:T(8,128)(2,1)S(1)} %pad_maximum_fusion.20.refs_0_), channel_id=1, source_target_pairs={{0,6},{1,7},{2,0},{3,1},{4,2},{5,3},{6,4},{7,5},{8,14},{9,15},{10,... | collective-permute-start | bytes 688136 | tf_op jit(solution)/shard_map/ppermute | solution.py:295
  17.3 41.1 %copy-start.39 = (s32[1,512]{1,0:T(1,128)S(1)}, s32[1,512]{1,0:T(1,128)}, u32[]{:S(2)}) copy-start(s32[1,512]{1,0:T(1,128)} %param.16) | copy-start | bytes 6148
  17.3 42.0 %copy-start.14 = (bf16[1,512,1024]{2,1,0:T(8,128)(2,1)S(1)}, bf16[1,512,1024]{2,1,0:T(8,128)(2,1)}, u32[]{:S(2)}) copy-start(bf16[1,512,1024]{2,1,0:T(8,128)(2,1)} %param.15) | copy-start | bytes 3145732
  18.2 42.0 %copy-start.30 = (bf16[128,1024]{1,0:T(8,128)(2,1)}, bf16[128,1024]{1,0:T(8,128)(2,1)S(1)}, u32[]{:S(2)}) copy-start(bf16[128,1024]{1,0:T(8,128)(2,1)S(1)} %pad_maximum_fusion.19.refs_0_) | copy-start | bytes 786436
  33.8 24.5 %collective-permute-start.8 = (bf16[4,128,896]{2,1,0:T(8,128)(2,1)}, bf16[4,128,896]{2,1,0:T(8,128)(2,1)S(1)}, u32[]{:S(2)}, u32[]{:S(2)}) collective-permute-start(bf16[4,128,896]{2,1,0:T(8,128)(2,1)} %ring_order.2.mine_ref), channel_id=1, source_target_pairs={{0,1},{1,0},{2,3},{3,2},{4,5},{5,4},{6,7},{7,6},{8,9},{9,8},{10,11... | collective-permute-start | bytes 2752520 | tf_op jit(solution)/shard_map/ppermute | solution.py:292
  35.4 13.7 %collective-permute-start.5 = (bf16[128,1024]{1,0:T(8,128)(2,1)S(1)}, bf16[128,1024]{1,0:T(8,128)(2,1)S(1)}, u32[]{:S(2)}, u32[]{:S(2)}) collective-permute-start(bf16[128,1024]{1,0:T(8,128)(2,1)S(1)} %pad_maximum_fusion.19.refs_0_), channel_id=1, source_target_pairs={{0,2},{1,3},{2,4},{3,5},{4,6},{5,7},{6,0},{7,1},{8,10},{9,11},{10,... | collective-permute-start | bytes 786440 | tf_op jit(solution)/shard_map/ppermute | solution.py:295
  40.2 18.1 %collective-permute-start.6 = (bf16[128,1024]{1,0:T(8,128)(2,1)S(1)}, bf16[128,1024]{1,0:T(8,128)(2,1)S(1)}, u32[]{:S(2)}, u32[]{:S(2)}) collective-permute-start(bf16[128,1024]{1,0:T(8,128)(2,1)S(1)} %pad_maximum_fusion.19.refs_0_), channel_id=1, source_target_pairs={{0,4},{1,5},{2,6},{3,7},{4,0},{5,1},{6,2},{7,3},{8,12},{9,13},{10,... | collective-permute-start | bytes 786440 | tf_op jit(solution)/shard_map/ppermute | solution.py:295
  42.3 16.0 %collective-permute-start.7 = (bf16[128,1024]{1,0:T(8,128)(2,1)S(1)}, bf16[128,1024]{1,0:T(8,128)(2,1)S(1)}, u32[]{:S(2)}, u32[]{:S(2)}) collective-permute-start(bf16[128,1024]{1,0:T(8,128)(2,1)S(1)} %pad_maximum_fusion.19.refs_0_), channel_id=1, source_target_pairs={{0,6},{1,7},{2,0},{3,1},{4,2},{5,3},{6,4},{7,5},{8,14},{9,15},{10,... | collective-permute-start | bytes 786440 | tf_op jit(solution)/shard_map/ppermute | solution.py:295
  58.4 124.9 %all-gather.3.cloned.1.call-start = ((), (), s32[]{:S(2)}) async-start(), calls=%async_computation.2 | async-start | bytes 3244032 | tf_op jit(solution)/shard_map/all_gather | solution.py:283
  58.4 7.8 %collective-permute-start.1 = (s32[1,512]{1,0:T(1,128)S(1)}, s32[1,512]{1,0:T(1,128)S(1)}, u32[]{:S(2)}, u32[]{:S(2)}) collective-permute-start(s32[1,512]{1,0:T(1,128)S(1)} %copy-done.39), channel_id=1, source_target_pairs={{0,8},{8,0},{16,24},{24,16},{1,9},{9,1},{17,25},{25,17},{2,10},{10... | collective-permute-start | bytes 6152 | tf_op jit(solution)/shard_map/ppermute | solution.py:243
  58.5 49.7 %collective-permute-start = (bf16[512,1024]{1,0:T(8,128)(2,1)}, bf16[512,1024]{1,0:T(8,128)(2,1)}, u32[]{:S(2)}, u32[]{:S(2)}) collective-permute-start(bf16[512,1024]{1,0:T(8,128)(2,1)} %bitcast), channel_id=1, source_target_pairs={{0,8},{8,0},{16,24},{24,16},{1,9},{9,1},{17,25},{25,17},{2,10},{10... | collective-permute-start | bytes 3145736 | tf_op jit(solution)/shard_map/ppermute | solution.py:243
  60.2 46.9 %collective-permute-start.11 = (bf16[512,512]{1,0:T(8,128)(2,1)}, bf16[512,512]{1,0:T(8,128)(2,1)S(1)}, u32[]{:S(2)}, u32[]{:S(2)}) collective-permute-start(bf16[512,512]{1,0:T(8,128)(2,1)} %get-tuple-element.142), channel_id=1, source_target_pairs={{0,8},{8,0},{16,24},{24,16},{1,9},{9,1},{17,25},{25,17},{2,10},{10... | collective-permute-start | bytes 1572872 | tf_op jit(solution)/shard_map/ppermute | solution.py:243
  64.1 37.0 %collective-permute-start.10 = (bf16[2,4,128,768]{3,2,1,0:T(8,128)(2,1)}, bf16[2,4,128,768]{3,2,1,0:T(8,128)(2,1)}, u32[]{:S(2)}, u32[]{:S(2)}) collective-permute-start(bf16[2,4,128,768]{3,2,1,0:T(8,128)(2,1)} %pad_maximum_fusion.8), channel_id=1, source_target_pairs={{0,16},{8,24},{16,0},{24,8},{1,17},{9,25},{17,1},{25,9},{2,18},{10... | collective-permute-start | bytes 4718600 | tf_op jit(solution)/shard_map/ppermute | solution.py:246
  66.2 29.1 %collective-permute-start.9 = (bf16[4,128,1024]{2,1,0:T(8,128)(2,1)S(1)}, bf16[4,128,1024]{2,1,0:T(8,128)(2,1)S(1)}, u32[]{:S(2)}, u32[]{:S(2)}) collective-permute-start(bf16[4,128,1024]{2,1,0:T(8,128)(2,1)S(1)} %copy-done.9), channel_id=1, source_target_pairs={{0,1},{1,0},{2,3},{3,2},{4,5},{5,4},{6,7},{7,6},{8,9},{9,8},{10,11... | collective-permute-start | bytes 3145736 | tf_op jit(solution)/shard_map/ppermute | solution.py:292
  102.6 42.5 %collective-permute-start.12 = (bf16[2,4,128,896]{3,2,1,0:T(8,128)(2,1)}, bf16[2,4,128,896]{3,2,1,0:T(8,128)(2,1)}, u32[]{:S(2)}, u32[]{:S(2)}) collective-permute-start(bf16[2,4,128,896]{3,2,1,0:T(8,128)(2,1)} %pad_maximum_fusion.7), channel_id=1, source_target_pairs={{0,16},{8,24},{16,0},{24,8},{1,17},{9,25},{17,1},{25,9},{2,18},{10... | collective-permute-start | bytes 5505032 | tf_op jit(solution)/shard_map/ppermute | solution.py:246
  110.2 241.0 %reduce-scatter.3.cloned.1.call-start = ((), (), s32[]{:S(2)}) async-start(), calls=%async_computation.4 | async-start | bytes 6488064 | tf_op jit(solution)/shard_map/reduce_scatter | solution.py:286
  151.1 2.1 collective-permute-start.13
  157.9 2.9 collective-permute-start.14
  158.1 33.2 %collective-permute-start.18 = (bf16[512,1024]{1,0:T(8,128)(2,1)}, bf16[512,1024]{1,0:T(8,128)(2,1)}, u32[]{:S(2)}, u32[]{:S(2)}) collective-permute-start(bf16[512,1024]{1,0:T(8,128)(2,1)} %bitcast.22), channel_id=1, source_target_pairs={{0,8},{8,0},{16,24},{24,16},{1,9},{9,1},{17,25},{25,17},{2,10},{10... | collective-permute-start | bytes 3145736 | tf_op jit(solution)/shard_map/ppermute | solution.py:243
  165.0 18.3 %collective-permute-start.15 = (bf16[512,1024]{1,0:T(8,128)(2,1)}, bf16[512,1024]{1,0:T(8,128)(2,1)}, u32[]{:S(2)}, u32[]{:S(2)}) collective-permute-start(bf16[512,1024]{1,0:T(8,128)(2,1)} %multiply_convert_fusion.4), channel_id=1, source_target_pairs={{0,8},{8,0},{16,24},{24,16},{1,9},{9,1},{17,25},{25,17},{2,10},{10... | collective-permute-start | bytes 3145736 | tf_op jit(solution)/shard_map/ppermute | solution.py:243
  167.7 21.6 %collective-permute-start.16 = (bf16[1408,512]{1,0:T(8,128)(2,1)}, bf16[1408,512]{1,0:T(8,128)(2,1)}, u32[]{:S(2)}, u32[]{:S(2)}) collective-permute-start(bf16[1408,512]{1,0:T(8,128)(2,1)} %constant_dynamic-slice_fusion.4), channel_id=1, source_target_pairs={{0,8},{8,0},{16,24},{24,16},{1,9},{9,1},{17,25},{25,17},{2,10},{10... | collective-permute-start | bytes 4325384 | tf_op jit(solution)/shard_map/ppermute | solution.py:243
  230.2 193.1 %reduce-scatter.5.cloned.1.call-start = ((), (), s32[]{:S(2)}) async-start(), calls=%async_computation.5 | async-start | bytes 2654208 | tf_op jit(solution)/shard_map/reduce_scatter | solution.py:286
  238.1 9.4 %collective-permute-start.19 = (bf16[512,1024]{1,0:T(8,128)(2,1)S(1)}, bf16[512,1024]{1,0:T(8,128)(2,1)S(1)}, u32[]{:S(2)}, u32[]{:S(2)}) collective-permute-start(bf16[512,1024]{1,0:T(8,128)(2,1)S(1)} %slice.363), channel_id=1, source_target_pairs={{0,8},{8,0},{16,24},{24,16},{1,9},{9,1},{17,25},{25,17},{2,10},{10... | collective-permute-start | bytes 3145736 | tf_op jit(solution)/shard_map/ppermute | solution.py:243
  241.8 6.5 %collective-permute-start.17 = (bf16[512,1024]{1,0:T(8,128)(2,1)S(1)}, bf16[512,1024]{1,0:T(8,128)(2,1)S(1)}, u32[]{:S(2)}, u32[]{:S(2)}) collective-permute-start(bf16[512,1024]{1,0:T(8,128)(2,1)S(1)} %slice.364), channel_id=1, source_target_pairs={{0,8},{8,0},{16,24},{24,16},{1,9},{9,1},{17,25},{25,17},{2,10},{10... | collective-permute-start | bytes 3145736 | tf_op jit(solution)/shard_map/ppermute | solution.py:243
  247.3 5.5 %collective-permute-start.20 = (bf16[1408,512]{1,0:T(8,128)(2,1)S(1)}, bf16[1408,512]{1,0:T(8,128)(2,1)S(1)}, u32[]{:S(2)}, u32[]{:S(2)}) collective-permute-start(bf16[1408,512]{1,0:T(8,128)(2,1)S(1)} %constant_dynamic-slice_fusion.3), channel_id=1, source_target_pairs={{0,8},{8,0},{16,24},{24,16},{1,9},{9,1},{17,25},{25,17},{2,10},{10... | collective-permute-start | bytes 4325384 | tf_op jit(solution)/shard_map/ppermute | solution.py:243
  252.2 4.1 collective-permute-start.22
  254.9 62.5 %collective-permute-start.21 = (bf16[2816,256]{1,0:T(8,128)(2,1)}, bf16[2816,256]{1,0:T(8,128)(2,1)}, u32[]{:S(2)}, u32[]{:S(2)}) collective-permute-start(bf16[2816,256]{1,0:T(8,128)(2,1)} %get-tuple-element.122), channel_id=1, source_target_pairs={{0,16},{8,24},{16,0},{24,8},{1,17},{9,25},{17,1},{25,9},{2,18},{10... | collective-permute-start | bytes 4325384 | tf_op jit(solution)/shard_map/ppermute | solution.py:246
  257.7 48.5 %collective-permute-start.23 = (bf16[512,512]{1,0:T(8,128)(2,1)S(1)}, bf16[512,512]{1,0:T(8,128)(2,1)}, u32[]{:S(2)}, u32[]{:S(2)}) collective-permute-start(bf16[512,512]{1,0:T(8,128)(2,1)S(1)} %constant_dynamic-slice_fusion.2), channel_id=1, source_target_pairs={{0,8},{8,0},{16,24},{24,16},{1,9},{9,1},{17,25},{25,17},{2,10},{10... | collective-permute-start | bytes 1572872 | tf_op jit(solution)/shard_map/ppermute | solution.py:243
  301.5 14.9 %collective-permute-start.27 = (bf16[1024,256]{1,0:T(8,128)(2,1)S(1)}, bf16[1024,256]{1,0:T(8,128)(2,1)S(1)}, u32[]{:S(2)}, u32[]{:S(2)}) collective-permute-start(bf16[1024,256]{1,0:T(8,128)(2,1)S(1)} %constant_dynamic-slice_fusion), channel_id=1, source_target_pairs={{0,16},{8,24},{16,0},{24,8},{1,17},{9,25},{17,1},{25,9},{2,18},{10... | collective-permute-start | bytes 1572872 | tf_op jit(solution)/shard_map/ppermute | solution.py:246
  307.7 19.3 %collective-permute-start.24 = (bf16[1024,256]{1,0:T(8,128)(2,1)S(1)}, bf16[1024,256]{1,0:T(8,128)(2,1)S(1)}, u32[]{:S(2)}, u32[]{:S(2)}) collective-permute-start(bf16[1024,256]{1,0:T(8,128)(2,1)S(1)} %get-tuple-element.139), channel_id=1, source_target_pairs={{0,16},{8,24},{16,0},{24,8},{1,17},{9,25},{17,1},{25,9},{2,18},{10... | collective-permute-start | bytes 1572872 | tf_op jit(solution)/shard_map/ppermute | solution.py:246
  328.6 18.8 %collective-permute-start.25 = (bf16[512,1024]{1,0:T(8,128)(2,1)S(1)}, bf16[512,1024]{1,0:T(8,128)(2,1)S(1)}, u32[]{:S(2)}, u32[]{:S(2)}) collective-permute-start(bf16[512,1024]{1,0:T(8,128)(2,1)S(1)} %slice.362), channel_id=1, source_target_pairs={{0,8},{8,0},{16,24},{24,16},{1,9},{9,1},{17,25},{25,17},{2,10},{10... | collective-permute-start | bytes 3145736 | tf_op jit(solution)/shard_map/ppermute | solution.py:243
  332.9 13.5 %collective-permute-start.26 = (bf16[1024,256]{1,0:T(8,128)(2,1)S(1)}, bf16[1024,256]{1,0:T(8,128)(2,1)S(1)}, u32[]{:S(2)}, u32[]{:S(2)}) collective-permute-start(bf16[1024,256]{1,0:T(8,128)(2,1)S(1)} %constant_dynamic-slice_fusion.1), channel_id=1, source_target_pairs={{0,16},{8,24},{16,0},{24,8},{1,17},{9,25},{17,1},{25,9},{2,18},{10... | collective-permute-start | bytes 1572872 | tf_op jit(solution)/shard_map/ppermute | solution.py:246
  352.4 2.1 collective-permute-start.38
  352.6 18.6 %collective-permute-start.36 = (bf16[128,2816]{1,0:T(8,128)(2,1)}, bf16[128,2816]{1,0:T(8,128)(2,1)S(1)}, u32[]{:S(2)}, u32[]{:S(2)}) collective-permute-start(bf16[128,2816]{1,0:T(8,128)(2,1)} %reduce-scatter.3.cloned.1.call-done), channel_id=1, source_target_pairs={{0,16},{8,24},{16,0},{24,8},{1,17},{9,25},{17,1},{25,9},{2,18},{10... | collective-permute-start | bytes 2162696 | tf_op jit(solution)/shard_map/ppermute | solution.py:246
  355.7 31.0 %collective-permute-start.30 = (bf16[4,480,256]{2,1,0:T(8,128)(2,1)}, bf16[4,480,256]{2,1,0:T(8,128)(2,1)S(1)}, u32[]{:S(2)}, u32[]{:S(2)}) collective-permute-start(bf16[4,480,256]{2,1,0:T(8,128)(2,1)} %get-tuple-element.93), channel_id=1, source_target_pairs={{0,1},{1,0},{2,3},{3,2},{4,5},{5,4},{6,7},{7,6},{8,9},{9,8},{10,11... | collective-permute-start | bytes 2949128 | tf_op jit(solution)/shard_map/ppermute | solution.py:292
  356.4 36.2 %copy-start.6 = (f32[1024,1024]{1,0:T(8,128)S(1)}, f32[1024,1024]{1,0:T(8,128)}, u32[]{:S(2)}) copy-start(f32[1024,1024]{1,0:T(8,128)} %copy-done.5) | copy-start | bytes 12582916
  371.2 21.5 %copy-start.10 = (f32[512,1024]{1,0:T(8,128)S(1)}, f32[512,1024]{1,0:T(8,128)}, u32[]{:S(2)}) copy-start(f32[512,1024]{1,0:T(8,128)} %get-tuple-element.112) | copy-start | bytes 6291460
  372.7 44.5 %collective-permute-start.37 = (bf16[128,2816]{1,0:T(8,128)(2,1)S(1)}, bf16[128,2816]{1,0:T(8,128)(2,1)S(1)}, u32[]{:S(2)}, u32[]{:S(2)}) collective-permute-start(bf16[128,2816]{1,0:T(8,128)(2,1)S(1)} %add_convert_fusion.2), channel_id=1, source_target_pairs={{0,8},{8,0},{16,24},{24,16},{1,9},{9,1},{17,25},{25,17},{2,10},{10... | collective-permute-start | bytes 2162696 | tf_op jit(solution)/shard_map/ppermute | solution.py:243
  387.1 9.1 %collective-permute-start.33 = (bf16[480,256]{1,0:T(8,128)(2,1)S(1)}, bf16[480,256]{1,0:T(8,128)(2,1)S(1)}, u32[]{:S(2)}, u32[]{:S(2)}) collective-permute-start(bf16[480,256]{1,0:T(8,128)(2,1)S(1)} %get-tuple-element.146), channel_id=1, source_target_pairs={{0,6},{1,7},{2,0},{3,1},{4,2},{5,3},{6,4},{7,5},{8,14},{9,15},{10,... | collective-permute-start | bytes 737288 | tf_op jit(solution)/shard_map/ppermute | solution.py:295
  389.8 27.2 %collective-permute-start.32 = (bf16[480,256]{1,0:T(8,128)(2,1)S(1)}, bf16[480,256]{1,0:T(8,128)(2,1)S(1)}, u32[]{:S(2)}, u32[]{:S(2)}) collective-permute-start(bf16[480,256]{1,0:T(8,128)(2,1)S(1)} %get-tuple-element.147), channel_id=1, source_target_pairs={{0,4},{1,5},{2,6},{3,7},{4,0},{5,1},{6,2},{7,3},{8,12},{9,13},{10,... | collective-permute-start | bytes 737288 | tf_op jit(solution)/shard_map/ppermute | solution.py:295
  391.2 25.8 %collective-permute-start.31 = (bf16[480,256]{1,0:T(8,128)(2,1)S(1)}, bf16[480,256]{1,0:T(8,128)(2,1)S(1)}, u32[]{:S(2)}, u32[]{:S(2)}) collective-permute-start(bf16[480,256]{1,0:T(8,128)(2,1)S(1)} %get-tuple-element.145), channel_id=1, source_target_pairs={{0,2},{1,3},{2,4},{3,5},{4,6},{5,7},{6,0},{7,1},{8,10},{9,11},{10,... | collective-permute-start | bytes 737288 | tf_op jit(solution)/shard_map/ppermute | solution.py:295
  417.1 7.3 %collective-permute-start.34 = (bf16[480,256]{1,0:T(8,128)(2,1)S(1)}, bf16[480,256]{1,0:T(8,128)(2,1)S(1)}, u32[]{:S(2)}, u32[]{:S(2)}) collective-permute-start(bf16[480,256]{1,0:T(8,128)(2,1)S(1)} %fusion.33), channel_id=1, source_target_pairs={{0,16},{8,24},{16,0},{24,8},{1,17},{9,25},{17,1},{25,9},{2,18},{10... | collective-permute-start | bytes 737288 | tf_op jit(solution)/shard_map/ppermute | solution.py:246
  423.3 7.8 %collective-permute-start.28 = (bf16[128,1152]{1,0:T(8,128)(2,1)}, bf16[128,1152]{1,0:T(8,128)(2,1)S(1)}, u32[]{:S(2)}, u32[]{:S(2)}) collective-permute-start(bf16[128,1152]{1,0:T(8,128)(2,1)} %reduce-scatter.5.cloned.1.call-done), channel_id=1, source_target_pairs={{0,16},{8,24},{16,0},{24,8},{1,17},{9,25},{17,1},{25,9},{2,18},{10... | collective-permute-start | bytes 884744 | tf_op jit(solution)/shard_map/ppermute | solution.py:246
  424.6 8.6 %collective-permute-start.35 = (bf16[480,512]{1,0:T(8,128)(2,1)S(1)}, bf16[480,512]{1,0:T(8,128)(2,1)S(1)}, u32[]{:S(2)}, u32[]{:S(2)}) collective-permute-start(bf16[480,512]{1,0:T(8,128)(2,1)S(1)} %pad_maximum_fusion.18), channel_id=1, source_target_pairs={{0,8},{8,0},{16,24},{24,16},{1,9},{9,1},{17,25},{25,17},{2,10},{10... | collective-permute-start | bytes 1474568 | tf_op jit(solution)/shard_map/ppermute | solution.py:243
  433.0 2.4 collective-permute-start.29
  (39 other events, 242.3 us)
Sparse Core Ops, SparseCore 0:
  58.5 66.6 all-gather.4
  127.4 55.8 all-gather.2
  230.3 109.2 reduce-scatter.2
  351.4 71.8 reduce-scatter.4

commit v4 on v3

--- a/solution.py
+++ b/solution.py
@@ -319,7 +319,12 @@
     by_ring, tie = chips == 2 and fsdp <= 8, lax.optimization_barrier
     shard_a = jnp.concatenate([gains] + [cols(w, core) for w in (w_query, w_key, w_value)], axis=1)
     shard_b = jnp.concatenate([cols(w_output, core), cols(w_gate, core)], axis=1)
-    shard_c, shard_d = cols(w_up, core), cols(w_down, core)
+    height, down_height = w_query.shape[0], w_down.shape[0]
+    blocks = -(-down_height // height)
+    shard_d = jnp.pad(cols(w_down, core), ((0, blocks * height - down_height), (0, 0)))
+    shard_c = jnp.concatenate(
+        [cols(w_up, core)] + [shard_d[k * height : (k + 1) * height] for k in range(blocks)], axis=1
+    )
     if by_ring:
         join = functools.partial(joined, side, chip)
         pieces_a = ring_pieces(held_columns(shard_a))
@@ -327,7 +332,7 @@
         pieces_b = ring_pieces(held_b)
         mine_a = in_ring_order(place, pieces_a)
         far_a = sides(mine_a)
-        pieces_b, far_a, mine_a, shard_c, shard_d = tie((pieces_b, far_a, mine_a, shard_c, shard_d))
+        pieces_b, far_a, mine_a, shard_c = tie((pieces_b, far_a, mine_a, shard_c))
         mine_b = in_ring_order(place, pieces_b)
         halves_a = swapped_halves(shard_a, mine_a, far_a)
         mine_b, halves_a = tie((mine_b, halves_a))
@@ -339,7 +344,8 @@
         whole_a = join(mine_a, far_a, other_a)
     else:
         whole_a = gather(shard_a)
-    up_mat, whole_d = gather(shard_c), gather(shard_d)
+    whole_c = gather(shard_c)
+    up_mat, whole_d = whole_c[:, : w_up.shape[1] // 2], whole_c[:, w_up.shape[1] // 2 :]
     qkv_mat = whole_a[:, gains.shape[1] :]
     gain_rows = whole_a[:, : gains.shape[1]].reshape(fsdp, w_query.shape[0], -1)
     gain_one = gain_rows[:, 0, : attn_gain.shape[0]].reshape(1, width).astype(f32)
@@ -372,7 +378,14 @@
     normed_two = pair((mixed * inverse_two * gain_two).astype(bf16))
     gate = dot_nn(normed_two, gate_mat)
     up_val = dot_nn(normed_two, up_mat)
-    down_mat = rows_from_cols(whole_d)
+
+    def unpacked(packed):
+        stacked = jnp.concatenate(
+            [packed[:, k * hw : (k + 1) * hw].reshape(-1, height, hw) for k in range(blocks)], axis=1
+        )
+        return stacked[:, :down_height].reshape(-1, hw)
+
+    down_mat = in_order(unpacked(rows(whole_d, core)), unpacked(swap(rows(whole_d, 1 - core))), 1)
     sigma = jax.nn.sigmoid(gate)
     silu_gate = gate * sigma
     act = (silu_gate * up_val).astype(bf16)
@@ -398,14 +411,6 @@
     grad_attended = dot_nt(grad_attn, output_mat).astype(bf16)
     grad_out_w = chip_parts(grad_out_w)
     dq, dk, dv = attend_back(starts, cosine, sine, q_rot, k_rot, blended, grad_attended, length)
-    grad_down, grad_out_w, dq = tie((grad_down, grad_out_w, dq))
-    grad_do = jnp.concatenate(
-        [added(parts).reshape(fsdp, -1, hw // chips) for parts in (grad_down, grad_out_w)], axis=1
-    )
-    if by_ring:
-        grad_do = grad_do.reshape(ring, 2, *grad_do.shape[1:])
-        at_side = lambda which: lax.dynamic_slice_in_dim(grad_do, which, 1, 1)[:, 0]
-        do_mine, do_far = at_side(side), at_side(1 - side)
     grad_normed = mine_and_partner(
         dot_nt(dq, qkv_mat[:, :hw]) + dot_nt(dk, qkv_mat[:, hw : 2 * hw])
         + dot_nt(dv, qkv_mat[:, 2 * hw :])
@@ -435,9 +440,14 @@
     grad_q, grad_k = (chip_parts(dot_tn(normed, d).astype(bf16)) for d in (dq, dk))
     grad_v = dot_tn(normed, dv).astype(bf16)
     grad_a = jnp.concatenate([added(grad_q), added(grad_k), grad_v, extra], axis=1)
+    grad_a, grad_b, grad_down, grad_out_w = tie((grad_a, grad_b, grad_down, grad_out_w))
+    grad_do = jnp.concatenate(
+        [added(parts).reshape(fsdp, -1, hw // chips) for parts in (grad_down, grad_out_w)], axis=1
+    )
     if by_ring:
-        grad_a, grad_b, do_mine, do_far = tie((grad_a, grad_b, do_mine, do_far))
-        grad_do = added([do_mine, sides(do_far)])
+        grad_do = grad_do.reshape(ring, 2, *grad_do.shape[1:])
+        at_side = lambda which: lax.dynamic_slice_in_dim(grad_do, which, 1, 1)[:, 0]
+        grad_do = added([at_side(side), sides(at_side(1 - side))])
         at_place = lambda step: lax.dynamic_slice_in_dim(grad_do, (place + step) % ring, 1, 0)[0]
         grad_do = added([at_place(0)] + [around(at_place(step), step) for step in range(1, ring)])
     else:

time: 455 us -> 436 us (0.958)
  waiting for transfers between devices: 155 us -> 139 us
  starting transfers between devices: 35.6 us -> 42.1 us
    ppermute x9, waiting for transfers between devices: 51 us -> 36.2 us  [to_chip(): lax.ppermute(values, 'dp', [(i, (i + 2 * step) % dp) for i in range(dp)])]
    all_gather x2 -> x1, waiting for transfers between devices: 9.13 us -> 0.01 us  [gather(): return lax.all_gather(shard, 'fsdp', axis=0, tiled=True)]
    reduce_scatter x2, waiting for transfers between devices: 3.59 us -> 11.9 us  [scatter(): return lax.psum_scatter(whole, 'fsdp', scatter_dimension=0, tiled=True)]
  transfers between devices with their start and end apart: 43 -> 42, of which waited for: 19 -> 17; matrix products, arithmetic and copies ran while one was open for 27% -> 28% of each run, Pallas kernels for 15% -> 16%
where the time goes in v4:
time: 436 us; the launch traced here: 428 us
  waiting for transfers between devices  139 us (32%)
  matrix products  82.3 us (19%)
  Pallas kernels  69.8 us (16%)
  other arithmetic  58.6 us (13%)
  starting transfers between devices  42.1 us (10%)
  local copies, waits for them, and re-layouts  21.3 us (5%)
  between operations  15.4 us (4%)
    ppermute x3, waiting for transfers between devices, sides(): return lax.ppermute(values, 'fsdp', [(i, i ^ 1) for i in range(fsdp)])  44.6 us
    ppermute x9, waiting for transfers between devices, around(): lax.ppermute(values, 'fsdp', [(i, (i + 2 * step) % fsdp) for i in range(f...  43.8 us
    ppermute x9, waiting for transfers between devices, to_chip(): lax.ppermute(values, 'dp', [(i, (i + 2 * step) % dp) for i in range(dp)])  36.2 us
    pallas_call x1, Pallas kernels, attend_back(): pl.pallas_call(attend_back_kernel, grid=(tokens // length, width // LANES...  35.3 us
    dot_general x7, matrix products, dot_tn(): lax.dot_general(a, b, (((0,), (0,)), ((), ())), preferred_element_type=f32)  29.3 us
    dot_general x5, matrix products, dot_nn(): return jnp.dot(a, b, preferred_element_type=f32)  28.1 us
    dot_general x7, matrix products, dot_nt(): lax.dot_general(a, b, (((1,), (1,)), ((), ())), preferred_element_type=f32)  24.9 us
    ppermute x9, starting transfers between devices, around(): lax.ppermute(values, 'fsdp', [(i, (i + 2 * step) % fsdp) for i in range(f...  23.2 us
  transfers between devices with their start and end apart: 42, of which 17 were waited for; matrix products, arithmetic and copies ran while one was open for 28% of the time, Pallas kernels for 16%

profile of v4, /device:TPU:0, one launch (start us, length us, event | category | flops | bytes accessed | tf_op | source)
XLA Modules:
  0.0 428.1 jit_solution(4049868107857885835)
XLA Ops:
  10.1 3.1 collective-permute-start.2
  13.2 2.6 collective-permute-start.3
  18.4 3.5 collective-permute-done.2.refs_1_
  21.9 9.0 %collective-permute-done.3.refs_2_ = bf16[128,896]{1,0:T(8,128)(2,1)S(1)} collective-permute-done((bf16[128,896]{1,0:T(8,128)(2,1)S(1)}, bf16[128,896]{1,0:T(8,128)(2,1)S(1)}, u32[]{:S(2)}, u32[]{:S(2)}) %collective-permute-start.3) | collective-permute-done | bytes 229408 | tf_op jit(solution)/shard_map/ppermute | solution.py:295
  31.6 2.3 ring_order.2.mine_ref
  37.4 5.4 %collective-permute-start.5 = (bf16[128,1024]{1,0:T(8,128)(2,1)S(1)}, bf16[128,1024]{1,0:T(8,128)(2,1)S(1)}, u32[]{:S(2)}, u32[]{:S(2)}) collective-permute-start(bf16[128,1024]{1,0:T(8,128)(2,1)S(1)} %pad_maximum_fusion.24.refs_0_), channel_id=1, source_target_pairs={{0,2},{1,3},{2,4},{3,5},{4,6},{5,7},{6,0},{7,1},{8,10},{9,11},{10,... | collective-permute-start | bytes 786440 | tf_op jit(solution)/shard_map/ppermute | solution.py:295
  46.2 5.0 %collective-permute-done.5.refs_1_ = bf16[128,1024]{1,0:T(8,128)(2,1)S(1)} collective-permute-done((bf16[128,1024]{1,0:T(8,128)(2,1)S(1)}, bf16[128,1024]{1,0:T(8,128)(2,1)S(1)}, u32[]{:S(2)}, u32[]{:S(2)}) %collective-permute-start.5) | collective-permute-done | bytes 262176 | tf_op jit(solution)/shard_map/ppermute | solution.py:295
  51.2 9.2 %collective-permute-done.6.refs_2_ = bf16[128,1024]{1,0:T(8,128)(2,1)S(1)} collective-permute-done((bf16[128,1024]{1,0:T(8,128)(2,1)S(1)}, bf16[128,1024]{1,0:T(8,128)(2,1)S(1)}, u32[]{:S(2)}, u32[]{:S(2)}) %collective-permute-start.6) | collective-permute-done | bytes 262176 | tf_op jit(solution)/shard_map/ppermute | solution.py:295
  62.4 2.3 ring_order.3.mine_ref
  71.3 30.3 %collective-permute-done.9.far_ref = bf16[4,128,1024]{2,1,0:T(8,128)(2,1)S(1)} collective-permute-done((bf16[4,128,1024]{2,1,0:T(8,128)(2,1)S(1)}, bf16[4,128,1024]{2,1,0:T(8,128)(2,1)S(1)}, u32[]{:S(2)}, u32[]{:S(2)}) %collective-permute-start.9) | collective-permute-done | bytes 1048608 | tf_op jit(solution)/shard_map/ppermute | solution.py:292
  106.2 3.0 fusion.36
  110.3 2.2 multiply_reduce_fusion
  112.5 4.0 joined.2
  117.5 8.7 %fusion.2.q_ref.k_ref.v_ref = f32[1024,1536]{1,0:T(8,128)} fusion(bf16[1024,1664]{1,0:T(8,128)(2,1)} %bitcast.91, f32[1024]{0:T(1024)S(1)} %bitcast.114, f32[1024]{0:T(1024)S(1)} %add_rsqrt_fusion, bf16[512,1024]{1,0:T(8,128)(2,1)} %collective-permute-done, bf16[512,1024]{1,0:T(8,128)(2,1)} %bitcast), kind=kOutput, calls=%fused_computation.18 | convolution fusion | flops 3228565504 | bytes 11542528 | tf_op jit(solution)/shard_map/dot_general | solution.py:66
  126.2 21.1 %attend.1 = (bf16[1024,512]{1,0:T(8,128)(2,1)}, bf16[1024,512]{1,0:T(8,128)(2,1)}, bf16[1024,512]{1,0:T(8,128)(2,1)}, bf16[1024,512]{1,0:T(8,128)(2,1)}) custom-call(s32[1024,1]{1,0:T(8,128)} %copy.41.start_ref, f32[1024,128]{1,0:T(8,128)} %get-tuple-element.159.cos_ref, f32[1024,128]{1,0:T(8,128)} %get-tuple-element.158.sin_ref, ...), custom_call_target="tpu_custom_call" | custom-call | tf_op jit(solution)/shard_map/attend/pallas_call | solution.py:145
  147.3 4.7 %joined.3 = bf16[4,2,128,1920]{3,2,1,0:T(8,128)(2,1)} custom-call(s32[2]{0:T(128)} %pad_add_fusion.2.at_ref, bf16[4,128,1024]{2,1,0:T(8,128)(2,1)} %ring_order.3.mine_ref, bf16[4,128,1024]{2,1,0:T(8,128)(2,1)} %copy-done.18, bf16[2,4,128,896]{3,2,1,0:T(8,128)(2,1)} %collective-permute-done.12.other_ref), custom_call_target="tpu_custom_call" | custom-call | tf_op jit(solution)/shard_map/joined/pallas_call | solution.py:208
  157.0 2.0 copy-done.7
  159.8 2.1 maximum_convert_fusion
  162.6 2.5 multiply_reduce_fusion.7
  166.4 2.1 slice.286
  173.5 5.9 %fusion.6 = f32[1024,1408]{1,0:T(8,128)S(1)} fusion(bf16[1024,2944]{1,0:T(8,128)(2,1)} %all-gather.2.cloned.1.call-done, bf16[512,1024]{1,0:T(8,128)(2,1)} %collective-permute-done.15, bf16[512,1024]{1,0:T(8,128)(2,1)} %multiply_convert_fusion.4), kind=kOutput, calls=%fused_computation.24 | convolution fusion | flops 2956984320 | bytes 10747904 | tf_op jit(solution)/shard_map/dot_general | solution.py:66
  182.1 5.1 %fusion.20 = f32[1024,1408]{1,0:T(8,128)S(1)} fusion(bf16[1408,512]{1,0:T(8,128)(2,1)S(1)} %bitcast.108, bf16[1408,512]{1,0:T(8,128)(2,1)S(1)} %bitcast.106, bf16[512,1024]{1,0:T(8,128)(2,1)} %collective-permute-done.18, bf16[512,1024]{1,0:T(8,128)(2,1)} %bitcast.30), kind=kOutput, calls=%fused_computation.65 | convolution fusion | flops 2962751488 | bytes 10747904 | tf_op jit(solution)/shard_map/dot_general | solution.py:58
  187.3 8.9 %multiply_convert_fusion.1 = (bf16[1024,1408]{1,0:T(8,128)(2,1)}, bf16[1024,1408]{1,0:T(8,128)(2,1)S(1)}, bf16[1024,1408]{1,0:T(8,128)(2,1)}) fusion(f32[1024,1408]{1,0:T(8,128)S(1)} %fusion.20, f32[1024,1408]{1,0:T(8,128)S(1)} %fusion.6, bf16[1024,1920]{1,0:T(8,128)(2,1)S(1)} %bitcast.97, bf16[512,1024]{1,0:T(8,128)(2,1)} %collective-permute-done.15, ...), kind=kOutput, calls=%fused_computation.2 | convolution fusion | flops 2978611200 | bytes 25165824 | tf_op jit(solution)/shard_map/dot_general | solution.py:66
  196.1 6.5 %convolution_convert_fusion.1 = bf16[1024,1408]{1,0:T(8,128)(2,1)S(1)} fusion(bf16[1024,1408]{1,0:T(8,128)(2,1)S(1)} %get-tuple-element.72, bf16[512,1024]{1,0:T(8,128)(2,1)} %collective-permute-done.15, bf16[512,1024]{1,0:T(8,128)(2,1)} %multiply_convert_fusion.4), kind=kOutput, calls=%fused_computation.12 | convolution fusion | flops 2958426112 | bytes 7864320 | tf_op jit(solution)/shard_map/dot_general | solution.py:62
  202.6 5.3 %convolution_convert_fusion.2 = bf16[1024,1408]{1,0:T(8,128)(2,1)S(1)} fusion(bf16[1024,1408]{1,0:T(8,128)(2,1)S(1)} %copy-done.54, bf16[512,1024]{1,0:T(8,128)(2,1)} %collective-permute-done.15, bf16[512,1024]{1,0:T(8,128)(2,1)} %multiply_convert_fusion.4), kind=kOutput, calls=%fused_computation.13 | convolution fusion | flops 2958426112 | bytes 7864320 | tf_op jit(solution)/shard_map/dot_general | solution.py:62
  208.0 2.9 pad_maximum_fusion
  211.1 6.3 %fusion.8 = f32[1024,1024]{1,0:T(8,128)S(1)} fusion(bf16[1024,1408]{1,0:T(8,128)(2,1)} %get-tuple-element.71, bf16[1024,1920]{1,0:T(8,128)(2,1)} %bitcast.96), kind=kOutput, calls=%fused_computation.26 | convolution fusion | flops 2952790016 | bytes 9961472 | tf_op jit(solution)/shard_map/dot_general | solution.py:58
  217.4 5.4 %fusion.17 = f32[1024,1024]{1,0:T(8,128)S(1)} fusion(f32[1024,1024]{1,0:T(8,128)S(1)} %fusion.8, bf16[1024,1408]{1,0:T(8,128)(2,1)S(1)} %copy-done.53, bf16[1024,2944]{1,0:T(8,128)(2,1)} %all-gather.2.cloned.1.call-done), kind=kOutput, calls=%fused_computation.64 | convolution fusion | flops 2953838592 | bytes 14155776 | tf_op jit(solution)/shard_map/dot_general | solution.py:58
  223.5 3.4 fusion.21
  227.3 4.8 %convolution_convert_fusion = bf16[1408,1024]{1,0:T(8,128)(2,1)S(1)} fusion(bf16[1024,1408]{1,0:T(8,128)(2,1)S(1)} %copy-done.51, bf16[512,1024]{1,0:T(8,128)(2,1)} %collective-permute-done.18, bf16[512,1024]{1,0:T(8,128)(2,1)} %bitcast.30), kind=kOutput, calls=%fused_computation.11 | convolution fusion | flops 2958426112 | bytes 7864320 | tf_op jit(solution)/shard_map/dot_general | solution.py:62
  233.5 3.9 fusion.64
  240.7 2.5 convolution_convert_fusion.7.grad_ref
  243.2 35.3 %attend_back.1 = (bf16[1024,512]{1,0:T(8,128)(2,1)}, bf16[1024,512]{1,0:T(8,128)(2,1)}, bf16[1024,512]{1,0:T(8,128)(2,1)}) custom-call(s32[1024,1]{1,0:T(8,128)} %copy.41.start_ref, f32[1024,128]{1,0:T(8,128)} %get-tuple-element.159.cos_ref, f32[1024,128]{1,0:T(8,128)} %get-tuple-element.158.sin_ref, bf16[1024,512]{1,0:T(8,128)(2,1)} %get-tuple-element.73.q_rot_ref, ...), custom_call_target="tpu_custom_call" | custom-call | tf_op jit(solution)/shard_map/attend_back/pallas_call | solution.py:159
  279.6 3.0 fusion.28
  285.5 4.3 %convolution_convert_fusion.5 = bf16[1024,512]{1,0:T(8,128)(2,1)S(1)} fusion(bf16[1024,512]{1,0:T(8,128)(2,1)S(1)} %copy-done.50, f32[1024]{0:T(1024)S(1)} %bitcast.115, f32[1024]{0:T(1024)S(1)} %add_rsqrt_fusion, bf16[512,1024]{1,0:T(8,128)(2,1)} %collective-permute-done, bf16[512,1024]{1,0:T(8,128)(2,1)} %bitcast), kind=kOutput, calls=%fused_computation.71 | convolution fusion | flops 1081606144 | bytes 4202496 | tf_op jit(solution)/shard_map/dot_general | solution.py:62
  293.0 2.9 convolution_convert_fusion.6
  297.0 4.2 convolution_convert_fusion.4
  302.5 2.3 collective-permute-done.23
  306.0 10.0 %collective-permute-done.22 = bf16[1024,256]{1,0:T(8,128)(2,1)S(1)} collective-permute-done((bf16[1024,256]{1,0:T(8,128)(2,1)S(1)}, bf16[1024,256]{1,0:T(8,128)(2,1)S(1)}, u32[]{:S(2)}, u32[]{:S(2)}) %collective-permute-start.22) | collective-permute-done | bytes 524320 | tf_op jit(solution)/shard_map/ppermute | solution.py:246
  318.9 2.9 fusion.12
  321.8 5.4 %collective-permute-done.27 = bf16[1024,256]{1,0:T(8,128)(2,1)} collective-permute-done((bf16[1024,256]{1,0:T(8,128)(2,1)}, bf16[1024,256]{1,0:T(8,128)(2,1)}, u32[]{:S(2)}, u32[]{:S(2)}) %collective-permute-start.27) | collective-permute-done | bytes 524320 | tf_op jit(solution)/shard_map/ppermute | solution.py:246
  334.1 11.4 %collective-permute-done.36 = bf16[128,2816]{1,0:T(8,128)(2,1)S(1)} collective-permute-done((bf16[128,2816]{1,0:T(8,128)(2,1)}, bf16[128,2816]{1,0:T(8,128)(2,1)S(1)}, u32[]{:S(2)}, u32[]{:S(2)}) %collective-permute-start.36) | collective-permute-done | bytes 720928 | tf_op jit(solution)/shard_map/ppermute | solution.py:246
  347.1 14.3 %collective-permute-done.30 = bf16[4,480,256]{2,1,0:T(8,128)(2,1)S(1)} collective-permute-done((bf16[4,480,256]{2,1,0:T(8,128)(2,1)S(1)}, bf16[4,480,256]{2,1,0:T(8,128)(2,1)S(1)}, u32[]{:S(2)}, u32[]{:S(2)}) %collective-permute-start.30) | collective-permute-done | bytes 983072 | tf_op jit(solution)/shard_map/ppermute | solution.py:292
  361.7 7.7 %collective-permute-start.33 = (bf16[480,256]{1,0:T(8,128)(2,1)S(1)}, bf16[480,256]{1,0:T(8,128)(2,1)S(1)}, u32[]{:S(2)}, u32[]{:S(2)}) collective-permute-start(bf16[480,256]{1,0:T(8,128)(2,1)S(1)} %get-tuple-element.142), channel_id=1, source_target_pairs={{0,6},{1,7},{2,0},{3,1},{4,2},{5,3},{6,4},{7,5},{8,14},{9,15},{10,... | collective-permute-start | bytes 737288 | tf_op jit(solution)/shard_map/ppermute | solution.py:295
  372.0 3.8 collective-permute-done.33
  375.8 13.3 %collective-permute-done.32 = bf16[480,256]{1,0:T(8,128)(2,1)S(1)} collective-permute-done((bf16[480,256]{1,0:T(8,128)(2,1)S(1)}, bf16[480,256]{1,0:T(8,128)(2,1)S(1)}, u32[]{:S(2)}, u32[]{:S(2)}) %collective-permute-start.32) | collective-permute-done | bytes 245792 | tf_op jit(solution)/shard_map/ppermute | solution.py:295
  393.7 11.9 %reduce-scatter.5.cloned.1.call-done = bf16[128,1152]{1,0:T(8,128)(2,1)} async-done(((bf16[1024,1152]{1,0:T(8,128)(2,1)}), bf16[128,1152]{1,0:T(8,128)(2,1)}) %reduce-scatter.5.cloned.1.call-update) | async-done | bytes 294928 | tf_op jit(solution)/shard_map/reduce_scatter | solution.py:286
  407.2 5.6 %collective-permute-done.28 = bf16[128,1152]{1,0:T(8,128)(2,1)S(1)} collective-permute-done((bf16[128,1152]{1,0:T(8,128)(2,1)}, bf16[128,1152]{1,0:T(8,128)(2,1)S(1)}, u32[]{:S(2)}, u32[]{:S(2)}) %collective-permute-start.28) | collective-permute-done | bytes 294944 | tf_op jit(solution)/shard_map/ppermute | solution.py:246
  (298 shorter events, 88.5 us)
Async XLA Ops:
  7.2 159.2 %all-gather.2.cloned.1.call-start = ((), (), s32[]{:S(2)}) async-start(), calls=%async_computation.2 | async-start | bytes 6782976 | tf_op jit(solution)/shard_map/all_gather | solution.py:283
  10.1 11.7 %collective-permute-start.2 = (bf16[128,896]{1,0:T(8,128)(2,1)S(1)}, bf16[128,896]{1,0:T(8,128)(2,1)S(1)}, u32[]{:S(2)}, u32[]{:S(2)}) collective-permute-start(bf16[128,896]{1,0:T(8,128)(2,1)S(1)} %pad_maximum_fusion.25.refs_0_), channel_id=1, source_target_pairs={{0,2},{1,3},{2,4},{3,5},{4,6},{5,7},{6,0},{7,1},{8,10},{9,11},{10,... | collective-permute-start | bytes 688136 | tf_op jit(solution)/shard_map/ppermute | solution.py:295
  13.2 17.6 %collective-permute-start.3 = (bf16[128,896]{1,0:T(8,128)(2,1)S(1)}, bf16[128,896]{1,0:T(8,128)(2,1)S(1)}, u32[]{:S(2)}, u32[]{:S(2)}) collective-permute-start(bf16[128,896]{1,0:T(8,128)(2,1)S(1)} %pad_maximum_fusion.25.refs_0_), channel_id=1, source_target_pairs={{0,4},{1,5},{2,6},{3,7},{4,0},{5,1},{6,2},{7,3},{8,12},{9,13},{10,... | collective-permute-start | bytes 688136 | tf_op jit(solution)/shard_map/ppermute | solution.py:295
  15.8 15.0 %collective-permute-start.4 = (bf16[128,896]{1,0:T(8,128)(2,1)S(1)}, bf16[128,896]{1,0:T(8,128)(2,1)S(1)}, u32[]{:S(2)}, u32[]{:S(2)}) collective-permute-start(bf16[128,896]{1,0:T(8,128)(2,1)S(1)} %pad_maximum_fusion.25.refs_0_), channel_id=1, source_target_pairs={{0,6},{1,7},{2,0},{3,1},{4,2},{5,3},{6,4},{7,5},{8,14},{9,15},{10,... | collective-permute-start | bytes 688136 | tf_op jit(solution)/shard_map/ppermute | solution.py:295
  18.4 27.8 %copy-start.38 = (bf16[128,1024]{1,0:T(8,128)(2,1)}, bf16[128,1024]{1,0:T(8,128)(2,1)S(1)}, u32[]{:S(2)}) copy-start(bf16[128,1024]{1,0:T(8,128)(2,1)S(1)} %pad_maximum_fusion.24.refs_0_) | copy-start | bytes 786436
  33.9 26.7 %copy-start.46 = (s32[1,512]{1,0:T(1,128)S(1)}, s32[1,512]{1,0:T(1,128)}, u32[]{:S(2)}) copy-start(s32[1,512]{1,0:T(1,128)} %param.16) | copy-start | bytes 6148
  33.9 27.5 %copy-start.15 = (bf16[1,512,1024]{2,1,0:T(8,128)(2,1)S(1)}, bf16[1,512,1024]{2,1,0:T(8,128)(2,1)}, u32[]{:S(2)}) copy-start(bf16[1,512,1024]{2,1,0:T(8,128)(2,1)} %param.15) | copy-start | bytes 3145732
  33.9 26.6 %collective-permute-start.8 = (bf16[4,128,896]{2,1,0:T(8,128)(2,1)}, bf16[4,128,896]{2,1,0:T(8,128)(2,1)S(1)}, u32[]{:S(2)}, u32[]{:S(2)}) collective-permute-start(bf16[4,128,896]{2,1,0:T(8,128)(2,1)} %ring_order.2.mine_ref), channel_id=1, source_target_pairs={{0,1},{1,0},{2,3},{3,2},{4,5},{5,4},{6,7},{7,6},{8,9},{9,8},{10,11... | collective-permute-start | bytes 2752520 | tf_op jit(solution)/shard_map/ppermute | solution.py:292
  37.4 13.8 %collective-permute-start.5 = (bf16[128,1024]{1,0:T(8,128)(2,1)S(1)}, bf16[128,1024]{1,0:T(8,128)(2,1)S(1)}, u32[]{:S(2)}, u32[]{:S(2)}) collective-permute-start(bf16[128,1024]{1,0:T(8,128)(2,1)S(1)} %pad_maximum_fusion.24.refs_0_), channel_id=1, source_target_pairs={{0,2},{1,3},{2,4},{3,5},{4,6},{5,7},{6,0},{7,1},{8,10},{9,11},{10,... | collective-permute-start | bytes 786440 | tf_op jit(solution)/shard_map/ppermute | solution.py:295
  42.8 17.6 %collective-permute-start.6 = (bf16[128,1024]{1,0:T(8,128)(2,1)S(1)}, bf16[128,1024]{1,0:T(8,128)(2,1)S(1)}, u32[]{:S(2)}, u32[]{:S(2)}) collective-permute-start(bf16[128,1024]{1,0:T(8,128)(2,1)S(1)} %pad_maximum_fusion.24.refs_0_), channel_id=1, source_target_pairs={{0,4},{1,5},{2,6},{3,7},{4,0},{5,1},{6,2},{7,3},{8,12},{9,13},{10,... | collective-permute-start | bytes 786440 | tf_op jit(solution)/shard_map/ppermute | solution.py:295
  44.5 16.0 %collective-permute-start.7 = (bf16[128,1024]{1,0:T(8,128)(2,1)S(1)}, bf16[128,1024]{1,0:T(8,128)(2,1)}, u32[]{:S(2)}, u32[]{:S(2)}) collective-permute-start(bf16[128,1024]{1,0:T(8,128)(2,1)S(1)} %pad_maximum_fusion.24.refs_0_), channel_id=1, source_target_pairs={{0,6},{1,7},{2,0},{3,1},{4,2},{5,3},{6,4},{7,5},{8,14},{9,15},{10,... | collective-permute-start | bytes 786440 | tf_op jit(solution)/shard_map/ppermute | solution.py:295
  60.5 266.7 %reduce-scatter.3.cloned.1.call-start = ((), (), s32[]{:S(2)}) async-start(), calls=%async_computation.3 | async-start | bytes 6488064 | tf_op jit(solution)/shard_map/reduce_scatter | solution.py:286
  60.6 7.7 %collective-permute-start.1 = (s32[1,512]{1,0:T(1,128)S(1)}, s32[1,512]{1,0:T(1,128)S(1)}, u32[]{:S(2)}, u32[]{:S(2)}) collective-permute-start(s32[1,512]{1,0:T(1,128)S(1)} %copy-done.46), channel_id=1, source_target_pairs={{0,8},{8,0},{16,24},{24,16},{1,9},{9,1},{17,25},{25,17},{2,10},{10... | collective-permute-start | bytes 6152 | tf_op jit(solution)/shard_map/ppermute | solution.py:243
  60.6 49.6 %collective-permute-start = (bf16[512,1024]{1,0:T(8,128)(2,1)}, bf16[512,1024]{1,0:T(8,128)(2,1)}, u32[]{:S(2)}, u32[]{:S(2)}) collective-permute-start(bf16[512,1024]{1,0:T(8,128)(2,1)} %bitcast), channel_id=1, source_target_pairs={{0,8},{8,0},{16,24},{24,16},{1,9},{9,1},{17,25},{25,17},{2,10},{10... | collective-permute-start | bytes 3145736 | tf_op jit(solution)/shard_map/ppermute | solution.py:243
  62.3 46.9 %collective-permute-start.11 = (bf16[512,512]{1,0:T(8,128)(2,1)}, bf16[512,512]{1,0:T(8,128)(2,1)S(1)}, u32[]{:S(2)}, u32[]{:S(2)}) collective-permute-start(bf16[512,512]{1,0:T(8,128)(2,1)} %get-tuple-element.138), channel_id=1, source_target_pairs={{0,8},{8,0},{16,24},{24,16},{1,9},{9,1},{17,25},{25,17},{2,10},{10... | collective-permute-start | bytes 1572872 | tf_op jit(solution)/shard_map/ppermute | solution.py:243
  66.2 37.0 %collective-permute-start.10 = (bf16[2,4,128,768]{3,2,1,0:T(8,128)(2,1)}, bf16[2,4,128,768]{3,2,1,0:T(8,128)(2,1)}, u32[]{:S(2)}, u32[]{:S(2)}) collective-permute-start(bf16[2,4,128,768]{3,2,1,0:T(8,128)(2,1)} %pad_maximum_fusion.8), channel_id=1, source_target_pairs={{0,16},{8,24},{16,0},{24,8},{1,17},{9,25},{17,1},{25,9},{2,18},{10... | collective-permute-start | bytes 4718600 | tf_op jit(solution)/shard_map/ppermute | solution.py:246
  68.3 33.3 %collective-permute-start.9 = (bf16[4,128,1024]{2,1,0:T(8,128)(2,1)S(1)}, bf16[4,128,1024]{2,1,0:T(8,128)(2,1)S(1)}, u32[]{:S(2)}, u32[]{:S(2)}) collective-permute-start(bf16[4,128,1024]{2,1,0:T(8,128)(2,1)S(1)} %copy-done.9), channel_id=1, source_target_pairs={{0,1},{1,0},{2,3},{3,2},{4,5},{5,4},{6,7},{7,6},{8,9},{9,8},{10,11... | collective-permute-start | bytes 3145736 | tf_op jit(solution)/shard_map/ppermute | solution.py:292
  104.7 42.7 %collective-permute-start.12 = (bf16[2,4,128,896]{3,2,1,0:T(8,128)(2,1)}, bf16[2,4,128,896]{3,2,1,0:T(8,128)(2,1)}, u32[]{:S(2)}, u32[]{:S(2)}) collective-permute-start(bf16[2,4,128,896]{3,2,1,0:T(8,128)(2,1)} %pad_maximum_fusion.7), channel_id=1, source_target_pairs={{0,16},{8,24},{16,0},{24,8},{1,17},{9,25},{17,1},{25,9},{2,18},{10... | collective-permute-start | bytes 5505032 | tf_op jit(solution)/shard_map/ppermute | solution.py:246
  153.5 2.0 collective-permute-start.13
  159.2 2.9 collective-permute-start.14
  159.4 21.2 %collective-permute-start.18 = (bf16[512,1024]{1,0:T(8,128)(2,1)}, bf16[512,1024]{1,0:T(8,128)(2,1)}, u32[]{:S(2)}, u32[]{:S(2)}) collective-permute-start(bf16[512,1024]{1,0:T(8,128)(2,1)} %bitcast.30), channel_id=1, source_target_pairs={{0,8},{8,0},{16,24},{24,16},{1,9},{9,1},{17,25},{25,17},{2,10},{10... | collective-permute-start | bytes 3145736 | tf_op jit(solution)/shard_map/ppermute | solution.py:243
  166.3 7.2 %collective-permute-start.15 = (bf16[512,1024]{1,0:T(8,128)(2,1)}, bf16[512,1024]{1,0:T(8,128)(2,1)}, u32[]{:S(2)}, u32[]{:S(2)}) collective-permute-start(bf16[512,1024]{1,0:T(8,128)(2,1)} %multiply_convert_fusion.4), channel_id=1, source_target_pairs={{0,8},{8,0},{16,24},{24,16},{1,9},{9,1},{17,25},{25,17},{2,10},{10... | collective-permute-start | bytes 3145736 | tf_op jit(solution)/shard_map/ppermute | solution.py:243
  168.6 10.7 %collective-permute-start.16 = (bf16[512,1536]{1,0:T(8,128)(2,1)S(1)}, bf16[512,1536]{1,0:T(8,128)(2,1)S(1)}, u32[]{:S(2)}, u32[]{:S(2)}) collective-permute-start(bf16[512,1536]{1,0:T(8,128)(2,1)S(1)} %constant_dynamic-slice_fusion.7), channel_id=1, source_target_pairs={{0,8},{8,0},{16,24},{24,16},{1,9},{9,1},{17,25},{25,17},{2,10},{10... | collective-permute-start | bytes 4718600 | tf_op jit(solution)/shard_map/ppermute | solution.py:243
  210.9 194.7 %reduce-scatter.5.cloned.1.call-start = ((), (), s32[]{:S(2)}) async-start(), calls=%async_computation.4 | async-start | bytes 2654208 | tf_op jit(solution)/shard_map/reduce_scatter | solution.py:286
  223.0 9.7 %collective-permute-start.19 = (bf16[512,1024]{1,0:T(8,128)(2,1)S(1)}, bf16[512,1024]{1,0:T(8,128)(2,1)S(1)}, u32[]{:S(2)}, u32[]{:S(2)}) collective-permute-start(bf16[512,1024]{1,0:T(8,128)(2,1)S(1)} %slice.429), channel_id=1, source_target_pairs={{0,8},{8,0},{16,24},{24,16},{1,9},{9,1},{17,25},{25,17},{2,10},{10... | collective-permute-start | bytes 3145736 | tf_op jit(solution)/shard_map/ppermute | solution.py:243
  227.1 6.5 %collective-permute-start.17 = (bf16[512,1024]{1,0:T(8,128)(2,1)S(1)}, bf16[512,1024]{1,0:T(8,128)(2,1)S(1)}, u32[]{:S(2)}, u32[]{:S(2)}) collective-permute-start(bf16[512,1024]{1,0:T(8,128)(2,1)S(1)} %slice.430), channel_id=1, source_target_pairs={{0,8},{8,0},{16,24},{24,16},{1,9},{9,1},{17,25},{25,17},{2,10},{10... | collective-permute-start | bytes 3145736 | tf_op jit(solution)/shard_map/ppermute | solution.py:243
  232.2 5.5 %collective-permute-start.24 = (bf16[1408,512]{1,0:T(8,128)(2,1)S(1)}, bf16[1408,512]{1,0:T(8,128)(2,1)S(1)}, u32[]{:S(2)}, u32[]{:S(2)}) collective-permute-start(bf16[1408,512]{1,0:T(8,128)(2,1)S(1)} %constant_dynamic-slice_fusion.4), channel_id=1, source_target_pairs={{0,8},{8,0},{16,24},{24,16},{1,9},{9,1},{17,25},{25,17},{2,10},{10... | collective-permute-start | bytes 4325384 | tf_op jit(solution)/shard_map/ppermute | solution.py:243
  237.5 3.2 collective-permute-start.20
  239.8 82.1 %collective-permute-start.25 = (bf16[2816,256]{1,0:T(8,128)(2,1)}, bf16[2816,256]{1,0:T(8,128)(2,1)}, u32[]{:S(2)}, u32[]{:S(2)}) collective-permute-start(bf16[2816,256]{1,0:T(8,128)(2,1)} %get-tuple-element.117), channel_id=1, source_target_pairs={{0,16},{8,24},{16,0},{24,8},{1,17},{9,25},{17,1},{25,9},{2,18},{10... | collective-permute-start | bytes 4325384 | tf_op jit(solution)/shard_map/ppermute | solution.py:246
  285.3 32.8 %copy-start.5 = (f32[1024,1024]{1,0:T(8,128)}, f32[1024,1024]{1,0:T(8,128)S(1)}, u32[]{:S(2)}) copy-start(f32[1024,1024]{1,0:T(8,128)S(1)} %add_add_fusion) | copy-start | bytes 12582916
  285.5 32.6 %collective-permute-start.21 = (bf16[512,1024]{1,0:T(8,128)(2,1)S(1)}, bf16[512,1024]{1,0:T(8,128)(2,1)S(1)}, u32[]{:S(2)}, u32[]{:S(2)}) collective-permute-start(bf16[512,1024]{1,0:T(8,128)(2,1)S(1)} %slice.428), channel_id=1, source_target_pairs={{0,8},{8,0},{16,24},{24,16},{1,9},{9,1},{17,25},{25,17},{2,10},{10... | collective-permute-start | bytes 3145736 | tf_op jit(solution)/shard_map/ppermute | solution.py:243
  290.0 14.9 %collective-permute-start.23 = (bf16[1024,256]{1,0:T(8,128)(2,1)S(1)}, bf16[1024,256]{1,0:T(8,128)(2,1)S(1)}, u32[]{:S(2)}, u32[]{:S(2)}) collective-permute-start(bf16[1024,256]{1,0:T(8,128)(2,1)S(1)} %constant_dynamic-slice_fusion.5), channel_id=1, source_target_pairs={{0,16},{8,24},{16,0},{24,8},{1,17},{9,25},{17,1},{25,9},{2,18},{10... | collective-permute-start | bytes 1572872 | tf_op jit(solution)/shard_map/ppermute | solution.py:246
  292.4 8.8 %collective-permute-start.26 = (bf16[512,512]{1,0:T(8,128)(2,1)S(1)}, bf16[512,512]{1,0:T(8,128)(2,1)S(1)}, u32[]{:S(2)}, u32[]{:S(2)}) collective-permute-start(bf16[512,512]{1,0:T(8,128)(2,1)S(1)} %constant_dynamic-slice_fusion.3), channel_id=1, source_target_pairs={{0,8},{8,0},{16,24},{24,16},{1,9},{9,1},{17,25},{25,17},{2,10},{10... | collective-permute-start | bytes 1572872 | tf_op jit(solution)/shard_map/ppermute | solution.py:243
  296.0 20.0 %collective-permute-start.22 = (bf16[1024,256]{1,0:T(8,128)(2,1)S(1)}, bf16[1024,256]{1,0:T(8,128)(2,1)S(1)}, u32[]{:S(2)}, u32[]{:S(2)}) collective-permute-start(bf16[1024,256]{1,0:T(8,128)(2,1)S(1)} %constant_dynamic-slice_fusion.6), channel_id=1, source_target_pairs={{0,16},{8,24},{16,0},{24,8},{1,17},{9,25},{17,1},{25,9},{2,18},{10... | collective-permute-start | bytes 1572872 | tf_op jit(solution)/shard_map/ppermute | solution.py:246
  301.2 15.8 %collective-permute-start.38 = (bf16[512,512]{1,0:T(8,128)(2,1)S(1)}, bf16[512,512]{1,0:T(8,128)(2,1)S(1)}, u32[]{:S(2)}, u32[]{:S(2)}) collective-permute-start(bf16[512,512]{1,0:T(8,128)(2,1)S(1)} %slice.273), channel_id=1, source_target_pairs={{0,8},{8,0},{16,24},{24,16},{1,9},{9,1},{17,25},{25,17},{2,10},{10... | collective-permute-start | bytes 1572872 | tf_op jit(solution)/shard_map/ppermute | solution.py:243
  304.8 22.4 %collective-permute-start.27 = (bf16[1024,256]{1,0:T(8,128)(2,1)}, bf16[1024,256]{1,0:T(8,128)(2,1)}, u32[]{:S(2)}, u32[]{:S(2)}) collective-permute-start(bf16[1024,256]{1,0:T(8,128)(2,1)} %get-tuple-element.135), channel_id=1, source_target_pairs={{0,16},{8,24},{16,0},{24,8},{1,17},{9,25},{17,1},{25,9},{2,18},{10... | collective-permute-start | bytes 1572872 | tf_op jit(solution)/shard_map/ppermute | solution.py:246
  327.3 18.3 %collective-permute-start.36 = (bf16[128,2816]{1,0:T(8,128)(2,1)}, bf16[128,2816]{1,0:T(8,128)(2,1)S(1)}, u32[]{:S(2)}, u32[]{:S(2)}) collective-permute-start(bf16[128,2816]{1,0:T(8,128)(2,1)} %reduce-scatter.3.cloned.1.call-done), channel_id=1, source_target_pairs={{0,16},{8,24},{16,0},{24,8},{1,17},{9,25},{17,1},{25,9},{2,18},{10... | collective-permute-start | bytes 2162696 | tf_op jit(solution)/shard_map/ppermute | solution.py:246
  331.6 29.7 %collective-permute-start.30 = (bf16[4,480,256]{2,1,0:T(8,128)(2,1)S(1)}, bf16[4,480,256]{2,1,0:T(8,128)(2,1)S(1)}, u32[]{:S(2)}, u32[]{:S(2)}) collective-permute-start(bf16[4,480,256]{2,1,0:T(8,128)(2,1)S(1)} %fusion.31), channel_id=1, source_target_pairs={{0,1},{1,0},{2,3},{3,2},{4,5},{5,4},{6,7},{7,6},{8,9},{9,8},{10,11... | collective-permute-start | bytes 2949128 | tf_op jit(solution)/shard_map/ppermute | solution.py:292
  332.5 37.5 %copy-start.6 = (f32[1024,1024]{1,0:T(8,128)S(1)}, f32[1024,1024]{1,0:T(8,128)}, u32[]{:S(2)}) copy-start(f32[1024,1024]{1,0:T(8,128)} %copy-done.5) | copy-start | bytes 12582916
  345.5 24.5 %copy-start.10 = (f32[512,1024]{1,0:T(8,128)S(1)}, f32[512,1024]{1,0:T(8,128)}, u32[]{:S(2)}) copy-start(f32[512,1024]{1,0:T(8,128)} %get-tuple-element.104) | copy-start | bytes 6291460
  347.0 44.2 %collective-permute-start.37 = (bf16[128,2816]{1,0:T(8,128)(2,1)S(1)}, bf16[128,2816]{1,0:T(8,128)(2,1)S(1)}, u32[]{:S(2)}, u32[]{:S(2)}) collective-permute-start(bf16[128,2816]{1,0:T(8,128)(2,1)S(1)} %add_convert_fusion.1), channel_id=1, source_target_pairs={{0,8},{8,0},{16,24},{24,16},{1,9},{9,1},{17,25},{25,17},{2,10},{10... | collective-permute-start | bytes 2162696 | tf_op jit(solution)/shard_map/ppermute | solution.py:243
  361.7 14.1 %collective-permute-start.33 = (bf16[480,256]{1,0:T(8,128)(2,1)S(1)}, bf16[480,256]{1,0:T(8,128)(2,1)S(1)}, u32[]{:S(2)}, u32[]{:S(2)}) collective-permute-start(bf16[480,256]{1,0:T(8,128)(2,1)S(1)} %get-tuple-element.142), channel_id=1, source_target_pairs={{0,6},{1,7},{2,0},{3,1},{4,2},{5,3},{6,4},{7,5},{8,14},{9,15},{10,... | collective-permute-start | bytes 737288 | tf_op jit(solution)/shard_map/ppermute | solution.py:295
  369.4 19.7 %collective-permute-start.32 = (bf16[480,256]{1,0:T(8,128)(2,1)S(1)}, bf16[480,256]{1,0:T(8,128)(2,1)S(1)}, u32[]{:S(2)}, u32[]{:S(2)}) collective-permute-start(bf16[480,256]{1,0:T(8,128)(2,1)S(1)} %get-tuple-element.143), channel_id=1, source_target_pairs={{0,4},{1,5},{2,6},{3,7},{4,0},{5,1},{6,2},{7,3},{8,12},{9,13},{10,... | collective-permute-start | bytes 737288 | tf_op jit(solution)/shard_map/ppermute | solution.py:295
  369.4 19.7 %collective-permute-start.31 = (bf16[480,256]{1,0:T(8,128)(2,1)S(1)}, bf16[480,256]{1,0:T(8,128)(2,1)S(1)}, u32[]{:S(2)}, u32[]{:S(2)}) collective-permute-start(bf16[480,256]{1,0:T(8,128)(2,1)S(1)} %get-tuple-element.141), channel_id=1, source_target_pairs={{0,2},{1,3},{2,4},{3,5},{4,6},{5,7},{6,0},{7,1},{8,10},{9,11},{10,... | collective-permute-start | bytes 737288 | tf_op jit(solution)/shard_map/ppermute | solution.py:295
  389.3 17.8 %collective-permute-start.34 = (bf16[480,256]{1,0:T(8,128)(2,1)S(1)}, bf16[480,256]{1,0:T(8,128)(2,1)S(1)}, u32[]{:S(2)}, u32[]{:S(2)}) collective-permute-start(bf16[480,256]{1,0:T(8,128)(2,1)S(1)} %fusion.41), channel_id=1, source_target_pairs={{0,16},{8,24},{16,0},{24,8},{1,17},{9,25},{17,1},{25,9},{2,18},{10... | collective-permute-start | bytes 737288 | tf_op jit(solution)/shard_map/ppermute | solution.py:246
  405.6 7.2 %collective-permute-start.28 = (bf16[128,1152]{1,0:T(8,128)(2,1)}, bf16[128,1152]{1,0:T(8,128)(2,1)S(1)}, u32[]{:S(2)}, u32[]{:S(2)}) collective-permute-start(bf16[128,1152]{1,0:T(8,128)(2,1)} %reduce-scatter.5.cloned.1.call-done), channel_id=1, source_target_pairs={{0,16},{8,24},{16,0},{24,8},{1,17},{9,25},{17,1},{25,9},{2,18},{10... | collective-permute-start | bytes 884744 | tf_op jit(solution)/shard_map/ppermute | solution.py:246
  407.1 7.6 %collective-permute-start.35 = (bf16[480,512]{1,0:T(8,128)(2,1)S(1)}, bf16[480,512]{1,0:T(8,128)(2,1)S(1)}, u32[]{:S(2)}, u32[]{:S(2)}) collective-permute-start(bf16[480,512]{1,0:T(8,128)(2,1)S(1)} %pad_maximum_fusion.23), channel_id=1, source_target_pairs={{0,8},{8,0},{16,24},{24,16},{1,9},{9,1},{17,25},{25,17},{2,10},{10... | collective-permute-start | bytes 1474568 | tf_op jit(solution)/shard_map/ppermute | solution.py:243
  414.6 2.4 collective-permute-start.29
  (49 other events, 238.0 us)
Sparse Core Ops, SparseCore 0:
  60.6 103.4 all-gather.1
  211.0 114.2 reduce-scatter.2
  328.8 76.7 reduce-scatter.4

commit v5 on v4

--- a/solution.py
+++ b/solution.py
@@ -185,12 +185,13 @@
     )(jnp.stack([place]), *pieces)
 
 
-def join_kernel(at_ref, mine_ref, far_ref, other_ref, out_ref):
-    size = other_ref.shape[3]
+def join_kernel(at_ref, mine_ref, far_ref, mine_other_ref, far_other_ref, out_ref):
+    size = mine_other_ref.shape[2]
     shared = mine_ref.shape[2] - size
     side, chip = at_ref[0], at_ref[1]
-    for from_side, own in enumerate((mine_ref, far_ref)):
-        row = side if from_side == 0 else 1 - side
+    for own, other_ref, row in (
+        (mine_ref, mine_other_ref, side), (far_ref, far_other_ref, 1 - side)
+    ):
         if shared:
             out_ref[:, row, :, :shared] = own[:, :, :shared]
         for which in range(2):
@@ -198,20 +199,20 @@
             def _():
                 first, second = shared + which * size, shared + (1 - which) * size
                 out_ref[:, row, :, first : first + size] = own[:, :, shared:]
-                out_ref[:, row, :, second : second + size] = other_ref[from_side]
-
-
-def joined(side, chip, mine, far, other):
+                out_ref[:, row, :, second : second + size] = other_ref[...]
+
+
+def joined(side, chip, mine, far, mine_other, far_other):
     ring, height, held = mine.shape
     in_vmem = pl.BlockSpec(memory_space=pltpu.VMEM)
-    full = jax.ShapeDtypeStruct((ring, 2, height, held + other.shape[3]), mine.dtype)
+    full = jax.ShapeDtypeStruct((ring, 2, height, held + mine_other.shape[2]), mine.dtype)
     whole = pl.pallas_call(
         join_kernel,
-        in_specs=[pl.BlockSpec(memory_space=pltpu.SMEM)] + [in_vmem] * 3,
+        in_specs=[pl.BlockSpec(memory_space=pltpu.SMEM)] + [in_vmem] * 4,
         out_specs=in_vmem,
         out_shape=full,
         name="joined",
-    )(jnp.stack([side, chip]), mine, far, other)
+    )(jnp.stack([side, chip]), mine, far, mine_other, far_other)
     return whole.reshape(ring * 2 * height, full.shape[3])
 
 
@@ -307,9 +308,8 @@
     def ring_pieces(held):
         return [held] + [around(held, step) for step in range(1, ring)]
 
-    def swapped_halves(shard, mine, far):
-        shared = shared_lanes(shard)
-        return jnp.stack([mine[:, :, shared:], far[:, :, shared:]])
+    def half_of(shard, values):
+        return values[:, :, shared_lanes(shard) :]
 
     def mine_and_partner(partial):
         return partial[:length] + swap(partial[length:].astype(bf16)).astype(f32)
@@ -331,17 +331,16 @@
         pieces_a, held_b = tie((pieces_a, held_columns(shard_b)))
         pieces_b = ring_pieces(held_b)
         mine_a = in_ring_order(place, pieces_a)
-        far_a = sides(mine_a)
-        pieces_b, far_a, mine_a, shard_c = tie((pieces_b, far_a, mine_a, shard_c))
+        mine_a, half_a = tie((mine_a, half_of(shard_a, mine_a)))
+        far_a, mine_other_a = sides(mine_a), to_chip(half_a, 1)
+        pieces_b, far_a, mine_a, mine_other_a, shard_c = tie(
+            (pieces_b, far_a, mine_a, mine_other_a, shard_c)
+        )
+        half_a = half_of(shard_a, far_a)
         mine_b = in_ring_order(place, pieces_b)
-        halves_a = swapped_halves(shard_a, mine_a, far_a)
-        mine_b, halves_a = tie((mine_b, halves_a))
-        far_b, other_a = sides(mine_b), to_chip(halves_a, 1)
-        far_b, other_a = tie((far_b, other_a))
-        halves_b = swapped_halves(shard_b, mine_b, far_b)
-        halves_b, other_a = tie((halves_b, other_a))
-        other_b = to_chip(halves_b, 1)
-        whole_a = join(mine_a, far_a, other_a)
+        half_a, mine_b, half_b = tie((half_a, mine_b, half_of(shard_b, mine_b)))
+        far_other_a, far_b, mine_other_b = to_chip(half_a, 1), sides(mine_b), to_chip(half_b, 1)
+        whole_a = join(mine_a, far_a, mine_other_a, far_other_a)
     else:
         whole_a = gather(shard_a)
     whole_c = gather(shard_c)
@@ -363,10 +362,16 @@
     inverse_one = norm_stats(hidden)
     normed = (hidden * inverse_one * gain_one).astype(bf16)
     qkv = dot_nn(normed, qkv_mat)
+    if by_ring:
+        far_b, qkv = tie((far_b, qkv))
+        half_b, qkv = tie((half_of(shard_b, far_b), qkv))
+        far_other_b = to_chip(half_b, 1)
     attended, q_rot, k_rot, blended = attend(starts, cosine, sine, qkv, first_half, length)
     if by_ring:
-        attended, other_b = tie((attended, other_b))
-        whole_b = join(mine_b, far_b, other_b)
+        attended, far_b, mine_other_b, far_other_b = tie(
+            (attended, far_b, mine_other_b, far_other_b)
+        )
+        whole_b = join(mine_b, far_b, mine_other_b, far_other_b)
     else:
         whole_b = gather(shard_b)
     output_mat, gate_mat = rows_from_cols(whole_b[:, :hw]), whole_b[:, hw:]
@@ -411,6 +416,9 @@
     grad_attended = dot_nt(grad_attn, output_mat).astype(bf16)
     grad_out_w = chip_parts(grad_out_w)
     dq, dk, dv = attend_back(starts, cosine, sine, q_rot, k_rot, blended, grad_attended, length)
+    grad_q, grad_k = (dot_tn(normed, d).astype(bf16) for d in (dq, dk))
+    grad_q, grad_k, dq, dk, dv = tie((grad_q, grad_k, dq, dk, dv))
+    grad_q, grad_k = chip_parts(grad_q), chip_parts(grad_k)
     grad_normed = mine_and_partner(
         dot_nt(dq, qkv_mat[:, :hw]) + dot_nt(dk, qkv_mat[:, hw : 2 * hw])
         + dot_nt(dv, qkv_mat[:, 2 * hw :])
@@ -437,10 +445,10 @@
         axis=1,
     )
     extra = jnp.pad(extra, ((0, 0), (0, LANES - extra.shape[1]))).astype(bf16)
-    grad_q, grad_k = (chip_parts(dot_tn(normed, d).astype(bf16)) for d in (dq, dk))
     grad_v = dot_tn(normed, dv).astype(bf16)
     grad_a = jnp.concatenate([added(grad_q), added(grad_k), grad_v, extra], axis=1)
-    grad_a, grad_b, grad_down, grad_out_w = tie((grad_a, grad_b, grad_down, grad_out_w))
+    grad_a, grad_b = tie((grad_a, grad_b))
+    grad_b, grad_down, grad_out_w = tie((grad_b, grad_down, grad_out_w))
     grad_do = jnp.concatenate(
         [added(parts).reshape(fsdp, -1, hw // chips) for parts in (grad_down, grad_out_w)], axis=1
     )

time: 436 us -> 426 us (0.977)
  local copies, waits for them, and re-layouts: 21.3 us -> 30.1 us
  waiting for transfers between devices: 139 us -> 131 us
  starting transfers between devices: 42.1 us -> 37.7 us
    ppermute x3, waiting for transfers between devices: 44.6 us -> 16.9 us  [sides(): return lax.ppermute(values, 'fsdp', [(i, i ^ 1) for i in range(fsdp)])]
    ppermute x9 -> x11, waiting for transfers between devices: 36.2 us -> 55.2 us  [to_chip(): lax.ppermute(values, 'dp', [(i, (i + 2 * step) % dp) for i in range(dp)])]
    slice x1 -> x5, local copies, waits for them, and re-layouts: 0.22 us -> 7.85 us  [the longest x4 7.64 us: half_of(): return values[:, :, shared_lanes(shard):]]
    all_gather x1, waiting for transfers between devices: 0.01 us -> 5.09 us  [gather(): return lax.all_gather(shard, 'fsdp', axis=0, tiled=True)]
    ppermute x9 -> x11, starting transfers between devices: 11.6 us -> 11.5 us  [to_chip(): lax.ppermute(values, 'dp', [(i, (i + 2 * step) % dp) for i in range(dp)])]
  transfers between devices with their start and end apart: 42 -> 44, of which waited for: 17 -> 18; matrix products, arithmetic and copies ran while one was open for 28% -> 28% of each run, Pallas kernels for 16% -> 16%
where the time goes in v5:
time: 426 us; the launch traced here: 418 us
  waiting for transfers between devices  131 us (31%)
  matrix products  79.5 us (19%)
  Pallas kernels  69.6 us (16%)
  other arithmetic  54.9 us (13%)
  starting transfers between devices  37.7 us (9%)
  local copies, waits for them, and re-layouts  30.1 us (7%)
  between operations  15.4 us (4%)
    ppermute x11, waiting for transfers between devices, to_chip(): lax.ppermute(values, 'dp', [(i, (i + 2 * step) % dp) for i in range(dp)])  55.2 us
    ppermute x9, waiting for transfers between devices, around(): lax.ppermute(values, 'fsdp', [(i, (i + 2 * step) % fsdp) for i in range(f...  41.9 us
    pallas_call x1, Pallas kernels, attend_back(): pl.pallas_call(attend_back_kernel, grid=(tokens // length, width // LANES...  35.4 us
    dot_general x5, matrix products, dot_nn(): return jnp.dot(a, b, preferred_element_type=f32)  29 us
    dot_general x7, matrix products, dot_tn(): lax.dot_general(a, b, (((0,), (0,)), ((), ())), preferred_element_type=f32)  27.3 us
    dot_general x7, matrix products, dot_nt(): lax.dot_general(a, b, (((1,), (1,)), ((), ())), preferred_element_type=f32)  23.2 us
    pallas_call x1, Pallas kernels, attend(): pl.pallas_call(attend_kernel, grid=(tokens // length, pairs), in_specs=[p...  21.1 us
    ppermute x9, starting transfers between devices, around(): lax.ppermute(values, 'fsdp', [(i, (i + 2 * step) % fsdp) for i in range(f...  19.7 us
  transfers between devices with their start and end apart: 44, of which 18 were waited for; matrix products, arithmetic and copies ran while one was open for 28% of the time, Pallas kernels for 16%

profile of v5, /device:TPU:0, one launch (start us, length us, event | category | flops | bytes accessed | tf_op | source)
XLA Modules:
  0.0 418.1 jit_solution(15702372452275368857)
XLA Ops:
  10.1 3.1 collective-permute-start.2
  13.2 2.6 collective-permute-start.3
  18.4 3.5 collective-permute-done.2.refs_1_
  21.9 9.0 %collective-permute-done.3.refs_2_ = bf16[128,896]{1,0:T(8,128)(2,1)S(1)} collective-permute-done((bf16[128,896]{1,0:T(8,128)(2,1)S(1)}, bf16[128,896]{1,0:T(8,128)(2,1)S(1)}, u32[]{:S(2)}, u32[]{:S(2)}) %collective-permute-start.3) | collective-permute-done | bytes 229408 | tf_op jit(solution)/shard_map/ppermute | solution.py:296
  31.6 2.3 ring_order.2.mine_ref
  41.0 5.4 %collective-permute-start.5 = (bf16[128,1024]{1,0:T(8,128)(2,1)S(1)}, bf16[128,1024]{1,0:T(8,128)(2,1)S(1)}, u32[]{:S(2)}, u32[]{:S(2)}) collective-permute-start(bf16[128,1024]{1,0:T(8,128)(2,1)S(1)} %pad_maximum_fusion.22.refs_0_), channel_id=1, source_target_pairs={{0,2},{1,3},{2,4},{3,5},{4,6},{5,7},{6,0},{7,1},{8,10},{9,11},{10,... | collective-permute-start | bytes 786440 | tf_op jit(solution)/shard_map/ppermute | solution.py:296
  49.7 5.0 %collective-permute-done.5.refs_1_ = bf16[128,1024]{1,0:T(8,128)(2,1)S(1)} collective-permute-done((bf16[128,1024]{1,0:T(8,128)(2,1)S(1)}, bf16[128,1024]{1,0:T(8,128)(2,1)S(1)}, u32[]{:S(2)}, u32[]{:S(2)}) %collective-permute-start.5) | collective-permute-done | bytes 262176 | tf_op jit(solution)/shard_map/ppermute | solution.py:296
  54.7 9.1 %collective-permute-done.6.refs_2_ = bf16[128,1024]{1,0:T(8,128)(2,1)} collective-permute-done((bf16[128,1024]{1,0:T(8,128)(2,1)S(1)}, bf16[128,1024]{1,0:T(8,128)(2,1)}, u32[]{:S(2)}, u32[]{:S(2)}) %collective-permute-start.6) | collective-permute-done | bytes 262176 | tf_op jit(solution)/shard_map/ppermute | solution.py:296
  68.2 2.2 ring_order.3.mine_ref
  70.4 2.3 slice.278
  77.7 15.7 %collective-permute-done.11.far_other_ref = bf16[4,128,768]{2,1,0:T(8,128)(2,1)} collective-permute-done((bf16[4,128,768]{2,1,0:T(8,128)(2,1)}, bf16[4,128,768]{2,1,0:T(8,128)(2,1)}, u32[]{:S(2)}, u32[]{:S(2)}) %collective-permute-start.11) | collective-permute-done | bytes 786464 | tf_op jit(solution)/shard_map/ppermute | solution.py:247
  93.4 4.0 joined.2
  98.4 8.3 %fusion.2.q_ref.k_ref.v_ref = f32[1024,1536]{1,0:T(8,128)} fusion(bf16[1024,1664]{1,0:T(8,128)(2,1)} %bitcast.83, f32[1024]{0:T(1024)S(1)} %bitcast.113, f32[1024]{0:T(1024)S(1)} %add_rsqrt_fusion, bf16[512,1024]{1,0:T(8,128)(2,1)} %collective-permute-done, bf16[512,1024]{1,0:T(8,128)(2,1)S(1)} %bitcast.94), kind=kOutput, calls=%fused_computation.18 | convolution fusion | flops 3228565504 | bytes 11542528 | tf_op jit(solution)/shard_map/dot_general | solution.py:66
  106.7 2.5 collective-permute-done.10.far_ref
  113.4 3.0 fusion.39
  117.5 21.1 %attend.1 = (bf16[1024,512]{1,0:T(8,128)(2,1)}, bf16[1024,512]{1,0:T(8,128)(2,1)}, bf16[1024,512]{1,0:T(8,128)(2,1)}, bf16[1024,512]{1,0:T(8,128)(2,1)}) custom-call(s32[1024,1]{1,0:T(8,128)} %copy.37.start_ref, f32[1024,128]{1,0:T(8,128)} %get-tuple-element.183.cos_ref, f32[1024,128]{1,0:T(8,128)} %get-tuple-element.182.sin_ref, ...), custom_call_target="tpu_custom_call" | custom-call | tf_op jit(solution)/shard_map/attend/pallas_call | solution.py:145
  138.7 4.6 %joined.3 = bf16[4,2,128,1920]{3,2,1,0:T(8,128)(2,1)} custom-call(s32[2]{0:T(128)} %pad_add_fusion.2.at_ref, bf16[4,128,1024]{2,1,0:T(8,128)(2,1)} %ring_order.3.mine_ref, bf16[4,128,1024]{2,1,0:T(8,128)(2,1)} %collective-permute-done.10.far_ref, bf16[4,128,896]{2,1,0:T(8,128)(2,1)} %collective-permute-done.13.mine_other_ref, ...), custom_call_target="tpu_custom_call" | custom-call | tf_op jit(solution)/shard_map/joined/pallas_call | solution.py:209
  148.0 2.7 fusion.38
  155.9 2.5 multiply_reduce_fusion.7
  159.7 5.1 %all-gather.2.cloned.1.call-done = bf16[1024,2944]{1,0:T(8,128)(2,1)} async-done(((bf16[128,2944]{1,0:T(8,128)(2,1)}), bf16[1024,2944]{1,0:T(8,128)(2,1)}) %all-gather.2.cloned.1.call-update) | async-done | bytes 6029328 | tf_op jit(solution)/shard_map/all_gather | solution.py:284
  164.8 2.1 slice.288
  171.9 5.9 %fusion.6 = f32[1024,1408]{1,0:T(8,128)S(1)} fusion(bf16[1024,2944]{1,0:T(8,128)(2,1)} %all-gather.2.cloned.1.call-done, bf16[512,1024]{1,0:T(8,128)(2,1)} %collective-permute-done.17, bf16[512,1024]{1,0:T(8,128)(2,1)} %multiply_convert_fusion.4), kind=kOutput, calls=%fused_computation.24 | convolution fusion | flops 2956984320 | bytes 10747904 | tf_op jit(solution)/shard_map/dot_general | solution.py:66
  180.5 5.1 %fusion.20 = f32[1024,1408]{1,0:T(8,128)S(1)} fusion(bf16[1408,512]{1,0:T(8,128)(2,1)S(1)} %bitcast.107, bf16[1408,512]{1,0:T(8,128)(2,1)S(1)} %bitcast.105, bf16[512,1024]{1,0:T(8,128)(2,1)} %collective-permute-done.20, bf16[512,1024]{1,0:T(8,128)(2,1)} %bitcast.26), kind=kOutput, calls=%fused_computation.65 | convolution fusion | flops 2962751488 | bytes 10747904 | tf_op jit(solution)/shard_map/dot_general | solution.py:58
  185.7 8.8 %multiply_convert_fusion.1 = (bf16[1024,1408]{1,0:T(8,128)(2,1)}, bf16[1024,1408]{1,0:T(8,128)(2,1)S(1)}, bf16[1024,1408]{1,0:T(8,128)(2,1)}) fusion(f32[1024,1408]{1,0:T(8,128)S(1)} %fusion.20, f32[1024,1408]{1,0:T(8,128)S(1)} %fusion.6, bf16[1024,1920]{1,0:T(8,128)(2,1)S(1)} %bitcast.89, bf16[512,1024]{1,0:T(8,128)(2,1)} %collective-permute-done.17, ...), kind=kOutput, calls=%fused_computation.2 | convolution fusion | flops 2978611200 | bytes 25165824 | tf_op jit(solution)/shard_map/dot_general | solution.py:66
  194.5 6.4 %convolution_convert_fusion.1 = bf16[1024,1408]{1,0:T(8,128)(2,1)S(1)} fusion(bf16[1024,1408]{1,0:T(8,128)(2,1)S(1)} %get-tuple-element.90, bf16[512,1024]{1,0:T(8,128)(2,1)} %collective-permute-done.17, bf16[512,1024]{1,0:T(8,128)(2,1)} %multiply_convert_fusion.4), kind=kOutput, calls=%fused_computation.12 | convolution fusion | flops 2958426112 | bytes 7864320 | tf_op jit(solution)/shard_map/dot_general | solution.py:62
  200.9 5.3 %convolution_convert_fusion.2 = bf16[1024,1408]{1,0:T(8,128)(2,1)S(1)} fusion(bf16[1024,1408]{1,0:T(8,128)(2,1)S(1)} %copy-done.48, bf16[512,1024]{1,0:T(8,128)(2,1)} %collective-permute-done.17, bf16[512,1024]{1,0:T(8,128)(2,1)} %multiply_convert_fusion.4), kind=kOutput, calls=%fused_computation.13 | convolution fusion | flops 2958426112 | bytes 7864320 | tf_op jit(solution)/shard_map/dot_general | solution.py:62
  206.3 2.8 pad_maximum_fusion
  209.4 6.3 %fusion.8 = f32[1024,1024]{1,0:T(8,128)S(1)} fusion(bf16[1024,1408]{1,0:T(8,128)(2,1)} %get-tuple-element.89, bf16[1024,1920]{1,0:T(8,128)(2,1)} %bitcast.88), kind=kOutput, calls=%fused_computation.26 | convolution fusion | flops 2952790016 | bytes 9961472 | tf_op jit(solution)/shard_map/dot_general | solution.py:58
  215.7 5.4 %fusion.17 = f32[1024,1024]{1,0:T(8,128)S(1)} fusion(f32[1024,1024]{1,0:T(8,128)S(1)} %fusion.8, bf16[1024,1408]{1,0:T(8,128)(2,1)S(1)} %copy-done.47, bf16[1024,2944]{1,0:T(8,128)(2,1)} %all-gather.2.cloned.1.call-done), kind=kOutput, calls=%fused_computation.64 | convolution fusion | flops 2953838592 | bytes 14155776 | tf_op jit(solution)/shard_map/dot_general | solution.py:58
  221.5 3.4 fusion.21
  225.6 4.8 %convolution_convert_fusion = bf16[1408,1024]{1,0:T(8,128)(2,1)S(1)} fusion(bf16[1024,1408]{1,0:T(8,128)(2,1)S(1)} %copy-done.45, bf16[512,1024]{1,0:T(8,128)(2,1)} %collective-permute-done.20, bf16[512,1024]{1,0:T(8,128)(2,1)} %bitcast.26), kind=kOutput, calls=%fused_computation.11 | convolution fusion | flops 2958426112 | bytes 7864320 | tf_op jit(solution)/shard_map/dot_general | solution.py:62
  231.5 3.9 fusion.67
  239.6 2.5 convolution_convert_fusion.7.grad_ref
  242.1 35.4 %attend_back.1 = (bf16[1024,512]{1,0:T(8,128)(2,1)}, bf16[1024,512]{1,0:T(8,128)(2,1)}, bf16[1024,512]{1,0:T(8,128)(2,1)}) custom-call(s32[1024,1]{1,0:T(8,128)} %copy.37.start_ref, f32[1024,128]{1,0:T(8,128)} %get-tuple-element.183.cos_ref, f32[1024,128]{1,0:T(8,128)} %get-tuple-element.182.sin_ref, bf16[1024,512]{1,0:T(8,128)(2,1)} %get-tuple-element.91.q_rot_ref, ...), custom_call_target="tpu_custom_call" | custom-call | tf_op jit(solution)/shard_map/attend_back/pallas_call | solution.py:159
  277.5 3.0 convolution_convert_fusion.6
  280.5 2.8 convolution_convert_fusion.5
  292.7 3.6 convolution_convert_fusion.4
  297.8 4.8 %collective-permute-done.25 = bf16[1024,256]{1,0:T(8,128)(2,1)S(1)} collective-permute-done((bf16[1024,256]{1,0:T(8,128)(2,1)S(1)}, bf16[1024,256]{1,0:T(8,128)(2,1)S(1)}, u32[]{:S(2)}, u32[]{:S(2)}) %collective-permute-start.25) | collective-permute-done | bytes 524320 | tf_op jit(solution)/shard_map/ppermute | solution.py:247
  303.1 10.7 %collective-permute-done.24 = bf16[1024,256]{1,0:T(8,128)(2,1)S(1)} collective-permute-done((bf16[1024,256]{1,0:T(8,128)(2,1)S(1)}, bf16[1024,256]{1,0:T(8,128)(2,1)S(1)}, u32[]{:S(2)}, u32[]{:S(2)}) %collective-permute-start.24) | collective-permute-done | bytes 524320 | tf_op jit(solution)/shard_map/ppermute | solution.py:247
  316.0 2.6 fusion.12
  318.7 5.9 %collective-permute-done.31 = bf16[1024,256]{1,0:T(8,128)(2,1)} collective-permute-done((bf16[1024,256]{1,0:T(8,128)(2,1)}, bf16[1024,256]{1,0:T(8,128)(2,1)}, u32[]{:S(2)}, u32[]{:S(2)}) %collective-permute-start.31) | collective-permute-done | bytes 524320 | tf_op jit(solution)/shard_map/ppermute | solution.py:247
  330.5 12.0 %collective-permute-done.38 = bf16[128,2816]{1,0:T(8,128)(2,1)S(1)} collective-permute-done((bf16[128,2816]{1,0:T(8,128)(2,1)}, bf16[128,2816]{1,0:T(8,128)(2,1)S(1)}, u32[]{:S(2)}, u32[]{:S(2)}) %collective-permute-start.38) | collective-permute-done | bytes 720928 | tf_op jit(solution)/shard_map/ppermute | solution.py:247
  344.0 14.4 %collective-permute-done.32 = bf16[4,480,256]{2,1,0:T(8,128)(2,1)S(1)} collective-permute-done((bf16[4,480,256]{2,1,0:T(8,128)(2,1)S(1)}, bf16[4,480,256]{2,1,0:T(8,128)(2,1)S(1)}, u32[]{:S(2)}, u32[]{:S(2)}) %collective-permute-start.32) | collective-permute-done | bytes 983072 | tf_op jit(solution)/shard_map/ppermute | solution.py:293
  358.8 2.9 collective-permute-start.35
  365.7 2.4 collective-permute-done.35
  368.1 13.0 %collective-permute-done.34 = bf16[480,256]{1,0:T(8,128)(2,1)S(1)} collective-permute-done((bf16[480,256]{1,0:T(8,128)(2,1)S(1)}, bf16[480,256]{1,0:T(8,128)(2,1)S(1)}, u32[]{:S(2)}, u32[]{:S(2)}) %collective-permute-start.34) | collective-permute-done | bytes 245792 | tf_op jit(solution)/shard_map/ppermute | solution.py:296
  385.6 9.3 %reduce-scatter.5.cloned.1.call-done = bf16[128,1152]{1,0:T(8,128)(2,1)} async-done(((bf16[1024,1152]{1,0:T(8,128)(2,1)}), bf16[128,1152]{1,0:T(8,128)(2,1)}) %reduce-scatter.5.cloned.1.call-update) | async-done | bytes 294928 | tf_op jit(solution)/shard_map/reduce_scatter | solution.py:287
  396.6 6.2 %collective-permute-done.26 = bf16[128,1152]{1,0:T(8,128)(2,1)S(1)} collective-permute-done((bf16[128,1152]{1,0:T(8,128)(2,1)}, bf16[128,1152]{1,0:T(8,128)(2,1)S(1)}, u32[]{:S(2)}, u32[]{:S(2)}) %collective-permute-start.26) | collective-permute-done | bytes 294944 | tf_op jit(solution)/shard_map/ppermute | solution.py:247
  (288 shorter events, 97.3 us)
Async XLA Ops:
  7.2 157.6 %all-gather.2.cloned.1.call-start = ((), (), s32[]{:S(2)}) async-start(), calls=%async_computation.2 | async-start | bytes 6782976 | tf_op jit(solution)/shard_map/all_gather | solution.py:284
  10.1 11.7 %collective-permute-start.2 = (bf16[128,896]{1,0:T(8,128)(2,1)S(1)}, bf16[128,896]{1,0:T(8,128)(2,1)S(1)}, u32[]{:S(2)}, u32[]{:S(2)}) collective-permute-start(bf16[128,896]{1,0:T(8,128)(2,1)S(1)} %pad_maximum_fusion.23.refs_0_), channel_id=1, source_target_pairs={{0,2},{1,3},{2,4},{3,5},{4,6},{5,7},{6,0},{7,1},{8,10},{9,11},{10,... | collective-permute-start | bytes 688136 | tf_op jit(solution)/shard_map/ppermute | solution.py:296
  13.2 17.6 %collective-permute-start.3 = (bf16[128,896]{1,0:T(8,128)(2,1)S(1)}, bf16[128,896]{1,0:T(8,128)(2,1)S(1)}, u32[]{:S(2)}, u32[]{:S(2)}) collective-permute-start(bf16[128,896]{1,0:T(8,128)(2,1)S(1)} %pad_maximum_fusion.23.refs_0_), channel_id=1, source_target_pairs={{0,4},{1,5},{2,6},{3,7},{4,0},{5,1},{6,2},{7,3},{8,12},{9,13},{10,... | collective-permute-start | bytes 688136 | tf_op jit(solution)/shard_map/ppermute | solution.py:296
  15.8 15.0 %collective-permute-start.4 = (bf16[128,896]{1,0:T(8,128)(2,1)S(1)}, bf16[128,896]{1,0:T(8,128)(2,1)S(1)}, u32[]{:S(2)}, u32[]{:S(2)}) collective-permute-start(bf16[128,896]{1,0:T(8,128)(2,1)S(1)} %pad_maximum_fusion.23.refs_0_), channel_id=1, source_target_pairs={{0,6},{1,7},{2,0},{3,1},{4,2},{5,3},{6,4},{7,5},{8,14},{9,15},{10,... | collective-permute-start | bytes 688136 | tf_op jit(solution)/shard_map/ppermute | solution.py:296
  18.4 29.6 %copy-start.33 = (bf16[128,1024]{1,0:T(8,128)(2,1)}, bf16[128,1024]{1,0:T(8,128)(2,1)S(1)}, u32[]{:S(2)}) copy-start(bf16[128,1024]{1,0:T(8,128)(2,1)S(1)} %pad_maximum_fusion.22.refs_0_) | copy-start | bytes 786436
  35.9 28.5 %copy-start.14 = (bf16[1,512,1024]{2,1,0:T(8,128)(2,1)S(1)}, bf16[1,512,1024]{2,1,0:T(8,128)(2,1)}, u32[]{:S(2)}) copy-start(bf16[1,512,1024]{2,1,0:T(8,128)(2,1)} %param.15) | copy-start | bytes 3145732
  35.9 27.9 %collective-permute-start.8 = (bf16[4,128,896]{2,1,0:T(8,128)(2,1)}, bf16[4,128,896]{2,1,0:T(8,128)(2,1)}, u32[]{:S(2)}, u32[]{:S(2)}) collective-permute-start(bf16[4,128,896]{2,1,0:T(8,128)(2,1)} %ring_order.2.mine_ref), channel_id=1, source_target_pairs={{0,1},{1,0},{2,3},{3,2},{4,5},{5,4},{6,7},{7,6},{8,9},{9,8},{10,11... | collective-permute-start | bytes 2752520 | tf_op jit(solution)/shard_map/ppermute | solution.py:293
  37.5 26.4 %collective-permute-start.9 = (bf16[4,128,768]{2,1,0:T(8,128)(2,1)}, bf16[4,128,768]{2,1,0:T(8,128)(2,1)}, u32[]{:S(2)}, u32[]{:S(2)}) collective-permute-start(bf16[4,128,768]{2,1,0:T(8,128)(2,1)} %slice.277), channel_id=1, source_target_pairs={{0,16},{8,24},{16,0},{24,8},{1,17},{9,25},{17,1},{25,9},{2,18},{10... | collective-permute-start | bytes 2359304 | tf_op jit(solution)/shard_map/ppermute | solution.py:247
  41.0 13.7 %collective-permute-start.5 = (bf16[128,1024]{1,0:T(8,128)(2,1)S(1)}, bf16[128,1024]{1,0:T(8,128)(2,1)S(1)}, u32[]{:S(2)}, u32[]{:S(2)}) collective-permute-start(bf16[128,1024]{1,0:T(8,128)(2,1)S(1)} %pad_maximum_fusion.22.refs_0_), channel_id=1, source_target_pairs={{0,2},{1,3},{2,4},{3,5},{4,6},{5,7},{6,0},{7,1},{8,10},{9,11},{10,... | collective-permute-start | bytes 786440 | tf_op jit(solution)/shard_map/ppermute | solution.py:296
  46.4 17.4 %collective-permute-start.6 = (bf16[128,1024]{1,0:T(8,128)(2,1)S(1)}, bf16[128,1024]{1,0:T(8,128)(2,1)}, u32[]{:S(2)}, u32[]{:S(2)}) collective-permute-start(bf16[128,1024]{1,0:T(8,128)(2,1)S(1)} %pad_maximum_fusion.22.refs_0_), channel_id=1, source_target_pairs={{0,4},{1,5},{2,6},{3,7},{4,0},{5,1},{6,2},{7,3},{8,12},{9,13},{10,... | collective-permute-start | bytes 786440 | tf_op jit(solution)/shard_map/ppermute | solution.py:296
  48.0 15.8 %collective-permute-start.7 = (bf16[128,1024]{1,0:T(8,128)(2,1)S(1)}, bf16[128,1024]{1,0:T(8,128)(2,1)}, u32[]{:S(2)}, u32[]{:S(2)}) collective-permute-start(bf16[128,1024]{1,0:T(8,128)(2,1)S(1)} %pad_maximum_fusion.22.refs_0_), channel_id=1, source_target_pairs={{0,6},{1,7},{2,0},{3,1},{4,2},{5,3},{6,4},{7,5},{8,14},{9,15},{10,... | collective-permute-start | bytes 786440 | tf_op jit(solution)/shard_map/ppermute | solution.py:296
  63.8 254.8 %reduce-scatter.3.cloned.1.call-start = ((), (), s32[]{:S(2)}) async-start(), calls=%async_computation.3 | async-start | bytes 6488064 | tf_op jit(solution)/shard_map/reduce_scatter | solution.py:287
  63.9 2.2 collective-permute-start.1
  64.0 9.9 %collective-permute-start = (bf16[512,1024]{1,0:T(8,128)(2,1)S(1)}, bf16[512,1024]{1,0:T(8,128)(2,1)}, u32[]{:S(2)}, u32[]{:S(2)}) collective-permute-start(bf16[512,1024]{1,0:T(8,128)(2,1)S(1)} %bitcast.92), channel_id=1, source_target_pairs={{0,8},{8,0},{16,24},{24,16},{1,9},{9,1},{17,25},{25,17},{2,10},{10... | collective-permute-start | bytes 3145736 | tf_op jit(solution)/shard_map/ppermute | solution.py:244
  65.4 51.1 %collective-permute-start.12 = (bf16[512,512]{1,0:T(8,128)(2,1)}, bf16[512,512]{1,0:T(8,128)(2,1)S(1)}, u32[]{:S(2)}, u32[]{:S(2)}) collective-permute-start(bf16[512,512]{1,0:T(8,128)(2,1)} %get-tuple-element.162), channel_id=1, source_target_pairs={{0,8},{8,0},{16,24},{24,16},{1,9},{9,1},{17,25},{25,17},{2,10},{10... | collective-permute-start | bytes 1572872 | tf_op jit(solution)/shard_map/ppermute | solution.py:244
  72.7 20.7 %collective-permute-start.11 = (bf16[4,128,768]{2,1,0:T(8,128)(2,1)}, bf16[4,128,768]{2,1,0:T(8,128)(2,1)}, u32[]{:S(2)}, u32[]{:S(2)}) collective-permute-start(bf16[4,128,768]{2,1,0:T(8,128)(2,1)} %slice.220), channel_id=1, source_target_pairs={{0,16},{8,24},{16,0},{24,8},{1,17},{9,25},{17,1},{25,9},{2,18},{10... | collective-permute-start | bytes 2359304 | tf_op jit(solution)/shard_map/ppermute | solution.py:247
  75.7 33.4 %collective-permute-start.10 = (bf16[4,128,1024]{2,1,0:T(8,128)(2,1)S(1)}, bf16[4,128,1024]{2,1,0:T(8,128)(2,1)}, u32[]{:S(2)}, u32[]{:S(2)}) collective-permute-start(bf16[4,128,1024]{2,1,0:T(8,128)(2,1)S(1)} %copy-done.9), channel_id=1, source_target_pairs={{0,1},{1,0},{2,3},{3,2},{4,5},{5,4},{6,7},{7,6},{8,9},{9,8},{10,11... | collective-permute-start | bytes 3145736 | tf_op jit(solution)/shard_map/ppermute | solution.py:293
  76.4 62.2 %collective-permute-start.13 = (bf16[4,128,896]{2,1,0:T(8,128)(2,1)}, bf16[4,128,896]{2,1,0:T(8,128)(2,1)}, u32[]{:S(2)}, u32[]{:S(2)}) collective-permute-start(bf16[4,128,896]{2,1,0:T(8,128)(2,1)} %slice.278), channel_id=1, source_target_pairs={{0,16},{8,24},{16,0},{24,8},{1,17},{9,25},{17,1},{25,9},{2,18},{10... | collective-permute-start | bytes 2752520 | tf_op jit(solution)/shard_map/ppermute | solution.py:247
  110.4 28.3 %collective-permute-start.14 = (bf16[4,128,896]{2,1,0:T(8,128)(2,1)S(1)}, bf16[4,128,896]{2,1,0:T(8,128)(2,1)}, u32[]{:S(2)}, u32[]{:S(2)}) collective-permute-start(bf16[4,128,896]{2,1,0:T(8,128)(2,1)S(1)} %slice.225), channel_id=1, source_target_pairs={{0,16},{8,24},{16,0},{24,8},{1,17},{9,25},{17,1},{25,9},{2,18},{10... | collective-permute-start | bytes 2752520 | tf_op jit(solution)/shard_map/ppermute | solution.py:247
  144.6 2.1 collective-permute-start.15
  152.8 2.9 collective-permute-start.16
  153.0 25.9 %collective-permute-start.20 = (bf16[512,1024]{1,0:T(8,128)(2,1)}, bf16[512,1024]{1,0:T(8,128)(2,1)}, u32[]{:S(2)}, u32[]{:S(2)}) collective-permute-start(bf16[512,1024]{1,0:T(8,128)(2,1)} %bitcast.26), channel_id=1, source_target_pairs={{0,8},{8,0},{16,24},{24,16},{1,9},{9,1},{17,25},{25,17},{2,10},{10... | collective-permute-start | bytes 3145736 | tf_op jit(solution)/shard_map/ppermute | solution.py:244
  159.6 12.3 %collective-permute-start.17 = (bf16[512,1024]{1,0:T(8,128)(2,1)}, bf16[512,1024]{1,0:T(8,128)(2,1)}, u32[]{:S(2)}, u32[]{:S(2)}) collective-permute-start(bf16[512,1024]{1,0:T(8,128)(2,1)} %multiply_convert_fusion.4), channel_id=1, source_target_pairs={{0,8},{8,0},{16,24},{24,16},{1,9},{9,1},{17,25},{25,17},{2,10},{10... | collective-permute-start | bytes 3145736 | tf_op jit(solution)/shard_map/ppermute | solution.py:244
  167.1 10.7 %collective-permute-start.18 = (bf16[512,1536]{1,0:T(8,128)(2,1)S(1)}, bf16[512,1536]{1,0:T(8,128)(2,1)S(1)}, u32[]{:S(2)}, u32[]{:S(2)}) collective-permute-start(bf16[512,1536]{1,0:T(8,128)(2,1)S(1)} %constant_dynamic-slice_fusion.7), channel_id=1, source_target_pairs={{0,8},{8,0},{16,24},{24,16},{1,9},{9,1},{17,25},{25,17},{2,10},{10... | collective-permute-start | bytes 4718600 | tf_op jit(solution)/shard_map/ppermute | solution.py:244
  209.2 185.7 %reduce-scatter.5.cloned.1.call-start = ((), (), s32[]{:S(2)}) async-start(), calls=%async_computation.4 | async-start | bytes 2654208 | tf_op jit(solution)/shard_map/reduce_scatter | solution.py:287
  221.3 9.4 %collective-permute-start.21 = (bf16[512,1024]{1,0:T(8,128)(2,1)S(1)}, bf16[512,1024]{1,0:T(8,128)(2,1)S(1)}, u32[]{:S(2)}, u32[]{:S(2)}) collective-permute-start(bf16[512,1024]{1,0:T(8,128)(2,1)S(1)} %slice.429), channel_id=1, source_target_pairs={{0,8},{8,0},{16,24},{24,16},{1,9},{9,1},{17,25},{25,17},{2,10},{10... | collective-permute-start | bytes 3145736 | tf_op jit(solution)/shard_map/ppermute | solution.py:244
  225.0 6.5 %collective-permute-start.19 = (bf16[512,1024]{1,0:T(8,128)(2,1)S(1)}, bf16[512,1024]{1,0:T(8,128)(2,1)S(1)}, u32[]{:S(2)}, u32[]{:S(2)}) collective-permute-start(bf16[512,1024]{1,0:T(8,128)(2,1)S(1)} %slice.430), channel_id=1, source_target_pairs={{0,8},{8,0},{16,24},{24,16},{1,9},{9,1},{17,25},{25,17},{2,10},{10... | collective-permute-start | bytes 3145736 | tf_op jit(solution)/shard_map/ppermute | solution.py:244
  230.5 5.4 %collective-permute-start.28 = (bf16[1408,512]{1,0:T(8,128)(2,1)S(1)}, bf16[1408,512]{1,0:T(8,128)(2,1)S(1)}, u32[]{:S(2)}, u32[]{:S(2)}) collective-permute-start(bf16[1408,512]{1,0:T(8,128)(2,1)S(1)} %constant_dynamic-slice_fusion.4), channel_id=1, source_target_pairs={{0,8},{8,0},{16,24},{24,16},{1,9},{9,1},{17,25},{25,17},{2,10},{10... | collective-permute-start | bytes 4325384 | tf_op jit(solution)/shard_map/ppermute | solution.py:244
  235.4 4.1 collective-permute-start.22
  238.0 80.6 %collective-permute-start.29 = (bf16[2816,256]{1,0:T(8,128)(2,1)}, bf16[2816,256]{1,0:T(8,128)(2,1)}, u32[]{:S(2)}, u32[]{:S(2)}) collective-permute-start(bf16[2816,256]{1,0:T(8,128)(2,1)} %get-tuple-element.141), channel_id=1, source_target_pairs={{0,16},{8,24},{16,0},{24,8},{1,17},{9,25},{17,1},{25,9},{2,18},{10... | collective-permute-start | bytes 4325384 | tf_op jit(solution)/shard_map/ppermute | solution.py:247
  242.1 35.4 %copy-start.17 = (bf16[1,512,1024]{2,1,0:T(8,128)(2,1)S(1)}, bf16[1,512,1024]{2,1,0:T(8,128)(2,1)}, u32[]{:S(2)}) copy-start(bf16[1,512,1024]{2,1,0:T(8,128)(2,1)} %param.14) | copy-start | bytes 3145732
  287.5 27.3 %collective-permute-start.23 = (bf16[512,1024]{1,0:T(8,128)(2,1)S(1)}, bf16[512,1024]{1,0:T(8,128)(2,1)S(1)}, u32[]{:S(2)}, u32[]{:S(2)}) collective-permute-start(bf16[512,1024]{1,0:T(8,128)(2,1)S(1)} %slice.428), channel_id=1, source_target_pairs={{0,8},{8,0},{16,24},{24,16},{1,9},{9,1},{17,25},{25,17},{2,10},{10... | collective-permute-start | bytes 3145736 | tf_op jit(solution)/shard_map/ppermute | solution.py:244
  287.7 14.9 %collective-permute-start.25 = (bf16[1024,256]{1,0:T(8,128)(2,1)S(1)}, bf16[1024,256]{1,0:T(8,128)(2,1)S(1)}, u32[]{:S(2)}, u32[]{:S(2)}) collective-permute-start(bf16[1024,256]{1,0:T(8,128)(2,1)S(1)} %constant_dynamic-slice_fusion.5), channel_id=1, source_target_pairs={{0,16},{8,24},{16,0},{24,8},{1,17},{9,25},{17,1},{25,9},{2,18},{10... | collective-permute-start | bytes 1572872 | tf_op jit(solution)/shard_map/ppermute | solution.py:247
  292.1 4.2 %collective-permute-start.30 = (bf16[512,512]{1,0:T(8,128)(2,1)S(1)}, bf16[512,512]{1,0:T(8,128)(2,1)S(1)}, u32[]{:S(2)}, u32[]{:S(2)}) collective-permute-start(bf16[512,512]{1,0:T(8,128)(2,1)S(1)} %constant_dynamic-slice_fusion.3), channel_id=1, source_target_pairs={{0,8},{8,0},{16,24},{24,16},{1,9},{9,1},{17,25},{25,17},{2,10},{10... | collective-permute-start | bytes 1572872 | tf_op jit(solution)/shard_map/ppermute | solution.py:244
  292.2 21.6 %collective-permute-start.24 = (bf16[1024,256]{1,0:T(8,128)(2,1)S(1)}, bf16[1024,256]{1,0:T(8,128)(2,1)S(1)}, u32[]{:S(2)}, u32[]{:S(2)}) collective-permute-start(bf16[1024,256]{1,0:T(8,128)(2,1)S(1)} %constant_dynamic-slice_fusion.6), channel_id=1, source_target_pairs={{0,16},{8,24},{16,0},{24,8},{1,17},{9,25},{17,1},{25,9},{2,18},{10... | collective-permute-start | bytes 1572872 | tf_op jit(solution)/shard_map/ppermute | solution.py:247
  296.3 18.4 %collective-permute-start.40 = (bf16[512,512]{1,0:T(8,128)(2,1)S(1)}, bf16[512,512]{1,0:T(8,128)(2,1)S(1)}, u32[]{:S(2)}, u32[]{:S(2)}) collective-permute-start(bf16[512,512]{1,0:T(8,128)(2,1)S(1)} %slice.273), channel_id=1, source_target_pairs={{0,8},{8,0},{16,24},{24,16},{1,9},{9,1},{17,25},{25,17},{2,10},{10... | collective-permute-start | bytes 1572872 | tf_op jit(solution)/shard_map/ppermute | solution.py:244
  302.5 22.1 %collective-permute-start.31 = (bf16[1024,256]{1,0:T(8,128)(2,1)}, bf16[1024,256]{1,0:T(8,128)(2,1)}, u32[]{:S(2)}, u32[]{:S(2)}) collective-permute-start(bf16[1024,256]{1,0:T(8,128)(2,1)} %get-tuple-element.157), channel_id=1, source_target_pairs={{0,16},{8,24},{16,0},{24,8},{1,17},{9,25},{17,1},{25,9},{2,18},{10... | collective-permute-start | bytes 1572872 | tf_op jit(solution)/shard_map/ppermute | solution.py:247
  324.6 17.9 %collective-permute-start.38 = (bf16[128,2816]{1,0:T(8,128)(2,1)}, bf16[128,2816]{1,0:T(8,128)(2,1)S(1)}, u32[]{:S(2)}, u32[]{:S(2)}) collective-permute-start(bf16[128,2816]{1,0:T(8,128)(2,1)} %reduce-scatter.3.cloned.1.call-done), channel_id=1, source_target_pairs={{0,16},{8,24},{16,0},{24,8},{1,17},{9,25},{17,1},{25,9},{2,18},{10... | collective-permute-start | bytes 2162696 | tf_op jit(solution)/shard_map/ppermute | solution.py:247
  328.2 30.3 %collective-permute-start.32 = (bf16[4,480,256]{2,1,0:T(8,128)(2,1)S(1)}, bf16[4,480,256]{2,1,0:T(8,128)(2,1)S(1)}, u32[]{:S(2)}, u32[]{:S(2)}) collective-permute-start(bf16[4,480,256]{2,1,0:T(8,128)(2,1)S(1)} %fusion.34), channel_id=1, source_target_pairs={{0,1},{1,0},{2,3},{3,2},{4,5},{5,4},{6,7},{7,6},{8,9},{9,8},{10,11... | collective-permute-start | bytes 2949128 | tf_op jit(solution)/shard_map/ppermute | solution.py:293
  328.9 34.8 %copy-start.6 = (f32[1024,1024]{1,0:T(8,128)S(1)}, f32[1024,1024]{1,0:T(8,128)}, u32[]{:S(2)}) copy-start(f32[1024,1024]{1,0:T(8,128)} %copy-done.5) | copy-start | bytes 12582916
  344.0 39.1 %collective-permute-start.39 = (bf16[128,2816]{1,0:T(8,128)(2,1)S(1)}, bf16[128,2816]{1,0:T(8,128)(2,1)S(1)}, u32[]{:S(2)}, u32[]{:S(2)}) collective-permute-start(bf16[128,2816]{1,0:T(8,128)(2,1)S(1)} %add_convert_fusion.1), channel_id=1, source_target_pairs={{0,8},{8,0},{16,24},{24,16},{1,9},{9,1},{17,25},{25,17},{2,10},{10... | collective-permute-start | bytes 2162696 | tf_op jit(solution)/shard_map/ppermute | solution.py:244
  358.8 9.3 %collective-permute-start.35 = (bf16[480,256]{1,0:T(8,128)(2,1)S(1)}, bf16[480,256]{1,0:T(8,128)(2,1)S(1)}, u32[]{:S(2)}, u32[]{:S(2)}) collective-permute-start(bf16[480,256]{1,0:T(8,128)(2,1)S(1)} %get-tuple-element.166), channel_id=1, source_target_pairs={{0,6},{1,7},{2,0},{3,1},{4,2},{5,3},{6,4},{7,5},{8,14},{9,15},{10,... | collective-permute-start | bytes 737288 | tf_op jit(solution)/shard_map/ppermute | solution.py:296
  361.7 19.3 %collective-permute-start.34 = (bf16[480,256]{1,0:T(8,128)(2,1)S(1)}, bf16[480,256]{1,0:T(8,128)(2,1)S(1)}, u32[]{:S(2)}, u32[]{:S(2)}) collective-permute-start(bf16[480,256]{1,0:T(8,128)(2,1)S(1)} %get-tuple-element.167), channel_id=1, source_target_pairs={{0,4},{1,5},{2,6},{3,7},{4,0},{5,1},{6,2},{7,3},{8,12},{9,13},{10,... | collective-permute-start | bytes 737288 | tf_op jit(solution)/shard_map/ppermute | solution.py:296
  361.7 19.3 %collective-permute-start.33 = (bf16[480,256]{1,0:T(8,128)(2,1)S(1)}, bf16[480,256]{1,0:T(8,128)(2,1)S(1)}, u32[]{:S(2)}, u32[]{:S(2)}) collective-permute-start(bf16[480,256]{1,0:T(8,128)(2,1)S(1)} %get-tuple-element.165), channel_id=1, source_target_pairs={{0,2},{1,3},{2,4},{3,5},{4,6},{5,7},{6,0},{7,1},{8,10},{9,11},{10,... | collective-permute-start | bytes 737288 | tf_op jit(solution)/shard_map/ppermute | solution.py:296
  381.2 15.2 %collective-permute-start.36 = (bf16[480,256]{1,0:T(8,128)(2,1)S(1)}, bf16[480,256]{1,0:T(8,128)(2,1)S(1)}, u32[]{:S(2)}, u32[]{:S(2)}) collective-permute-start(bf16[480,256]{1,0:T(8,128)(2,1)S(1)} %fusion.44), channel_id=1, source_target_pairs={{0,16},{8,24},{16,0},{24,8},{1,17},{9,25},{17,1},{25,9},{2,18},{10... | collective-permute-start | bytes 737288 | tf_op jit(solution)/shard_map/ppermute | solution.py:247
  394.9 7.8 %collective-permute-start.26 = (bf16[128,1152]{1,0:T(8,128)(2,1)}, bf16[128,1152]{1,0:T(8,128)(2,1)S(1)}, u32[]{:S(2)}, u32[]{:S(2)}) collective-permute-start(bf16[128,1152]{1,0:T(8,128)(2,1)} %reduce-scatter.5.cloned.1.call-done), channel_id=1, source_target_pairs={{0,16},{8,24},{16,0},{24,8},{1,17},{9,25},{17,1},{25,9},{2,18},{10... | collective-permute-start | bytes 884744 | tf_op jit(solution)/shard_map/ppermute | solution.py:247
  396.5 8.2 %collective-permute-start.37 = (bf16[480,512]{1,0:T(8,128)(2,1)S(1)}, bf16[480,512]{1,0:T(8,128)(2,1)S(1)}, u32[]{:S(2)}, u32[]{:S(2)}) collective-permute-start(bf16[480,512]{1,0:T(8,128)(2,1)S(1)} %pad_maximum_fusion.21), channel_id=1, source_target_pairs={{0,8},{8,0},{16,24},{24,16},{1,9},{9,1},{17,25},{25,17},{2,10},{10... | collective-permute-start | bytes 1474568 | tf_op jit(solution)/shard_map/ppermute | solution.py:244
  404.6 2.4 collective-permute-start.27
  (45 other events, 337.7 us)
Sparse Core Ops, SparseCore 0:
  64.0 100.8 all-gather.1
  209.3 108.8 reduce-scatter.2
  321.7 73.1 reduce-scatter.4

commit v6 on v5

--- a/solution.py
+++ b/solution.py
@@ -344,7 +344,6 @@
     else:
         whole_a = gather(shard_a)
     whole_c = gather(shard_c)
-    up_mat, whole_d = whole_c[:, : w_up.shape[1] // 2], whole_c[:, w_up.shape[1] // 2 :]
     qkv_mat = whole_a[:, gains.shape[1] :]
     gain_rows = whole_a[:, : gains.shape[1]].reshape(fsdp, w_query.shape[0], -1)
     gain_one = gain_rows[:, 0, : attn_gain.shape[0]].reshape(1, width).astype(f32)
@@ -381,6 +380,10 @@
     mixed = hidden[:length] + mine_and_partner(dot_nn(attended, output_mat))
     inverse_two = norm_stats(mixed)
     normed_two = pair((mixed * inverse_two * gain_two).astype(bf16))
+    normed_two, whole_c, square_first, square_blend = tie(
+        (normed_two, whole_c, square_first, square_blend)
+    )
+    up_mat, whole_d = whole_c[:, : w_up.shape[1] // 2], whole_c[:, w_up.shape[1] // 2 :]
     gate = dot_nn(normed_two, gate_mat)
     up_val = dot_nn(normed_two, up_mat)
 

time: 426 us -> 423 us (level)
  matrix products: 79.5 us -> 73.1 us
    dot_general x7, matrix products: 27.3 us -> 22.9 us  [dot_tn(): lax.dot_general(a, b, (((0,), (0,)), ((), ())), preferred_element_type=f32)]
where the time goes in v6:
time: 423 us; the launch traced here: 415 us
  waiting for transfers between devices  132 us (31%)
  matrix products  73.1 us (17%)
  Pallas kernels  69.4 us (16%)
  other arithmetic  53.6 us (13%)
  starting transfers between devices  38 us (9%)
  local copies, waits for them, and re-layouts  33.7 us (8%)
  between operations  15.3 us (4%)
    ppermute x11, waiting for transfers between devices, to_chip(): lax.ppermute(values, 'dp', [(i, (i + 2 * step) % dp) for i in range(dp)])  55.4 us
    ppermute x9, waiting for transfers between devices, around(): lax.ppermute(values, 'fsdp', [(i, (i + 2 * step) % fsdp) for i in range(f...  42 us
    pallas_call x1, Pallas kernels, attend_back(): pl.pallas_call(attend_back_kernel, grid=(tokens // length, width // LANES...  35.3 us
    dot_general x5, matrix products, dot_nn(): return jnp.dot(a, b, preferred_element_type=f32)  27 us
    dot_general x7, matrix products, dot_nt(): lax.dot_general(a, b, (((1,), (1,)), ((), ())), preferred_element_type=f32)  23.2 us
    dot_general x7, matrix products, dot_tn(): lax.dot_general(a, b, (((0,), (0,)), ((), ())), preferred_element_type=f32)  22.9 us
    pallas_call x1, Pallas kernels, attend(): pl.pallas_call(attend_kernel, grid=(tokens // length, pairs), in_specs=[p...  21.1 us
    ppermute x9, starting transfers between devices, around(): lax.ppermute(values, 'fsdp', [(i, (i + 2 * step) % fsdp) for i in range(f...  19.7 us
  transfers between devices with their start and end apart: 44, of which 18 were waited for; matrix products, arithmetic and copies ran while one was open for 28% of the time, Pallas kernels for 16%

profile of v6, /device:TPU:0, one launch (start us, length us, event | category | flops | bytes accessed | tf_op | source)
XLA Modules:
  0.0 414.9 jit_solution(13950399231659817199)
XLA Ops:
  10.1 3.1 collective-permute-start.2
  13.2 2.6 collective-permute-start.3
  18.4 3.5 collective-permute-done.2.refs_1_
  21.9 9.0 %collective-permute-done.3.refs_2_ = bf16[128,896]{1,0:T(8,128)(2,1)S(1)} collective-permute-done((bf16[128,896]{1,0:T(8,128)(2,1)S(1)}, bf16[128,896]{1,0:T(8,128)(2,1)S(1)}, u32[]{:S(2)}, u32[]{:S(2)}) %collective-permute-start.3) | collective-permute-done | bytes 229408 | tf_op jit(solution)/shard_map/ppermute | solution.py:296
  31.6 2.3 ring_order.2.mine_ref
  41.0 5.4 %collective-permute-start.5 = (bf16[128,1024]{1,0:T(8,128)(2,1)S(1)}, bf16[128,1024]{1,0:T(8,128)(2,1)S(1)}, u32[]{:S(2)}, u32[]{:S(2)}) collective-permute-start(bf16[128,1024]{1,0:T(8,128)(2,1)S(1)} %pad_maximum_fusion.22.refs_0_), channel_id=1, source_target_pairs={{0,2},{1,3},{2,4},{3,5},{4,6},{5,7},{6,0},{7,1},{8,10},{9,11},{10,... | collective-permute-start | bytes 786440 | tf_op jit(solution)/shard_map/ppermute | solution.py:296
  49.7 5.0 %collective-permute-done.5.refs_1_ = bf16[128,1024]{1,0:T(8,128)(2,1)S(1)} collective-permute-done((bf16[128,1024]{1,0:T(8,128)(2,1)S(1)}, bf16[128,1024]{1,0:T(8,128)(2,1)S(1)}, u32[]{:S(2)}, u32[]{:S(2)}) %collective-permute-start.5) | collective-permute-done | bytes 262176 | tf_op jit(solution)/shard_map/ppermute | solution.py:296
  54.7 9.1 %collective-permute-done.6.refs_2_ = bf16[128,1024]{1,0:T(8,128)(2,1)} collective-permute-done((bf16[128,1024]{1,0:T(8,128)(2,1)S(1)}, bf16[128,1024]{1,0:T(8,128)(2,1)}, u32[]{:S(2)}, u32[]{:S(2)}) %collective-permute-start.6) | collective-permute-done | bytes 262176 | tf_op jit(solution)/shard_map/ppermute | solution.py:296
  66.1 2.1 slice.220
  68.2 2.2 ring_order.3.mine_ref
  70.4 2.3 slice.278
  77.7 15.7 %collective-permute-done.11.far_other_ref = bf16[4,128,768]{2,1,0:T(8,128)(2,1)} collective-permute-done((bf16[4,128,768]{2,1,0:T(8,128)(2,1)}, bf16[4,128,768]{2,1,0:T(8,128)(2,1)}, u32[]{:S(2)}, u32[]{:S(2)}) %collective-permute-start.11) | collective-permute-done | bytes 786464 | tf_op jit(solution)/shard_map/ppermute | solution.py:247
  93.4 4.0 joined.2
  98.4 8.3 %fusion.2.q_ref.k_ref.v_ref = f32[1024,1536]{1,0:T(8,128)} fusion(bf16[1024,1664]{1,0:T(8,128)(2,1)} %bitcast.87, f32[1024]{0:T(1024)S(1)} %bitcast.117, f32[1024]{0:T(1024)S(1)} %add_rsqrt_fusion, bf16[512,1024]{1,0:T(8,128)(2,1)} %collective-permute-done, bf16[512,1024]{1,0:T(8,128)(2,1)S(1)} %bitcast.98), kind=kOutput, calls=%fused_computation.18 | convolution fusion | flops 3228565504 | bytes 11542528 | tf_op jit(solution)/shard_map/dot_general | solution.py:66
  106.7 2.5 collective-permute-done.10.far_ref
  113.4 3.0 fusion.39
  117.5 21.1 %attend.1 = (bf16[1024,512]{1,0:T(8,128)(2,1)}, bf16[1024,512]{1,0:T(8,128)(2,1)}, bf16[1024,512]{1,0:T(8,128)(2,1)}, bf16[1024,512]{1,0:T(8,128)(2,1)}) custom-call(s32[1024,1]{1,0:T(8,128)} %copy.37.start_ref, f32[1024,128]{1,0:T(8,128)} %get-tuple-element.191.cos_ref, f32[1024,128]{1,0:T(8,128)} %get-tuple-element.190.sin_ref, ...), custom_call_target="tpu_custom_call" | custom-call | tf_op jit(solution)/shard_map/attend/pallas_call | solution.py:145
  138.7 4.5 %joined.3 = bf16[4,2,128,1920]{3,2,1,0:T(8,128)(2,1)} custom-call(s32[2]{0:T(128)} %pad_add_fusion.2.at_ref, bf16[4,128,1024]{2,1,0:T(8,128)(2,1)} %ring_order.3.mine_ref, bf16[4,128,1024]{2,1,0:T(8,128)(2,1)} %collective-permute-done.10.far_ref, bf16[4,128,896]{2,1,0:T(8,128)(2,1)} %collective-permute-done.13.mine_other_ref, ...), custom_call_target="tpu_custom_call" | custom-call | tf_op jit(solution)/shard_map/joined/pallas_call | solution.py:209
  147.9 2.7 fusion.38
  159.6 5.2 %all-gather.2.cloned.1.call-done = bf16[1024,2944]{1,0:T(8,128)(2,1)} async-done(((bf16[128,2944]{1,0:T(8,128)(2,1)}), bf16[1024,2944]{1,0:T(8,128)(2,1)}) %all-gather.2.cloned.1.call-update) | async-done | bytes 6029328 | tf_op jit(solution)/shard_map/all_gather | solution.py:284
  164.8 2.1 slice.232
  173.4 5.2 %fusion.10 = f32[1024,1408]{1,0:T(8,128)S(1)} fusion(bf16[1024,1024]{1,0:T(8,128)(2,1)S(1)} %copy-done.21, bf16[1024,2944]{1,0:T(8,128)(2,1)} %all-gather.2.cloned.1.call-done), kind=kOutput, calls=%fused_computation.28 | convolution fusion | flops 2952790016 | bytes 10747904 | tf_op jit(solution)/shard_map/dot_general | solution.py:66
  182.7 5.1 %fusion.20 = f32[1024,1408]{1,0:T(8,128)S(1)} fusion(bf16[1408,512]{1,0:T(8,128)(2,1)S(1)} %bitcast.111, bf16[1408,512]{1,0:T(8,128)(2,1)S(1)} %bitcast.109, bf16[512,1024]{1,0:T(8,128)(2,1)} %collective-permute-done.20, bf16[512,1024]{1,0:T(8,128)(2,1)} %bitcast.26), kind=kOutput, calls=%fused_computation.65 | convolution fusion | flops 2962751488 | bytes 10747904 | tf_op jit(solution)/shard_map/dot_general | solution.py:58
  187.9 7.4 %multiply_convert_fusion.1 = (bf16[1024,1408]{1,0:T(8,128)(2,1)}, bf16[1024,1408]{1,0:T(8,128)(2,1)S(1)}, bf16[1024,1408]{1,0:T(8,128)(2,1)}) fusion(f32[1024,1408]{1,0:T(8,128)S(1)} %fusion.20, f32[1024,1408]{1,0:T(8,128)S(1)} %fusion.10, bf16[1024,1024]{1,0:T(8,128)(2,1)S(1)} %copy-done.21, bf16[1024,1920]{1,0:T(8,128)(2,1)S(1)} %bitcast.93), kind=kOutput, calls=%fused_computation.2 | convolution fusion | flops 2974416896 | bytes 25165824 | tf_op jit(solution)/shard_map/dot_general | solution.py:66
  195.3 3.7 convolution_convert_fusion.1
  199.0 3.7 convolution_convert_fusion.2
  202.8 2.9 pad_maximum_fusion
  205.9 6.3 %fusion.4 = f32[1024,1024]{1,0:T(8,128)S(1)} fusion(bf16[1024,1408]{1,0:T(8,128)(2,1)} %get-tuple-element.96, bf16[1024,1920]{1,0:T(8,128)(2,1)} %bitcast.92), kind=kOutput, calls=%fused_computation.22 | convolution fusion | flops 2952790016 | bytes 9961472 | tf_op jit(solution)/shard_map/dot_general | solution.py:58
  212.2 5.4 %fusion.17 = f32[1024,1024]{1,0:T(8,128)S(1)} fusion(f32[1024,1024]{1,0:T(8,128)S(1)} %fusion.4, bf16[1024,1408]{1,0:T(8,128)(2,1)S(1)} %copy-done.47, bf16[1024,2944]{1,0:T(8,128)(2,1)} %all-gather.2.cloned.1.call-done), kind=kOutput, calls=%fused_computation.64 | convolution fusion | flops 2953838592 | bytes 14155776 | tf_op jit(solution)/shard_map/dot_general | solution.py:58
  218.0 3.4 fusion.21
  222.1 4.8 %convolution_convert_fusion = bf16[1408,1024]{1,0:T(8,128)(2,1)S(1)} fusion(bf16[1024,1408]{1,0:T(8,128)(2,1)S(1)} %copy-done.45, bf16[512,1024]{1,0:T(8,128)(2,1)} %collective-permute-done.20, bf16[512,1024]{1,0:T(8,128)(2,1)} %bitcast.26), kind=kOutput, calls=%fused_computation.11 | convolution fusion | flops 2958426112 | bytes 7864320 | tf_op jit(solution)/shard_map/dot_general | solution.py:62
  228.0 3.9 fusion.67
  236.1 2.5 convolution_convert_fusion.7.grad_ref
  238.6 35.3 %attend_back.1 = (bf16[1024,512]{1,0:T(8,128)(2,1)}, bf16[1024,512]{1,0:T(8,128)(2,1)}, bf16[1024,512]{1,0:T(8,128)(2,1)}) custom-call(s32[1024,1]{1,0:T(8,128)} %copy.37.start_ref, f32[1024,128]{1,0:T(8,128)} %get-tuple-element.191.cos_ref, f32[1024,128]{1,0:T(8,128)} %get-tuple-element.190.sin_ref, bf16[1024,512]{1,0:T(8,128)(2,1)} %get-tuple-element.98.q_rot_ref, ...), custom_call_target="tpu_custom_call" | custom-call | tf_op jit(solution)/shard_map/attend_back/pallas_call | solution.py:159
  273.9 3.0 convolution_convert_fusion.6
  277.0 2.8 convolution_convert_fusion.5
  289.2 3.6 convolution_convert_fusion.4
  294.2 4.7 %collective-permute-done.25 = bf16[1024,256]{1,0:T(8,128)(2,1)S(1)} collective-permute-done((bf16[1024,256]{1,0:T(8,128)(2,1)S(1)}, bf16[1024,256]{1,0:T(8,128)(2,1)S(1)}, u32[]{:S(2)}, u32[]{:S(2)}) %collective-permute-start.25) | collective-permute-done | bytes 524320 | tf_op jit(solution)/shard_map/ppermute | solution.py:247
  299.6 10.6 %collective-permute-done.24 = bf16[1024,256]{1,0:T(8,128)(2,1)S(1)} collective-permute-done((bf16[1024,256]{1,0:T(8,128)(2,1)S(1)}, bf16[1024,256]{1,0:T(8,128)(2,1)S(1)}, u32[]{:S(2)}, u32[]{:S(2)}) %collective-permute-start.24) | collective-permute-done | bytes 524320 | tf_op jit(solution)/shard_map/ppermute | solution.py:247
  312.5 2.7 fusion.12
  315.2 5.9 %collective-permute-done.31 = bf16[1024,256]{1,0:T(8,128)(2,1)} collective-permute-done((bf16[1024,256]{1,0:T(8,128)(2,1)}, bf16[1024,256]{1,0:T(8,128)(2,1)}, u32[]{:S(2)}, u32[]{:S(2)}) %collective-permute-start.31) | collective-permute-done | bytes 524320 | tf_op jit(solution)/shard_map/ppermute | solution.py:247
  327.0 12.0 %collective-permute-done.38 = bf16[128,2816]{1,0:T(8,128)(2,1)S(1)} collective-permute-done((bf16[128,2816]{1,0:T(8,128)(2,1)}, bf16[128,2816]{1,0:T(8,128)(2,1)S(1)}, u32[]{:S(2)}, u32[]{:S(2)}) %collective-permute-start.38) | collective-permute-done | bytes 720928 | tf_op jit(solution)/shard_map/ppermute | solution.py:247
  340.5 14.5 %collective-permute-done.32 = bf16[4,480,256]{2,1,0:T(8,128)(2,1)S(1)} collective-permute-done((bf16[4,480,256]{2,1,0:T(8,128)(2,1)S(1)}, bf16[4,480,256]{2,1,0:T(8,128)(2,1)S(1)}, u32[]{:S(2)}, u32[]{:S(2)}) %collective-permute-start.32) | collective-permute-done | bytes 983072 | tf_op jit(solution)/shard_map/ppermute | solution.py:293
  355.3 3.1 collective-permute-start.35
  362.1 2.6 collective-permute-done.35
  364.7 12.9 %collective-permute-done.34 = bf16[480,256]{1,0:T(8,128)(2,1)S(1)} collective-permute-done((bf16[480,256]{1,0:T(8,128)(2,1)S(1)}, bf16[480,256]{1,0:T(8,128)(2,1)S(1)}, u32[]{:S(2)}, u32[]{:S(2)}) %collective-permute-start.34) | collective-permute-done | bytes 245792 | tf_op jit(solution)/shard_map/ppermute | solution.py:296
  382.1 9.3 %reduce-scatter.5.cloned.1.call-done = bf16[128,1152]{1,0:T(8,128)(2,1)} async-done(((bf16[1024,1152]{1,0:T(8,128)(2,1)}), bf16[128,1152]{1,0:T(8,128)(2,1)}) %reduce-scatter.5.cloned.1.call-update) | async-done | bytes 294928 | tf_op jit(solution)/shard_map/reduce_scatter | solution.py:287
  393.1 6.4 %collective-permute-done.26 = bf16[128,1152]{1,0:T(8,128)(2,1)S(1)} collective-permute-done((bf16[128,1152]{1,0:T(8,128)(2,1)}, bf16[128,1152]{1,0:T(8,128)(2,1)S(1)}, u32[]{:S(2)}, u32[]{:S(2)}) %collective-permute-start.26) | collective-permute-done | bytes 294944 | tf_op jit(solution)/shard_map/ppermute | solution.py:247
  (289 shorter events, 100.3 us)
Async XLA Ops:
  7.2 157.6 %all-gather.2.cloned.1.call-start = ((), (), s32[]{:S(2)}) async-start(), calls=%async_computation.2 | async-start | bytes 6782976 | tf_op jit(solution)/shard_map/all_gather | solution.py:284
  10.1 11.7 %collective-permute-start.2 = (bf16[128,896]{1,0:T(8,128)(2,1)S(1)}, bf16[128,896]{1,0:T(8,128)(2,1)S(1)}, u32[]{:S(2)}, u32[]{:S(2)}) collective-permute-start(bf16[128,896]{1,0:T(8,128)(2,1)S(1)} %pad_maximum_fusion.23.refs_0_), channel_id=1, source_target_pairs={{0,2},{1,3},{2,4},{3,5},{4,6},{5,7},{6,0},{7,1},{8,10},{9,11},{10,... | collective-permute-start | bytes 688136 | tf_op jit(solution)/shard_map/ppermute | solution.py:296
  13.2 17.6 %collective-permute-start.3 = (bf16[128,896]{1,0:T(8,128)(2,1)S(1)}, bf16[128,896]{1,0:T(8,128)(2,1)S(1)}, u32[]{:S(2)}, u32[]{:S(2)}) collective-permute-start(bf16[128,896]{1,0:T(8,128)(2,1)S(1)} %pad_maximum_fusion.23.refs_0_), channel_id=1, source_target_pairs={{0,4},{1,5},{2,6},{3,7},{4,0},{5,1},{6,2},{7,3},{8,12},{9,13},{10,... | collective-permute-start | bytes 688136 | tf_op jit(solution)/shard_map/ppermute | solution.py:296
  15.8 15.0 %collective-permute-start.4 = (bf16[128,896]{1,0:T(8,128)(2,1)S(1)}, bf16[128,896]{1,0:T(8,128)(2,1)S(1)}, u32[]{:S(2)}, u32[]{:S(2)}) collective-permute-start(bf16[128,896]{1,0:T(8,128)(2,1)S(1)} %pad_maximum_fusion.23.refs_0_), channel_id=1, source_target_pairs={{0,6},{1,7},{2,0},{3,1},{4,2},{5,3},{6,4},{7,5},{8,14},{9,15},{10,... | collective-permute-start | bytes 688136 | tf_op jit(solution)/shard_map/ppermute | solution.py:296
  18.4 29.6 %copy-start.33 = (bf16[128,1024]{1,0:T(8,128)(2,1)}, bf16[128,1024]{1,0:T(8,128)(2,1)S(1)}, u32[]{:S(2)}) copy-start(bf16[128,1024]{1,0:T(8,128)(2,1)S(1)} %pad_maximum_fusion.22.refs_0_) | copy-start | bytes 786436
  35.9 28.5 %copy-start.13 = (bf16[1,512,1024]{2,1,0:T(8,128)(2,1)S(1)}, bf16[1,512,1024]{2,1,0:T(8,128)(2,1)}, u32[]{:S(2)}) copy-start(bf16[1,512,1024]{2,1,0:T(8,128)(2,1)} %param.15) | copy-start | bytes 3145732
  35.9 27.9 %collective-permute-start.8 = (bf16[4,128,896]{2,1,0:T(8,128)(2,1)}, bf16[4,128,896]{2,1,0:T(8,128)(2,1)}, u32[]{:S(2)}, u32[]{:S(2)}) collective-permute-start(bf16[4,128,896]{2,1,0:T(8,128)(2,1)} %ring_order.2.mine_ref), channel_id=1, source_target_pairs={{0,1},{1,0},{2,3},{3,2},{4,5},{5,4},{6,7},{7,6},{8,9},{9,8},{10,11... | collective-permute-start | bytes 2752520 | tf_op jit(solution)/shard_map/ppermute | solution.py:293
  37.5 26.4 %collective-permute-start.9 = (bf16[4,128,768]{2,1,0:T(8,128)(2,1)}, bf16[4,128,768]{2,1,0:T(8,128)(2,1)}, u32[]{:S(2)}, u32[]{:S(2)}) collective-permute-start(bf16[4,128,768]{2,1,0:T(8,128)(2,1)} %slice.277), channel_id=1, source_target_pairs={{0,16},{8,24},{16,0},{24,8},{1,17},{9,25},{17,1},{25,9},{2,18},{10... | collective-permute-start | bytes 2359304 | tf_op jit(solution)/shard_map/ppermute | solution.py:247
  41.0 13.7 %collective-permute-start.5 = (bf16[128,1024]{1,0:T(8,128)(2,1)S(1)}, bf16[128,1024]{1,0:T(8,128)(2,1)S(1)}, u32[]{:S(2)}, u32[]{:S(2)}) collective-permute-start(bf16[128,1024]{1,0:T(8,128)(2,1)S(1)} %pad_maximum_fusion.22.refs_0_), channel_id=1, source_target_pairs={{0,2},{1,3},{2,4},{3,5},{4,6},{5,7},{6,0},{7,1},{8,10},{9,11},{10,... | collective-permute-start | bytes 786440 | tf_op jit(solution)/shard_map/ppermute | solution.py:296
  46.4 17.4 %collective-permute-start.6 = (bf16[128,1024]{1,0:T(8,128)(2,1)S(1)}, bf16[128,1024]{1,0:T(8,128)(2,1)}, u32[]{:S(2)}, u32[]{:S(2)}) collective-permute-start(bf16[128,1024]{1,0:T(8,128)(2,1)S(1)} %pad_maximum_fusion.22.refs_0_), channel_id=1, source_target_pairs={{0,4},{1,5},{2,6},{3,7},{4,0},{5,1},{6,2},{7,3},{8,12},{9,13},{10,... | collective-permute-start | bytes 786440 | tf_op jit(solution)/shard_map/ppermute | solution.py:296
  48.0 15.8 %collective-permute-start.7 = (bf16[128,1024]{1,0:T(8,128)(2,1)S(1)}, bf16[128,1024]{1,0:T(8,128)(2,1)}, u32[]{:S(2)}, u32[]{:S(2)}) collective-permute-start(bf16[128,1024]{1,0:T(8,128)(2,1)S(1)} %pad_maximum_fusion.22.refs_0_), channel_id=1, source_target_pairs={{0,6},{1,7},{2,0},{3,1},{4,2},{5,3},{6,4},{7,5},{8,14},{9,15},{10,... | collective-permute-start | bytes 786440 | tf_op jit(solution)/shard_map/ppermute | solution.py:296
  63.8 251.3 %reduce-scatter.3.cloned.1.call-start = ((), (), s32[]{:S(2)}) async-start(), calls=%async_computation.3 | async-start | bytes 6488064 | tf_op jit(solution)/shard_map/reduce_scatter | solution.py:287
  63.9 2.2 collective-permute-start.1
  64.0 9.9 %collective-permute-start = (bf16[512,1024]{1,0:T(8,128)(2,1)S(1)}, bf16[512,1024]{1,0:T(8,128)(2,1)}, u32[]{:S(2)}, u32[]{:S(2)}) collective-permute-start(bf16[512,1024]{1,0:T(8,128)(2,1)S(1)} %bitcast.96), channel_id=1, source_target_pairs={{0,8},{8,0},{16,24},{24,16},{1,9},{9,1},{17,25},{25,17},{2,10},{10... | collective-permute-start | bytes 3145736 | tf_op jit(solution)/shard_map/ppermute | solution.py:244
  65.4 51.1 %collective-permute-start.12 = (bf16[512,512]{1,0:T(8,128)(2,1)}, bf16[512,512]{1,0:T(8,128)(2,1)S(1)}, u32[]{:S(2)}, u32[]{:S(2)}) collective-permute-start(bf16[512,512]{1,0:T(8,128)(2,1)} %get-tuple-element.170), channel_id=1, source_target_pairs={{0,8},{8,0},{16,24},{24,16},{1,9},{9,1},{17,25},{25,17},{2,10},{10... | collective-permute-start | bytes 1572872 | tf_op jit(solution)/shard_map/ppermute | solution.py:244
  72.7 20.7 %collective-permute-start.11 = (bf16[4,128,768]{2,1,0:T(8,128)(2,1)}, bf16[4,128,768]{2,1,0:T(8,128)(2,1)}, u32[]{:S(2)}, u32[]{:S(2)}) collective-permute-start(bf16[4,128,768]{2,1,0:T(8,128)(2,1)} %slice.220), channel_id=1, source_target_pairs={{0,16},{8,24},{16,0},{24,8},{1,17},{9,25},{17,1},{25,9},{2,18},{10... | collective-permute-start | bytes 2359304 | tf_op jit(solution)/shard_map/ppermute | solution.py:247
  75.7 33.4 %collective-permute-start.10 = (bf16[4,128,1024]{2,1,0:T(8,128)(2,1)S(1)}, bf16[4,128,1024]{2,1,0:T(8,128)(2,1)}, u32[]{:S(2)}, u32[]{:S(2)}) collective-permute-start(bf16[4,128,1024]{2,1,0:T(8,128)(2,1)S(1)} %copy-done.8), channel_id=1, source_target_pairs={{0,1},{1,0},{2,3},{3,2},{4,5},{5,4},{6,7},{7,6},{8,9},{9,8},{10,11... | collective-permute-start | bytes 3145736 | tf_op jit(solution)/shard_map/ppermute | solution.py:293
  76.4 62.2 %collective-permute-start.13 = (bf16[4,128,896]{2,1,0:T(8,128)(2,1)}, bf16[4,128,896]{2,1,0:T(8,128)(2,1)}, u32[]{:S(2)}, u32[]{:S(2)}) collective-permute-start(bf16[4,128,896]{2,1,0:T(8,128)(2,1)} %slice.278), channel_id=1, source_target_pairs={{0,16},{8,24},{16,0},{24,8},{1,17},{9,25},{17,1},{25,9},{2,18},{10... | collective-permute-start | bytes 2752520 | tf_op jit(solution)/shard_map/ppermute | solution.py:247
  110.4 28.3 %collective-permute-start.14 = (bf16[4,128,896]{2,1,0:T(8,128)(2,1)S(1)}, bf16[4,128,896]{2,1,0:T(8,128)(2,1)}, u32[]{:S(2)}, u32[]{:S(2)}) collective-permute-start(bf16[4,128,896]{2,1,0:T(8,128)(2,1)S(1)} %slice.225), channel_id=1, source_target_pairs={{0,16},{8,24},{16,0},{24,8},{1,17},{9,25},{17,1},{25,9},{2,18},{10... | collective-permute-start | bytes 2752520 | tf_op jit(solution)/shard_map/ppermute | solution.py:247
  144.5 2.1 collective-permute-start.15
  150.7 2.7 collective-permute-start.16
  154.9 3.2 collective-permute-start.17
  169.8 8.8 %collective-permute-start.18 = (bf16[512,1536]{1,0:T(8,128)(2,1)}, bf16[512,1536]{1,0:T(8,128)(2,1)}, u32[]{:S(2)}, u32[]{:S(2)}) collective-permute-start(bf16[512,1536]{1,0:T(8,128)(2,1)} %constant_dynamic-slice_fusion.7), channel_id=1, source_target_pairs={{0,8},{8,0},{16,24},{24,16},{1,9},{9,1},{17,25},{25,17},{2,10},{10... | collective-permute-start | bytes 4718600 | tf_op jit(solution)/shard_map/ppermute | solution.py:244
  169.8 11.3 %collective-permute-start.20 = (bf16[512,1024]{1,0:T(8,128)(2,1)}, bf16[512,1024]{1,0:T(8,128)(2,1)}, u32[]{:S(2)}, u32[]{:S(2)}) collective-permute-start(bf16[512,1024]{1,0:T(8,128)(2,1)} %bitcast.26), channel_id=1, source_target_pairs={{0,8},{8,0},{16,24},{24,16},{1,9},{9,1},{17,25},{25,17},{2,10},{10... | collective-permute-start | bytes 3145736 | tf_op jit(solution)/shard_map/ppermute | solution.py:244
  205.7 185.8 %reduce-scatter.5.cloned.1.call-start = ((), (), s32[]{:S(2)}) async-start(), calls=%async_computation.4 | async-start | bytes 2654208 | tf_op jit(solution)/shard_map/reduce_scatter | solution.py:287
  217.9 9.4 %collective-permute-start.21 = (bf16[512,1024]{1,0:T(8,128)(2,1)S(1)}, bf16[512,1024]{1,0:T(8,128)(2,1)S(1)}, u32[]{:S(2)}, u32[]{:S(2)}) collective-permute-start(bf16[512,1024]{1,0:T(8,128)(2,1)S(1)} %slice.427), channel_id=1, source_target_pairs={{0,8},{8,0},{16,24},{24,16},{1,9},{9,1},{17,25},{25,17},{2,10},{10... | collective-permute-start | bytes 3145736 | tf_op jit(solution)/shard_map/ppermute | solution.py:244
  221.5 6.5 %collective-permute-start.19 = (bf16[512,1024]{1,0:T(8,128)(2,1)S(1)}, bf16[512,1024]{1,0:T(8,128)(2,1)S(1)}, u32[]{:S(2)}, u32[]{:S(2)}) collective-permute-start(bf16[512,1024]{1,0:T(8,128)(2,1)S(1)} %slice.428), channel_id=1, source_target_pairs={{0,8},{8,0},{16,24},{24,16},{1,9},{9,1},{17,25},{25,17},{2,10},{10... | collective-permute-start | bytes 3145736 | tf_op jit(solution)/shard_map/ppermute | solution.py:244
  227.0 5.5 %collective-permute-start.28 = (bf16[1408,512]{1,0:T(8,128)(2,1)S(1)}, bf16[1408,512]{1,0:T(8,128)(2,1)S(1)}, u32[]{:S(2)}, u32[]{:S(2)}) collective-permute-start(bf16[1408,512]{1,0:T(8,128)(2,1)S(1)} %constant_dynamic-slice_fusion.4), channel_id=1, source_target_pairs={{0,8},{8,0},{16,24},{24,16},{1,9},{9,1},{17,25},{25,17},{2,10},{10... | collective-permute-start | bytes 4325384 | tf_op jit(solution)/shard_map/ppermute | solution.py:244
  231.9 4.1 collective-permute-start.22
  234.6 80.6 %collective-permute-start.29 = (bf16[2816,256]{1,0:T(8,128)(2,1)}, bf16[2816,256]{1,0:T(8,128)(2,1)}, u32[]{:S(2)}, u32[]{:S(2)}) collective-permute-start(bf16[2816,256]{1,0:T(8,128)(2,1)} %get-tuple-element.149), channel_id=1, source_target_pairs={{0,16},{8,24},{16,0},{24,8},{1,17},{9,25},{17,1},{25,9},{2,18},{10... | collective-permute-start | bytes 4325384 | tf_op jit(solution)/shard_map/ppermute | solution.py:247
  238.6 35.3 %copy-start.16 = (bf16[1,512,1024]{2,1,0:T(8,128)(2,1)S(1)}, bf16[1,512,1024]{2,1,0:T(8,128)(2,1)}, u32[]{:S(2)}) copy-start(bf16[1,512,1024]{2,1,0:T(8,128)(2,1)} %param.14) | copy-start | bytes 3145732
  284.0 27.3 %collective-permute-start.23 = (bf16[512,1024]{1,0:T(8,128)(2,1)S(1)}, bf16[512,1024]{1,0:T(8,128)(2,1)S(1)}, u32[]{:S(2)}, u32[]{:S(2)}) collective-permute-start(bf16[512,1024]{1,0:T(8,128)(2,1)S(1)} %slice.426), channel_id=1, source_target_pairs={{0,8},{8,0},{16,24},{24,16},{1,9},{9,1},{17,25},{25,17},{2,10},{10... | collective-permute-start | bytes 3145736 | tf_op jit(solution)/shard_map/ppermute | solution.py:244
  284.1 14.9 %collective-permute-start.25 = (bf16[1024,256]{1,0:T(8,128)(2,1)S(1)}, bf16[1024,256]{1,0:T(8,128)(2,1)S(1)}, u32[]{:S(2)}, u32[]{:S(2)}) collective-permute-start(bf16[1024,256]{1,0:T(8,128)(2,1)S(1)} %constant_dynamic-slice_fusion.5), channel_id=1, source_target_pairs={{0,16},{8,24},{16,0},{24,8},{1,17},{9,25},{17,1},{25,9},{2,18},{10... | collective-permute-start | bytes 1572872 | tf_op jit(solution)/shard_map/ppermute | solution.py:247
  288.5 4.2 %collective-permute-start.30 = (bf16[512,512]{1,0:T(8,128)(2,1)S(1)}, bf16[512,512]{1,0:T(8,128)(2,1)S(1)}, u32[]{:S(2)}, u32[]{:S(2)}) collective-permute-start(bf16[512,512]{1,0:T(8,128)(2,1)S(1)} %constant_dynamic-slice_fusion.3), channel_id=1, source_target_pairs={{0,8},{8,0},{16,24},{24,16},{1,9},{9,1},{17,25},{25,17},{2,10},{10... | collective-permute-start | bytes 1572872 | tf_op jit(solution)/shard_map/ppermute | solution.py:244
  288.7 21.6 %collective-permute-start.24 = (bf16[1024,256]{1,0:T(8,128)(2,1)S(1)}, bf16[1024,256]{1,0:T(8,128)(2,1)S(1)}, u32[]{:S(2)}, u32[]{:S(2)}) collective-permute-start(bf16[1024,256]{1,0:T(8,128)(2,1)S(1)} %constant_dynamic-slice_fusion.6), channel_id=1, source_target_pairs={{0,16},{8,24},{16,0},{24,8},{1,17},{9,25},{17,1},{25,9},{2,18},{10... | collective-permute-start | bytes 1572872 | tf_op jit(solution)/shard_map/ppermute | solution.py:247
  292.8 18.4 %collective-permute-start.40 = (bf16[512,512]{1,0:T(8,128)(2,1)S(1)}, bf16[512,512]{1,0:T(8,128)(2,1)S(1)}, u32[]{:S(2)}, u32[]{:S(2)}) collective-permute-start(bf16[512,512]{1,0:T(8,128)(2,1)S(1)} %slice.273), channel_id=1, source_target_pairs={{0,8},{8,0},{16,24},{24,16},{1,9},{9,1},{17,25},{25,17},{2,10},{10... | collective-permute-start | bytes 1572872 | tf_op jit(solution)/shard_map/ppermute | solution.py:244
  299.0 22.1 %collective-permute-start.31 = (bf16[1024,256]{1,0:T(8,128)(2,1)}, bf16[1024,256]{1,0:T(8,128)(2,1)}, u32[]{:S(2)}, u32[]{:S(2)}) collective-permute-start(bf16[1024,256]{1,0:T(8,128)(2,1)} %get-tuple-element.165), channel_id=1, source_target_pairs={{0,16},{8,24},{16,0},{24,8},{1,17},{9,25},{17,1},{25,9},{2,18},{10... | collective-permute-start | bytes 1572872 | tf_op jit(solution)/shard_map/ppermute | solution.py:247
  321.1 17.9 %collective-permute-start.38 = (bf16[128,2816]{1,0:T(8,128)(2,1)}, bf16[128,2816]{1,0:T(8,128)(2,1)S(1)}, u32[]{:S(2)}, u32[]{:S(2)}) collective-permute-start(bf16[128,2816]{1,0:T(8,128)(2,1)} %reduce-scatter.3.cloned.1.call-done), channel_id=1, source_target_pairs={{0,16},{8,24},{16,0},{24,8},{1,17},{9,25},{17,1},{25,9},{2,18},{10... | collective-permute-start | bytes 2162696 | tf_op jit(solution)/shard_map/ppermute | solution.py:247
  324.7 30.3 %collective-permute-start.32 = (bf16[4,480,256]{2,1,0:T(8,128)(2,1)S(1)}, bf16[4,480,256]{2,1,0:T(8,128)(2,1)S(1)}, u32[]{:S(2)}, u32[]{:S(2)}) collective-permute-start(bf16[4,480,256]{2,1,0:T(8,128)(2,1)S(1)} %fusion.34), channel_id=1, source_target_pairs={{0,1},{1,0},{2,3},{3,2},{4,5},{5,4},{6,7},{7,6},{8,9},{9,8},{10,11... | collective-permute-start | bytes 2949128 | tf_op jit(solution)/shard_map/ppermute | solution.py:293
  325.4 34.8 %copy-start.6 = (f32[1024,1024]{1,0:T(8,128)S(1)}, f32[1024,1024]{1,0:T(8,128)}, u32[]{:S(2)}) copy-start(f32[1024,1024]{1,0:T(8,128)} %copy-done.5) | copy-start | bytes 12582916
  340.4 39.2 %collective-permute-start.39 = (bf16[128,2816]{1,0:T(8,128)(2,1)S(1)}, bf16[128,2816]{1,0:T(8,128)(2,1)S(1)}, u32[]{:S(2)}, u32[]{:S(2)}) collective-permute-start(bf16[128,2816]{1,0:T(8,128)(2,1)S(1)} %add_convert_fusion.1), channel_id=1, source_target_pairs={{0,8},{8,0},{16,24},{24,16},{1,9},{9,1},{17,25},{25,17},{2,10},{10... | collective-permute-start | bytes 2162696 | tf_op jit(solution)/shard_map/ppermute | solution.py:244
  355.3 9.4 %collective-permute-start.35 = (bf16[480,256]{1,0:T(8,128)(2,1)S(1)}, bf16[480,256]{1,0:T(8,128)(2,1)S(1)}, u32[]{:S(2)}, u32[]{:S(2)}) collective-permute-start(bf16[480,256]{1,0:T(8,128)(2,1)S(1)} %get-tuple-element.174), channel_id=1, source_target_pairs={{0,6},{1,7},{2,0},{3,1},{4,2},{5,3},{6,4},{7,5},{8,14},{9,15},{10,... | collective-permute-start | bytes 737288 | tf_op jit(solution)/shard_map/ppermute | solution.py:296
  358.4 19.2 %collective-permute-start.34 = (bf16[480,256]{1,0:T(8,128)(2,1)S(1)}, bf16[480,256]{1,0:T(8,128)(2,1)S(1)}, u32[]{:S(2)}, u32[]{:S(2)}) collective-permute-start(bf16[480,256]{1,0:T(8,128)(2,1)S(1)} %get-tuple-element.175), channel_id=1, source_target_pairs={{0,4},{1,5},{2,6},{3,7},{4,0},{5,1},{6,2},{7,3},{8,12},{9,13},{10,... | collective-permute-start | bytes 737288 | tf_op jit(solution)/shard_map/ppermute | solution.py:296
  358.4 19.2 %collective-permute-start.33 = (bf16[480,256]{1,0:T(8,128)(2,1)S(1)}, bf16[480,256]{1,0:T(8,128)(2,1)S(1)}, u32[]{:S(2)}, u32[]{:S(2)}) collective-permute-start(bf16[480,256]{1,0:T(8,128)(2,1)S(1)} %get-tuple-element.173), channel_id=1, source_target_pairs={{0,2},{1,3},{2,4},{3,5},{4,6},{5,7},{6,0},{7,1},{8,10},{9,11},{10,... | collective-permute-start | bytes 737288 | tf_op jit(solution)/shard_map/ppermute | solution.py:296
  377.8 15.2 %collective-permute-start.36 = (bf16[480,256]{1,0:T(8,128)(2,1)S(1)}, bf16[480,256]{1,0:T(8,128)(2,1)S(1)}, u32[]{:S(2)}, u32[]{:S(2)}) collective-permute-start(bf16[480,256]{1,0:T(8,128)(2,1)S(1)} %fusion.44), channel_id=1, source_target_pairs={{0,16},{8,24},{16,0},{24,8},{1,17},{9,25},{17,1},{25,9},{2,18},{10... | collective-permute-start | bytes 737288 | tf_op jit(solution)/shard_map/ppermute | solution.py:247
  391.5 8.0 %collective-permute-start.26 = (bf16[128,1152]{1,0:T(8,128)(2,1)}, bf16[128,1152]{1,0:T(8,128)(2,1)S(1)}, u32[]{:S(2)}, u32[]{:S(2)}) collective-permute-start(bf16[128,1152]{1,0:T(8,128)(2,1)} %reduce-scatter.5.cloned.1.call-done), channel_id=1, source_target_pairs={{0,16},{8,24},{16,0},{24,8},{1,17},{9,25},{17,1},{25,9},{2,18},{10... | collective-permute-start | bytes 884744 | tf_op jit(solution)/shard_map/ppermute | solution.py:247
  393.0 8.4 %collective-permute-start.37 = (bf16[480,512]{1,0:T(8,128)(2,1)S(1)}, bf16[480,512]{1,0:T(8,128)(2,1)S(1)}, u32[]{:S(2)}, u32[]{:S(2)}) collective-permute-start(bf16[480,512]{1,0:T(8,128)(2,1)S(1)} %pad_maximum_fusion.21), channel_id=1, source_target_pairs={{0,8},{8,0},{16,24},{24,16},{1,9},{9,1},{17,25},{25,17},{2,10},{10... | collective-permute-start | bytes 1474568 | tf_op jit(solution)/shard_map/ppermute | solution.py:244
  401.4 2.4 collective-permute-start.27
  (45 other events, 331.4 us)
Sparse Core Ops, SparseCore 0:
  64.0 100.8 all-gather.1
  205.8 108.8 reduce-scatter.2
  318.2 73.2 reduce-scatter.4
